TPU v7x, 32 devices: a whole 2x2x4 slice. The times are simulated.
32 devices in a mesh: dp: 8 (over z, y), tensor: 4 (over x, core).
Axes of the slice: x: 2, y: 2, z: 4, core: 2. Of those that a mesh axis runs over, the one named last changes fastest.
Arguments:
- tokens: bfloat16 [4, 2048, 2048], P(None, ('dp', 'tensor')), may hold values from -6 to 6
- cotangent: bfloat16 [4, 2048, 2048], P(None, ('dp', 'tensor')), may hold values from -6 to 6
- query_weight: bfloat16 [2048, 2048], P('dp', 'tensor'), may hold values from -0.125 to 0.125
- key_weight: bfloat16 [2048, 2048], P('dp', 'tensor'), may hold values from -0.125 to 0.125
- value_weight: bfloat16 [2048, 2048], P('dp', 'tensor'), may hold values from -0.125 to 0.125
- beta_weight: bfloat16 [2048, 16], P('dp', 'tensor'), may hold values from -0.125 to 0.125
- conv_filter: bfloat16 [12, 16, 128], P(None, 'tensor', 'dp'), may hold values from -3 to 3
- norm_gain: bfloat16 [2, 2048], P(None, 'dp'), may hold values from 0.25 to 1.75
- head_gain: bfloat16 [128], P('dp'), may hold values from 0.25 to 1.75
- out_weight: bfloat16 [2048, 2048], P('tensor', 'dp'), may hold values from -0.125 to 0.125
- gate_weight: bfloat16 [2048, 5632], P('dp', 'tensor'), may hold values from -0.125 to 0.125
- up_weight: bfloat16 [2048, 5632], P('dp', 'tensor'), may hold values from -0.125 to 0.125
- down_weight: bfloat16 [5632, 2048], P('tensor', 'dp'), may hold values from -0.078125 to 0.078125
Outputs:
- layer_out: bfloat16 [4, 2048, 2048], P(None, ('dp', 'tensor'))
- d_tokens: bfloat16 [4, 2048, 2048], P(None, ('dp', 'tensor'))
- grad_query_weight: float32 [2048, 2048], P('dp', 'tensor')
- grad_key_weight: float32 [2048, 2048], P('dp', 'tensor')
- grad_value_weight: float32 [2048, 2048], P('dp', 'tensor')
- grad_beta_weight: float32 [2048, 16], P('dp', 'tensor')
- grad_conv_filter: float32 [12, 16, 128], P(None, 'tensor', 'dp')
- grad_norm_gain: float32 [2, 2048], P(None, 'dp')
- grad_head_gain: float32 [128], P('dp')
- grad_out_weight: float32 [2048, 2048], P('tensor', 'dp')
- grad_gate_weight: float32 [2048, 5632], P('dp', 'tensor')
- grad_up_weight: float32 [2048, 5632], P('dp', 'tensor')
- grad_down_weight: float32 [5632, 2048], P('tensor', 'dp')
All inputs are finite; a program needn't handle non-finite values.
Results may differ from a plain program's by a relative error of at most 0.018.
Values may be sent and summed in bfloat16 or wider, within the bound.
A program may use at most 384 MiB of HBM per device.

v0:
```python
import jax
import jax.numpy as jnp
from jax import lax
from jax.sharding import PartitionSpec as P

HD = 128
KCONV = 4
GROUP = 64


highest_precision = lax.Precision.HIGHEST
epsilon = 1e-06


def from_behind(block, axis, distance):
    devices = range(lax.axis_size(axis))
    route = [(i - distance, i) for i in devices if i - distance in devices]
    return lax.ppermute(block, axis, route)


def entering(value, axis, combine, identity):
    devices, here = (lax.axis_size(axis), lax.axis_index(axis))
    everything = jax.tree.map(lambda part: lax.all_gather(part, axis), value)
    start = jax.tree.map(
        lambda part, zero: jnp.broadcast_to(jnp.asarray(zero, part.dtype), part.shape),
        value,
        identity,
    )

    def hop(k, before):
        reached = k < here
        new = combine(before, jax.tree.map(lambda part: part[k], everything))
        return jax.tree.map(lambda a, b: jnp.where(reached, a, b), new, before)

    return lax.fori_loop(0, devices, hop, start)


def entering_2(value, axis, combine, identity):
    devices, here = (lax.axis_size(axis), lax.axis_index(axis))
    everything = jax.tree.map(
        lambda part, kind: lax.all_gather(part.astype(kind), axis),
        value,
        jax.tree.map(lambda a: jnp.bfloat16 if a.dtype == jnp.float32 else a.dtype, value),
    )
    start = jax.tree.map(
        lambda part, zero: jnp.broadcast_to(jnp.asarray(zero, part.dtype), part.shape),
        value,
        identity,
    )

    def hop(k, before):
        at = devices - 1 - k
        reached = at > here
        new = combine(
            before, jax.tree.map(lambda part, own: part[at].astype(own.dtype), everything, value)
        )
        return jax.tree.map(lambda a, b: jnp.where(reached, a, b), new, before)

    return lax.fori_loop(0, devices, hop, start)


def rms_scale(values, gain_row):
    return (
        values * lax.rsqrt(jnp.mean(values * values, axis=-1, keepdims=True) + epsilon) * gain_row
    )


def unit_rows(values):
    return values * lax.rsqrt(jnp.sum(values * values, axis=-1, keepdims=True) + epsilon)


def mix_inputs(extended, conv_taps):
    seqs_here = extended.shape[0]
    piece_len = extended.shape[1] - KCONV + 1
    heads_here = conv_taps.shape[1]
    local_width = heads_here * HD
    filters = conv_taps.reshape(3, KCONV, local_width)
    outputs = []
    for column in range(3):
        part_in = extended[:, :, column * local_width : (column + 1) * local_width]
        running = jnp.zeros((seqs_here, piece_len, local_width), extended.dtype)
        for tap_index in range(KCONV):
            running = (
                running + filters[column, tap_index] * part_in[:, tap_index : tap_index + piece_len]
            )
        activated = jax.nn.silu(running).reshape(seqs_here, piece_len, heads_here, HD)
        if column < 2:
            activated = unit_rows(activated)
        outputs.append(jnp.swapaxes(activated, 1, 2))
    return tuple(outputs)


def to_groups(array_in):
    seqs_here, heads_here, piece_len = array_in.shape[:3]
    return array_in.reshape((seqs_here, heads_here, piece_len // GROUP, GROUP) + array_in.shape[3:])


def block_products(query_low, key_low):
    query_blocks = to_groups(query_low)
    key_blocks = to_groups(key_low)
    gram_all = jnp.einsum(
        "shbck,shbdk->shbcd", key_blocks, key_blocks, preferred_element_type=jnp.float32
    )
    scores_all = jnp.einsum(
        "shbck,shbdk->shbcd", query_blocks, key_blocks, preferred_element_type=jnp.float32
    )
    return (
        gram_all.reshape(query_low.shape[:3] + (GROUP,)),
        scores_all.reshape(query_low.shape[:3] + (GROUP,)),
    )


def block_products_back(round_query, round_key, back_gram, back_scores):
    query_blocks = to_groups(round_query)
    key_blocks = to_groups(round_key)
    gram_blocks = to_groups(back_gram)
    score_blocks = to_groups(back_scores)
    gram_sym = gram_blocks + jnp.swapaxes(gram_blocks, -1, -2)
    back_query = jnp.einsum(
        "shbcd,shbdk->shbck", score_blocks, key_blocks, precision=highest_precision
    )
    back_key = jnp.einsum("shbcd,shbdk->shbck", gram_sym, key_blocks, precision=highest_precision)
    back_key = back_key + jnp.einsum(
        "shbcd,shbck->shbdk", score_blocks, query_blocks, precision=highest_precision
    )
    return (back_query.reshape(round_query.shape), back_key.reshape(round_key.shape))


def piece_terms(query_rows, input_keys, values_in, strength, gram_all, scores_all):
    seqs_here, heads_here, piece_len, _ = query_rows.shape
    blocks = piece_len // GROUP

    def to_blocks(array_in):
        return jnp.moveaxis(
            array_in.reshape((seqs_here, heads_here, blocks, GROUP) + array_in.shape[3:]), 2, 0
        )

    wide_values = jnp.concatenate([values_in, jnp.zeros_like(values_in)], axis=-1)
    identity_part = jnp.broadcast_to(
        jnp.eye(HD, dtype=query_rows.dtype), (seqs_here, heads_here, HD, HD)
    )
    initial = jnp.concatenate([jnp.zeros_like(identity_part), identity_part], axis=-1)
    strict = jnp.tril(jnp.ones((GROUP, GROUP), query_rows.dtype), -1)
    inclusive = jnp.tril(jnp.ones((GROUP, GROUP), query_rows.dtype))

    def block_step(carried_state, inputs):
        block_query, block_key, block_value, block_strength, gram_matrix, raw_scores = inputs
        system = (
            jnp.eye(GROUP, dtype=query_rows.dtype)
            + block_strength[..., None] * gram_matrix * strict
        )
        key_mixture = jax.scipy.linalg.solve_triangular(
            system, block_strength[..., None] * block_key, lower=True, unit_diagonal=True
        )
        value_mixture = jax.scipy.linalg.solve_triangular(
            system, block_strength[..., None] * block_value, lower=True, unit_diagonal=True
        )
        state_update = value_mixture - jnp.einsum(
            "shck,shkv->shcv", key_mixture, carried_state, precision=highest_precision
        )
        scores = raw_scores * inclusive
        block_output = jnp.einsum(
            "shck,shkv->shcv", block_query, carried_state, precision=highest_precision
        )
        block_output = block_output + jnp.einsum(
            "shcd,shdv->shcv", scores, state_update, precision=highest_precision
        )
        updated_state = carried_state + jnp.einsum(
            "shck,shcv->shkv", block_key, state_update, precision=highest_precision
        )
        return (updated_state, block_output)

    final_state, outputs = lax.scan(
        block_step,
        initial,
        (
            to_blocks(query_rows),
            to_blocks(input_keys),
            to_blocks(wide_values),
            to_blocks(strength),
            to_blocks(gram_all),
            to_blocks(scores_all),
        ),
    )
    outputs = jnp.moveaxis(outputs, 0, 2).reshape(seqs_here, heads_here, piece_len, 2 * HD)
    return (outputs[..., :HD], outputs[..., HD:], final_state[..., :HD], final_state[..., HD:])


def compose_forward(earlier_pair, later_pair):
    joined_map = jnp.einsum(
        "...ij,...jk->...ik", later_pair[0], earlier_pair[0], precision=highest_precision
    )
    joined_base = (
        jnp.einsum(
            "...ij,...jk->...ik", later_pair[0], earlier_pair[1], precision=highest_precision
        )
        + later_pair[1]
    )
    return (joined_map, joined_base)


def compose_backward(earlier_pair, later_pair):
    joined_map = jnp.einsum(
        "...ij,...jk->...ik", earlier_pair[0], later_pair[0], precision=highest_precision
    )
    joined_base = (
        jnp.einsum(
            "...ji,...jk->...ik", later_pair[0], earlier_pair[1], precision=highest_precision
        )
        + later_pair[1]
    )
    return (joined_map, joined_base)


def shards(
    tokens,
    cotangent,
    query_weight,
    key_weight,
    value_weight,
    beta_weight,
    conv_filter,
    norm_gain,
    head_gain,
    out_weight,
    gate_weight,
    up_weight,
    down_weight,
):
    gathered = (
        lax.all_gather(query_weight, "dp", axis=0, tiled=True),
        lax.all_gather(key_weight, "dp", axis=0, tiled=True),
        lax.all_gather(value_weight, "dp", axis=0, tiled=True),
        lax.all_gather(beta_weight, "dp", axis=0, tiled=True),
        lax.all_gather(conv_filter, "dp", axis=2, tiled=True),
        lax.all_gather(norm_gain, "dp", axis=1, tiled=True),
        lax.all_gather(head_gain, "dp", axis=0, tiled=True),
        lax.all_gather(out_weight, "dp", axis=1, tiled=True),
        lax.all_gather(gate_weight, "dp", axis=0, tiled=True),
        lax.all_gather(up_weight, "dp", axis=0, tiled=True),
        lax.all_gather(down_weight, "dp", axis=1, tiled=True),
    )
    (
        full_query,
        full_key,
        full_value,
        full_beta,
        full_conv,
        full_gain,
        full_head,
        full_out,
        full_gate,
        full_up,
        full_down,
    ) = gathered
    rows_tokens, rows_cotangent = (
        lax.all_gather(tokens, "tensor", axis=1, tiled=True),
        lax.all_gather(cotangent, "tensor", axis=1, tiled=True),
    )
    seqs_here, piece_len, model_width = rows_tokens.shape
    heads_here = full_beta.shape[1]
    local_width = heads_here * HD
    own_tokens = tokens.astype(jnp.float32)
    gain_values = full_gain.astype(jnp.float32)
    wide_tokens = rows_tokens.astype(jnp.float32)
    scale_first = lax.rsqrt(jnp.mean(wide_tokens * wide_tokens, axis=-1, keepdims=True) + epsilon)
    unit_first = wide_tokens * scale_first
    normed_first = (unit_first * gain_values[0]).astype(jnp.bfloat16)
    proj_query = jnp.einsum(
        "std,dm->stm", normed_first, full_query, preferred_element_type=jnp.float32
    ).astype(jnp.bfloat16)
    proj_key = jnp.einsum(
        "std,dm->stm", normed_first, full_key, preferred_element_type=jnp.float32
    ).astype(jnp.bfloat16)
    proj_value = jnp.einsum(
        "std,dm->stm", normed_first, full_value, preferred_element_type=jnp.float32
    ).astype(jnp.bfloat16)
    projected = jnp.concatenate([proj_query, proj_key, proj_value], axis=2)
    logit_beta = jnp.einsum(
        "std,dh->sth", normed_first, full_beta, preferred_element_type=jnp.float32
    )
    strength = jax.nn.sigmoid(logit_beta)
    rim_rows = from_behind(projected[:, piece_len - KCONV + 1 :], "dp", 1)
    extended = jnp.concatenate([rim_rows, projected], axis=1).astype(jnp.float32)
    (query_rows, input_keys, values_in), mix_pullback = jax.vjp(
        mix_inputs, extended, full_conv.astype(jnp.float32)
    )
    query_low = query_rows.astype(jnp.bfloat16)
    key_low = input_keys.astype(jnp.bfloat16)
    round_query = query_low.astype(jnp.float32)
    round_key = key_low.astype(jnp.float32)
    round_value = values_in.astype(jnp.bfloat16).astype(jnp.float32)
    strength_heads = jnp.swapaxes(strength, 1, 2)
    gram_all, scores_all = block_products(query_low, key_low)
    (base_mix, carry_map, end_base, end_map), delta_pullback = jax.vjp(
        piece_terms, round_query, round_key, round_value, strength_heads, gram_all, scores_all
    )
    identity_map = jnp.broadcast_to(jnp.eye(HD, dtype=jnp.float32), end_map.shape)
    zero_base = jnp.zeros_like(end_base)
    _, state_in = entering((end_map, end_base), "dp", compose_forward, (identity_map, zero_base))
    mix_out = base_mix + jnp.einsum(
        "shtk,shkv->shtv", carry_map, state_in, precision=highest_precision
    )
    normed_float, head_pullback = jax.vjp(rms_scale, mix_out, full_head.astype(jnp.float32))
    normed_mix = normed_float.astype(jnp.bfloat16)
    out_split = full_out.reshape(heads_here, HD, model_width)
    branch_part = jnp.einsum(
        "shtd,hdm->stm", normed_mix, out_split, preferred_element_type=jnp.float32
    )
    branch = lax.psum_scatter(branch_part, "tensor", scatter_dimension=1, tiled=True)
    hidden_state = own_tokens + branch
    rows_hidden = lax.all_gather(hidden_state, "tensor", axis=1, tiled=True)
    scale_second = lax.rsqrt(jnp.mean(rows_hidden * rows_hidden, axis=-1, keepdims=True) + epsilon)
    unit_second = rows_hidden * scale_second
    normed_second = (unit_second * gain_values[1]).astype(jnp.bfloat16)
    gate_pre = jnp.einsum(
        "std,df->stf", normed_second, full_gate, preferred_element_type=jnp.float32
    )
    up_pre = jnp.einsum("std,df->stf", normed_second, full_up, preferred_element_type=jnp.float32)
    gate_sigmoid = jax.nn.sigmoid(gate_pre)
    ffn_hidden = (gate_pre * gate_sigmoid * up_pre).astype(jnp.bfloat16)
    ffn_part = jnp.einsum("stf,fd->std", ffn_hidden, full_down, preferred_element_type=jnp.float32)
    ffn_branch = lax.psum_scatter(
        ffn_part.astype(jnp.bfloat16), "tensor", scatter_dimension=1, tiled=True
    ).astype(jnp.float32)
    layer_out = (hidden_state + ffn_branch).astype(jnp.bfloat16)
    gathered = (
        lax.all_gather(query_weight, "dp", axis=0, tiled=True),
        lax.all_gather(key_weight, "dp", axis=0, tiled=True),
        lax.all_gather(value_weight, "dp", axis=0, tiled=True),
        lax.all_gather(beta_weight, "dp", axis=0, tiled=True),
        lax.all_gather(conv_filter, "dp", axis=2, tiled=True),
        lax.all_gather(norm_gain, "dp", axis=1, tiled=True),
        lax.all_gather(head_gain, "dp", axis=0, tiled=True),
        lax.all_gather(out_weight, "dp", axis=1, tiled=True),
        lax.all_gather(gate_weight, "dp", axis=0, tiled=True),
        lax.all_gather(up_weight, "dp", axis=0, tiled=True),
        lax.all_gather(down_weight, "dp", axis=1, tiled=True),
    )
    (
        full_query,
        full_key,
        full_value,
        full_beta,
        full_conv,
        full_gain,
        full_head,
        full_out,
        full_gate,
        full_up,
        full_down,
    ) = gathered
    out_split = full_out.reshape(heads_here, HD, model_width)
    back_hidden = jnp.einsum(
        "std,fd->stf", rows_cotangent, full_down, preferred_element_type=jnp.float32
    )
    grad_down = jnp.einsum(
        "stf,std->fd", ffn_hidden, rows_cotangent, preferred_element_type=jnp.float32
    )
    back_gate = (
        back_hidden * up_pre * gate_sigmoid * (1.0 + gate_pre * (1.0 - gate_sigmoid))
    ).astype(jnp.bfloat16)
    back_up = (back_hidden * gate_pre * gate_sigmoid).astype(jnp.bfloat16)
    grad_gate = jnp.einsum(
        "std,stf->df", normed_second, back_gate, preferred_element_type=jnp.float32
    )
    grad_up = jnp.einsum("std,stf->df", normed_second, back_up, preferred_element_type=jnp.float32)
    back_second = jnp.einsum(
        "stf,df->std", back_gate, full_gate, preferred_element_type=jnp.float32
    )
    back_second = back_second + jnp.einsum(
        "stf,df->std", back_up, full_up, preferred_element_type=jnp.float32
    )
    gain_second = jnp.sum(back_second * unit_second, axis=(0, 1))
    back_second_rows, gain_second_all = (
        lax.psum_scatter(back_second, "tensor", scatter_dimension=1, tiled=True),
        lax.psum_scatter(
            jnp.broadcast_to(gain_second, (lax.axis_size("tensor"), model_width)),
            "tensor",
            scatter_dimension=0,
            tiled=True,
        ),
    )
    _, second_pullback = jax.vjp(lambda values: rms_scale(values, gain_values[1]), hidden_state)
    back_state = cotangent.astype(jnp.float32) + second_pullback(back_second_rows)[0]
    rows_back = lax.all_gather(back_state.astype(jnp.bfloat16), "tensor", axis=1, tiled=True)
    grad_out = jnp.einsum(
        "shtd,stm->hdm", normed_mix, rows_back, preferred_element_type=jnp.float32
    ).reshape(local_width, model_width)
    back_normed = jnp.einsum(
        "stm,hdm->shtd", rows_back, out_split, preferred_element_type=jnp.float32
    )
    back_mix, head_part = head_pullback(back_normed)
    back_carry = jnp.einsum("shtv,shkv->shtk", back_mix, state_in, precision=highest_precision)
    local_back = jnp.einsum("shtk,shtv->shkv", carry_map, back_mix, precision=highest_precision)
    _, back_end = entering_2(
        (end_map, local_back), "dp", compose_backward, (identity_map, zero_base)
    )
    back_end_map = jnp.einsum("shkv,shjv->shkj", back_end, state_in, precision=highest_precision)
    back_query, back_key, back_value, back_strength, back_gram, back_scores = delta_pullback(
        (back_mix, back_carry, back_end, back_end_map)
    )
    extra_query, extra_key = block_products_back(round_query, round_key, back_gram, back_scores)
    back_query = back_query + extra_query
    back_key = back_key + extra_key
    back_extended, grad_conv = mix_pullback((back_query, back_key, back_value))
    rim_back = from_behind(back_extended[:, : KCONV - 1].astype(jnp.bfloat16), "dp", -1).astype(
        jnp.float32
    )
    back_projected = jnp.concatenate(
        [back_extended[:, KCONV - 1 : piece_len], back_extended[:, piece_len:] + rim_back], axis=1
    ).astype(jnp.bfloat16)
    back_logit = (jnp.swapaxes(back_strength, 1, 2) * strength * (1.0 - strength)).astype(
        jnp.bfloat16
    )
    back_proj_query = back_projected[:, :, :local_width]
    back_proj_key = back_projected[:, :, local_width : 2 * local_width]
    back_proj_value = back_projected[:, :, 2 * local_width :]
    grad_query = jnp.einsum(
        "std,stm->dm", normed_first, back_proj_query, preferred_element_type=jnp.float32
    )
    grad_key = jnp.einsum(
        "std,stm->dm", normed_first, back_proj_key, preferred_element_type=jnp.float32
    )
    grad_value = jnp.einsum(
        "std,stm->dm", normed_first, back_proj_value, preferred_element_type=jnp.float32
    )
    grad_beta = jnp.einsum(
        "std,sth->dh", normed_first, back_logit, preferred_element_type=jnp.float32
    )
    back_first = jnp.einsum(
        "stm,dm->std", back_proj_query, full_query, preferred_element_type=jnp.float32
    )
    back_first = back_first + jnp.einsum(
        "stm,dm->std", back_proj_key, full_key, preferred_element_type=jnp.float32
    )
    back_first = back_first + jnp.einsum(
        "stm,dm->std", back_proj_value, full_value, preferred_element_type=jnp.float32
    )
    back_first = back_first + jnp.einsum(
        "sth,dh->std", back_logit, full_beta, preferred_element_type=jnp.float32
    )
    gain_first = jnp.sum(back_first * unit_first, axis=(0, 1))
    small_terms = jnp.concatenate([gain_first, head_part])
    back_first_rows, small_all = (
        lax.psum_scatter(
            back_first.astype(jnp.bfloat16), "tensor", scatter_dimension=1, tiled=True
        ).astype(jnp.float32),
        lax.psum_scatter(
            jnp.broadcast_to(small_terms, (lax.axis_size("tensor"), model_width + HD)).astype(
                jnp.bfloat16
            ),
            "tensor",
            scatter_dimension=0,
            tiled=True,
        ).astype(jnp.float32),
    )
    _, first_pullback = jax.vjp(lambda values: rms_scale(values, gain_values[0]), own_tokens)
    d_tokens = (back_state + first_pullback(back_first_rows)[0]).astype(jnp.bfloat16)
    grad_gain = jnp.stack([small_all[0, :model_width], gain_second_all[0]])
    grad_head = small_all[0, model_width:]
    results = (
        lax.psum_scatter(
            grad_query.astype(jnp.bfloat16), "dp", scatter_dimension=0, tiled=True
        ).astype(jnp.float32),
        lax.psum_scatter(
            grad_key.astype(jnp.bfloat16), "dp", scatter_dimension=0, tiled=True
        ).astype(jnp.float32),
        lax.psum_scatter(
            grad_value.astype(jnp.bfloat16), "dp", scatter_dimension=0, tiled=True
        ).astype(jnp.float32),
        lax.psum_scatter(
            grad_beta.astype(jnp.bfloat16), "dp", scatter_dimension=0, tiled=True
        ).astype(jnp.float32),
        lax.psum_scatter(
            grad_conv.astype(jnp.bfloat16), "dp", scatter_dimension=2, tiled=True
        ).astype(jnp.float32),
        lax.psum_scatter(
            grad_gain.astype(jnp.bfloat16), "dp", scatter_dimension=1, tiled=True
        ).astype(jnp.float32),
        lax.psum_scatter(
            grad_head.astype(jnp.bfloat16), "dp", scatter_dimension=0, tiled=True
        ).astype(jnp.float32),
        lax.psum_scatter(
            grad_out.astype(jnp.bfloat16), "dp", scatter_dimension=1, tiled=True
        ).astype(jnp.float32),
        lax.psum_scatter(
            grad_gate.astype(jnp.bfloat16), "dp", scatter_dimension=0, tiled=True
        ).astype(jnp.float32),
        lax.psum_scatter(
            grad_up.astype(jnp.bfloat16), "dp", scatter_dimension=0, tiled=True
        ).astype(jnp.float32),
        lax.psum_scatter(
            grad_down.astype(jnp.bfloat16), "dp", scatter_dimension=1, tiled=True
        ).astype(jnp.float32),
    )
    return (layer_out, d_tokens) + tuple(results)


def solution(mesh):
    return jax.shard_map(
        shards,
        mesh=mesh,
        in_specs=(
            P(None, ("dp", "tensor"), None),
            P(None, ("dp", "tensor"), None),
            P("dp", "tensor"),
            P("dp", "tensor"),
            P("dp", "tensor"),
            P("dp", "tensor"),
            P(None, "tensor", "dp"),
            P(None, "dp"),
            P("dp"),
            P("tensor", "dp"),
            P("dp", "tensor"),
            P("dp", "tensor"),
            P("tensor", "dp"),
        ),
        out_specs=(
            P(None, ("dp", "tensor"), None),
            P(None, ("dp", "tensor"), None),
            P("dp", "tensor"),
            P("dp", "tensor"),
            P("dp", "tensor"),
            P("dp", "tensor"),
            P(None, "tensor", "dp"),
            P(None, "dp"),
            P("dp"),
            P("tensor", "dp"),
            P("dp", "tensor"),
            P("dp", "tensor"),
            P("tensor", "dp"),
        ),
        check_vma=False,
    )
```

profile of v0, /device:TPU:0, one launch (start us, length us, event | category | flops | bytes accessed | tf_op | source)
XLA Modules:
  0.0 3144.7 jit_solution(8327334752160606627)
XLA Ops:
  250.6 408.6 %while.91 = (s32[]{:T(128)}, f32[4,4,128,256]{3,2,1,0:T(8,128)S(1)}, f32[4,4,4,64,256]{4,3,2,1,0:T(8,128)}, f32[4,4,4,64,1]{3,2,1,4,0:T(4,128)}, f32[4,4,4,64,64...) while((s32[]{:T(128)}, ...), condition=%wide.region_4.5_spmd.clone.clone, body=%wide.region_3.4_spmd.clone.clone.sunk | while | flops 1713213440 | bytes 39520712 | solution.py:173
  264.6 78.6 %custom-call.44 = f32[4,4,1,64,64]{3,4,2,1,0:T(8,128)S(1)} custom-call(f32[4,4,1,64,64]{4,3,2,1,0:T(8,128)S(1)} %get-tuple-element.1934), custom_call_target="InvertDiagBlocksLowerTriangular" | custom-call | tf_op jit(solution)/shard_map/jvp()/while/body/eval_jaxpr/jit(_solve_triangular)/vmap(vmap())/triangular_solve | solution.py:155
  363.9 78.6 %custom-call.44 = f32[4,4,1,64,64]{3,4,2,1,0:T(8,128)S(1)} custom-call(f32[4,4,1,64,64]{4,3,2,1,0:T(8,128)S(1)} %get-tuple-element.1934), custom_call_target="InvertDiagBlocksLowerTriangular" | custom-call | tf_op jit(solution)/shard_map/jvp()/while/body/eval_jaxpr/jit(_solve_triangular)/vmap(vmap())/triangular_solve | solution.py:155
  463.2 78.6 %custom-call.44 = f32[4,4,1,64,64]{3,4,2,1,0:T(8,128)S(1)} custom-call(f32[4,4,1,64,64]{4,3,2,1,0:T(8,128)S(1)} %get-tuple-element.1934), custom_call_target="InvertDiagBlocksLowerTriangular" | custom-call | tf_op jit(solution)/shard_map/jvp()/while/body/eval_jaxpr/jit(_solve_triangular)/vmap(vmap())/triangular_solve | solution.py:155
  562.4 78.6 %custom-call.44 = f32[4,4,1,64,64]{3,4,2,1,0:T(8,128)S(1)} custom-call(f32[4,4,1,64,64]{4,3,2,1,0:T(8,128)S(1)} %get-tuple-element.1934), custom_call_target="InvertDiagBlocksLowerTriangular" | custom-call | tf_op jit(solution)/shard_map/jvp()/while/body/eval_jaxpr/jit(_solve_triangular)/vmap(vmap())/triangular_solve | solution.py:155
  689.4 97.6 %all-gather.42.cloned.1.call-done = f32[32,4,128,128]{3,2,1,0:T(8,128)} async-done(((f32[4,4,128,128]{3,2,1,0:T(8,128)}), f32[32,4,128,128]{3,2,1,0:T(8,128)}) %all-gather.42.cloned.1.call-update) | async-done | bytes 8388624 | tf_op jit(solution)/shard_map/all_gather | solution.py:23
  787.0 125.7 %all-gather.44.cloned.1.call-done = f32[32,4,128,128]{3,2,1,0:T(8,128)} async-done(((f32[4,4,128,128]{3,2,1,0:T(8,128)}), f32[32,4,128,128]{3,2,1,0:T(8,128)}) %all-gather.44.cloned.1.call-update) | async-done | bytes 8388624 | tf_op jit(solution)/shard_map/all_gather | solution.py:23
  973.4 68.7 %reduce-scatter.21.cloned.1.call-done = f32[4,64,2048]{2,1,0:T(8,128)} async-done(((f32[4,256,2048]{2,1,0:T(8,128)}), f32[4,64,2048]{2,1,0:T(8,128)}) %reduce-scatter.21.cloned.1.call-update) | async-done | bytes 2097168 | tf_op jit(solution)/shard_map/reduce_scatter | solution.py:310
  1078.2 95.7 %all-gather.36.cloned.1.call-done = bf16[1408,2048]{1,0:T(8,128)(2,1)} async-done(((bf16[1408,256]{1,0:T(8,128)(2,1)}), bf16[1408,2048]{1,0:T(8,128)(2,1)}) %all-gather.36.cloned.1.call-update) | async-done | bytes 5767184 | tf_op jit(solution)/shard_map/all_gather | solution.py:241
  1240.7 86.4 %all-gather.34.cloned.1.call-done = bf16[2048,1408]{1,0:T(8,128)(2,1)} async-done(((bf16[256,1408]{1,0:T(8,128)(2,1)}), bf16[2048,1408]{1,0:T(8,128)(2,1)}) %all-gather.34.cloned.1.call-update) | async-done | bytes 5767184 | tf_op jit(solution)/shard_map/all_gather | solution.py:240
  1338.7 81.6 %all-gather.32.cloned.1.call-done = bf16[2048,1408]{1,0:T(8,128)(2,1)} async-done(((bf16[256,1408]{1,0:T(8,128)(2,1)}), bf16[2048,1408]{1,0:T(8,128)(2,1)}) %all-gather.32.cloned.1.call-update) | async-done | bytes 5767184 | tf_op jit(solution)/shard_map/all_gather | solution.py:239
  1457.6 70.0 %reduce-scatter.25.cloned.1.call-done = f32[4,64,2048]{2,1,0:T(8,128)} async-done(((f32[4,256,2048]{2,1,0:T(8,128)}), f32[4,64,2048]{2,1,0:T(8,128)}) %reduce-scatter.25.cloned.1.call-update) | async-done | bytes 2097168 | tf_op jit(solution)/shard_map/reduce_scatter | solution.py:376
  1644.7 74.2 %all-gather.48.cloned.1.call-done = bf16[32,4,128,128]{3,2,1,0:T(8,128)(2,1)} async-done(((bf16[4,4,128,128]{3,2,1,0:T(8,128)(2,1)}), bf16[32,4,128,128]{3,2,1,0:T(8,128)(2,1)}) %all-gather.48.cloned.1.call-update) | async-done | bytes 4194320 | tf_op jit(solution)/shard_map/all_gather | solution.py:41
  1750.6 857.7 %while.92 = (s32[]{:T(128)}, f32[4,4,128,256]{3,2,1,0:T(8,128)S(1)}, f32[4,4,4,64,128]{4,3,0,2,1:T(8,128)}, f32[4,4,4,64,128]{4,3,0,2,1:T(8,128)}, f32[4,4,4,64,...) while((s32[]{:T(128)}, ...), condition=%wide.region_21.23_spmd.clone.clone, body=%wide.region_17.22_spmd.clone.clone.sunk | while | flops 3527306240 | bytes 89357480 | solution.py:173
  1760.8 80.0 %custom-call.46 = f32[4,4,1,64,64]{3,4,2,1,0:T(8,128)} custom-call(f32[4,4,1,64,64]{4,3,2,1,0:T(8,128)} %fusion.403), custom_call_target="InvertDiagBlocksLowerTriangular" | custom-call | tf_op jit(solution)/shard_map/transpose(jvp())/while/body/eval_jaxpr/jit(_solve_triangular)/vmap(vmap())/triangular_solve/custom-call.2 | solution.py:155
  1860.7 80.0 %custom-call.45 = f32[4,4,1,64,64]{3,4,2,1,0:T(8,128)} custom-call(f32[4,4,1,64,64]{4,3,2,1,0:T(8,128)} %add_bitcast_fusion.3), custom_call_target="InvertDiagBlocksLowerTriangular" | custom-call | tf_op jit(solution)/shard_map/transpose(jvp())/while/body/eval_jaxpr/jit(_solve_triangular)/vmap(vmap())/triangular_solve | solution.py:152
  1975.4 80.0 %custom-call.46 = f32[4,4,1,64,64]{3,4,2,1,0:T(8,128)} custom-call(f32[4,4,1,64,64]{4,3,2,1,0:T(8,128)} %fusion.403), custom_call_target="InvertDiagBlocksLowerTriangular" | custom-call | tf_op jit(solution)/shard_map/transpose(jvp())/while/body/eval_jaxpr/jit(_solve_triangular)/vmap(vmap())/triangular_solve/custom-call.2 | solution.py:155
  2075.0 80.0 %custom-call.45 = f32[4,4,1,64,64]{3,4,2,1,0:T(8,128)} custom-call(f32[4,4,1,64,64]{4,3,2,1,0:T(8,128)} %add_bitcast_fusion.3), custom_call_target="InvertDiagBlocksLowerTriangular" | custom-call | tf_op jit(solution)/shard_map/transpose(jvp())/while/body/eval_jaxpr/jit(_solve_triangular)/vmap(vmap())/triangular_solve | solution.py:152
  2189.6 80.0 %custom-call.46 = f32[4,4,1,64,64]{3,4,2,1,0:T(8,128)} custom-call(f32[4,4,1,64,64]{4,3,2,1,0:T(8,128)} %fusion.403), custom_call_target="InvertDiagBlocksLowerTriangular" | custom-call | tf_op jit(solution)/shard_map/transpose(jvp())/while/body/eval_jaxpr/jit(_solve_triangular)/vmap(vmap())/triangular_solve/custom-call.2 | solution.py:155
  2289.2 80.0 %custom-call.45 = f32[4,4,1,64,64]{3,4,2,1,0:T(8,128)} custom-call(f32[4,4,1,64,64]{4,3,2,1,0:T(8,128)} %add_bitcast_fusion.3), custom_call_target="InvertDiagBlocksLowerTriangular" | custom-call | tf_op jit(solution)/shard_map/transpose(jvp())/while/body/eval_jaxpr/jit(_solve_triangular)/vmap(vmap())/triangular_solve | solution.py:152
  2403.7 80.0 %custom-call.46 = f32[4,4,1,64,64]{3,4,2,1,0:T(8,128)} custom-call(f32[4,4,1,64,64]{4,3,2,1,0:T(8,128)} %fusion.403), custom_call_target="InvertDiagBlocksLowerTriangular" | custom-call | tf_op jit(solution)/shard_map/transpose(jvp())/while/body/eval_jaxpr/jit(_solve_triangular)/vmap(vmap())/triangular_solve/custom-call.2 | solution.py:155
  2503.3 80.0 %custom-call.45 = f32[4,4,1,64,64]{3,4,2,1,0:T(8,128)} custom-call(f32[4,4,1,64,64]{4,3,2,1,0:T(8,128)} %add_bitcast_fusion.3), custom_call_target="InvertDiagBlocksLowerTriangular" | custom-call | tf_op jit(solution)/shard_map/transpose(jvp())/while/body/eval_jaxpr/jit(_solve_triangular)/vmap(vmap())/triangular_solve | solution.py:152
  2830.5 68.6 %reduce-scatter.31.cloned.1.call-done = bf16[256,512]{1,0:T(8,128)(2,1)} async-done(((bf16[2048,512]{1,0:T(8,128)(2,1)}), bf16[256,512]{1,0:T(8,128)(2,1)}) %reduce-scatter.31.cloned.1.call-update) | async-done | bytes 262160 | tf_op jit(solution)/shard_map/reduce_scatter | solution.py:466
  2971.1 68.4 %reduce-scatter.33.cloned.1.call-done = bf16[256,512]{1,0:T(8,128)(2,1)} async-done(((bf16[2048,512]{1,0:T(8,128)(2,1)}), bf16[256,512]{1,0:T(8,128)(2,1)}) %reduce-scatter.33.cloned.1.call-update) | async-done | bytes 262160 | tf_op jit(solution)/shard_map/reduce_scatter | solution.py:469
  (706 shorter events, 1364.0 us)
Async XLA Ops:
  8.7 139.7 %all-gather.24.cloned.1.call-start = ((), (), s32[]{:S(2)}) async-start(), calls=%async_computation.16 | async-start | bytes 2359296 | tf_op jit(solution)/shard_map/all_gather | solution.py:232
  9.4 188.8 %all-gather.26.cloned.1.call-start = ((), (), s32[]{:S(2)}) async-start(), calls=%async_computation.17 | async-start | bytes 2359296 | tf_op jit(solution)/shard_map/all_gather | solution.py:233
  10.0 777.1 %all-gather.42.cloned.1.call-start = ((), (), s32[]{:S(2)}) async-start(), calls=%async_computation.36 | async-start | bytes 9437184 | tf_op jit(solution)/shard_map/all_gather | solution.py:23
  660.7 252.0 %all-gather.44.cloned.1.call-start = ((), (), s32[]{:S(2)}) async-start(), calls=%async_computation.37 | async-start | bytes 9437184 | tf_op jit(solution)/shard_map/all_gather | solution.py:23
  661.3 302.8 %all-gather.28.cloned.1.call-start = ((), (), s32[]{:S(2)}) async-start(), calls=%async_computation.18 | async-start | bytes 2359296 | tf_op jit(solution)/shard_map/all_gather | solution.py:238
  662.1 380.0 %reduce-scatter.21.cloned.1.call-start = ((), (), s32[]{:S(2)}) async-start(), calls=%async_computation.19 | async-start | bytes 10485760 | tf_op jit(solution)/shard_map/reduce_scatter | solution.py:310
  972.8 201.2 %all-gather.36.cloned.1.call-start = ((), (), s32[]{:S(2)}) async-start(), calls=%async_computation.23 | async-start | bytes 6488064 | tf_op jit(solution)/shard_map/all_gather | solution.py:241
  973.4 258.7 %all-gather.30.cloned.1.call-start = ((), (), s32[]{:S(2)}) async-start(), calls=%async_computation.20 | async-start | bytes 10485760 | tf_op jit(solution)/shard_map/all_gather | solution.py:312
  1045.6 281.4 %all-gather.34.cloned.1.call-start = ((), (), s32[]{:S(2)}) async-start(), calls=%async_computation.22 | async-start | bytes 6488064 | tf_op jit(solution)/shard_map/all_gather | solution.py:240
  1046.2 374.1 %all-gather.32.cloned.1.call-start = ((), (), s32[]{:S(2)}) async-start(), calls=%async_computation.21 | async-start | bytes 6488064 | tf_op jit(solution)/shard_map/all_gather | solution.py:239
  1047.0 480.6 %reduce-scatter.25.cloned.1.call-start = ((), (), s32[]{:S(2)}) async-start(), calls=%async_computation.26 | async-start | bytes 10485760 | tf_op jit(solution)/shard_map/reduce_scatter | solution.py:376
  1535.0 183.9 %all-gather.48.cloned.1.call-start = ((), (), s32[]{:S(2)}) async-start(), calls=%async_computation.39 | async-start | bytes 4718592 | tf_op jit(solution)/shard_map/all_gather | solution.py:41
  1582.8 1140.7 %reduce-scatter.37.cloned.1.call-start = ((), (), s32[]{:S(2)}) async-start(), calls=%async_computation.33 | async-start | bytes 6488064 | tf_op jit(solution)/shard_map/reduce_scatter | solution.py:487
  1594.1 1131.7 %reduce-scatter.39.cloned.1.call-start = ((), (), s32[]{:S(2)}) async-start(), calls=%async_computation.34 | async-start | bytes 6488064 | tf_op jit(solution)/shard_map/reduce_scatter | solution.py:490
  1605.2 1122.9 %reduce-scatter.41.cloned.1.call-start = ((), (), s32[]{:S(2)}) async-start(), calls=%async_computation.35 | async-start | bytes 6488064 | tf_op jit(solution)/shard_map/reduce_scatter | solution.py:493
  1615.9 1114.6 %reduce-scatter.35.cloned.1.call-start = ((), (), s32[]{:S(2)}) async-start(), calls=%async_computation.32 | async-start | bytes 2359296 | tf_op jit(solution)/shard_map/reduce_scatter | solution.py:484
  1643.0 1089.3 %reduce-scatter.45.cloned.1.call-start = ((), (), s32[]{:S(2)}) async-start(), calls=%async_computation.41 | async-start | bytes 36864
  2645.1 118.8 %reduce-scatter.43.cloned.1.call-start = ((), (), s32[]{:S(2)}) async-start(), calls=%async_computation.40 | async-start | bytes 589824
  2650.5 178.5 %reduce-scatter.47.cloned.1.call-start = ((), (), s32[]{:S(2)}) async-start(), calls=%async_computation.42 | async-start | bytes 589824
  2689.9 209.3 %reduce-scatter.31.cloned.1.call-start = ((), (), s32[]{:S(2)}) async-start(), calls=%async_computation.30 | async-start | bytes 2359296 | tf_op jit(solution)/shard_map/reduce_scatter | solution.py:466
  2696.1 273.2 %reduce-scatter.29.cloned.1.call-start = ((), (), s32[]{:S(2)}) async-start(), calls=%async_computation.29 | async-start | bytes 2359296 | tf_op jit(solution)/shard_map/reduce_scatter | solution.py:463
  2702.7 336.8 %reduce-scatter.33.cloned.1.call-start = ((), (), s32[]{:S(2)}) async-start(), calls=%async_computation.31 | async-start | bytes 2359296 | tf_op jit(solution)/shard_map/reduce_scatter | solution.py:469
  2710.1 375.5 %reduce-scatter.27.cloned.1.call-start = ((), (), s32[]{:S(2)}) async-start(), calls=%async_computation.28 | async-start | bytes 5242880 | tf_op jit(solution)/shard_map/reduce_scatter | solution.py:446
  2710.9 421.9 %reduce-scatter.23.cloned.1.call-start = ((), (), s32[]{:S(2)}) async-start(), calls=%async_computation.24 | async-start | bytes 5242880 | tf_op jit(solution)/shard_map/reduce_scatter | solution.py:323
  (135 other events, 5908.0 us)
Sparse Core Ops, SparseCore 0:
  48.9 49.5 all-gather.21
  100.6 47.7 all-gather.23
  150.4 47.7 all-gather.25
  660.9 126.1 all-gather.41
  789.6 123.1 all-gather.43
  914.8 49.2 all-gather.27
  972.2 69.8 reduce-scatter.20
  1080.3 93.5 all-gather.35
  1175.6 56.4 all-gather.29
  1234.4 92.6 all-gather.33
  1329.5 90.8 all-gather.31
  1457.6 69.9 reduce-scatter.24
  1571.2 73.3 all-gather.45
  1647.2 71.6 all-gather.47
  1722.4 108.4 reduce-scatter.36
  1834.6 110.7 reduce-scatter.38
  1948.9 109.6 reduce-scatter.40
  2062.2 68.6 reduce-scatter.34
  2645.2 53.7 reduce-scatter.44
  2702.9 60.9 reduce-scatter.42
  2768.0 60.9 reduce-scatter.46
  2832.5 66.5 reduce-scatter.30
  2902.5 66.7 reduce-scatter.28
  2972.7 66.7 reduce-scatter.32
  (5 shorter events, 193.8 us)
where the time goes:
time: 3160 us; the launch traced here: 3140 us
  waiting for transfers between devices  1300 us (41%)
  other arithmetic  1080 us (34%)
  matrix products  489 us (15%)
  blocking collectives  142 us (4%)
  local copies, waits for them, and re-layouts  98.9 us (3%)
    another operation x40, other arithmetic, block_step(): jax.scipy.linalg.solve_triangular(system, block_strength[..., None] * blo...  970 us
    all_gather x2, waiting for transfers between devices, entering(): everything = jax.tree.map(lambda part: lax.all_gather(part, axis), value)  223 us
    all_gather x1, waiting for transfers between devices, shards(): lax.all_gather(down_weight, 'dp', axis=1, tiled=True)  95.7 us
    all_gather x1, waiting for transfers between devices, shards(): lax.all_gather(up_weight, 'dp', axis=0, tiled=True)  86.4 us
    all_gather x1, waiting for transfers between devices, shards(): lax.all_gather(gate_weight, 'dp', axis=0, tiled=True)  81.6 us
    unnamed x32, waiting for transfers between devices  80 us
    all_gather x2, waiting for transfers between devices, entering_2(): lax.all_gather(part.astype(kind), axis)  75.9 us
    reduce_scatter x1, waiting for transfers between devices, shards(): lax.psum_scatter(back_second, 'tensor', scatter_dimension=1, tiled=True)  70 us
  transfers between devices with their start and end apart: 31, of which 23 were waited for; matrix products, arithmetic and copies ran while one was open for 36% of the time, Pallas kernels for 0%

commit v1 on v0

v1 whole, which is shorter than its diff:
```python
import functools

import jax
import jax.numpy as jnp
from jax import lax
from jax.experimental import pallas as pl
from jax.experimental.pallas import tpu as pltpu
from jax.sharding import PartitionSpec as P

HD = 128
KCONV = 4
RIM = 8
PAIR = 2

epsilon = 1e-06
f32 = jnp.float32
bf16 = jnp.bfloat16
MESH = pl.DeviceIdType.MESH
VMEM_LIMIT = 60 * 1024 * 1024


def halves(value):
    high = value.astype(bf16)
    return (high, (value - high.astype(f32)).astype(bf16))


def product(left, right, left_dim=1, right_dim=0):
    left = left if isinstance(left, tuple) else (left,)
    right = right if isinstance(right, tuple) else (right,)
    total = None
    for i, a in enumerate(left):
        for j, b in enumerate(right):
            if i + j < 2:
                term = lax.dot_general(
                    a, b, (((left_dim,), (right_dim,)), ((), ())), preferred_element_type=f32
                )
                total = term if total is None else total + term
    return total


def conv_act(x_ref, x_in, filt_ref, column, rows):
    x_ref[...] = x_in.astype(f32)
    running = None
    for tap in range(KCONV):
        term = filt_ref[pl.ds(column * KCONV + tap, 1), :] * x_ref[pl.ds(RIM - KCONV + 1 + tap, rows), :]
        running = term if running is None else running + term
    gate = jax.nn.sigmoid(running)
    return running, gate


def unit_scale(act):
    return lax.rsqrt(jnp.sum(act * act, axis=-1, keepdims=True) + epsilon)


def masks(rows):
    at_row = lax.broadcasted_iota(jnp.int32, (rows, rows), 0)
    at_col = lax.broadcasted_iota(jnp.int32, (rows, rows), 1)
    return at_row, at_col


def mixer_kernel(
    n, rows,
    pq_ref, pk_ref, pv_ref, strength_ref, filt_ref, gain_ref,
    normed_ref, mix_ref, carry_ref, inv_ref, kw_ref, state_ref,
    x_ref, low_ref, sol_ref, recv_ref, send_ref, send_sem, recv_sem,
):
    me = lax.axis_index("dp")
    seq, pair = pl.program_id(0), pl.program_id(1)
    step = seq * pl.num_programs(1) + pair
    steps = pl.num_programs(0) * pl.num_programs(1)

    def hop(at):
        return pltpu.make_async_remote_copy(
            src_ref=send_ref.at[at],
            dst_ref=recv_ref.at[at],
            send_sem=send_sem.at[at],
            recv_sem=recv_sem.at[at],
            device_id={"dp": lax.rem(me + 1, n)},
            device_id_type=MESH,
        )

    @pl.when(step == 0)
    def _():
        barrier = pltpu.get_barrier_semaphore()

        @pl.when(me > 0)
        def _():
            pl.semaphore_signal(barrier, inc=1, device_id={"dp": lax.rem(me + n - 1, n)}, device_id_type=MESH)

        @pl.when(me == 0)
        def _():
            recv_ref[...] = jnp.zeros_like(recv_ref)

        @pl.when(me < n - 1)
        def _():
            pl.semaphore_wait(barrier, 1)

    at_row, at_col = masks(rows)
    acts = []
    for column, ref in enumerate((pq_ref, pk_ref, pv_ref)):
        running, gate = conv_act(x_ref, ref[0], filt_ref, column, rows)
        acts.append(running * gate)
    strengths = strength_ref[0]
    lane = lax.broadcasted_iota(jnp.int32, strengths.shape, 1)
    heads = []
    for h in range(PAIR):
        cut = slice(h * HD, (h + 1) * HD)
        act_q, act_k = acts[0][:, cut], acts[1][:, cut]
        q = (act_q * unit_scale(act_q)).astype(bf16)
        k = (act_k * unit_scale(act_k)).astype(bf16)
        v = acts[2][:, cut].astype(bf16)
        beta = jnp.sum(jnp.where(lane == pair * PAIR + h, strengths, 0.0), axis=-1, keepdims=True)
        gram = product(k, k, 1, 1)
        low = jnp.where(at_row > at_col, beta * gram, 0.0)
        low_ref[h] = low
        first = (at_row & 1 == 1) & (at_row - 1 == at_col)
        sol_ref[h] = jnp.where(at_row == at_col, 1.0, 0.0) - jnp.where(first, low, 0.0)
        heads.append((q, k, v, beta))

    levels = (rows - 1).bit_length()

    def refine(level, carry):
        band_row, band_col = at_row >> level, at_col >> level
        band = (band_row & 1 == 1) & (band_row - 1 == band_col)
        sols = [halves(sol_ref[h]) for h in range(PAIR)]
        mids = [halves(product(halves(jnp.where(band, low_ref[h], 0.0)), sols[h])) for h in range(PAIR)]
        for h in range(PAIR):
            sol_ref[h] = sol_ref[h] - product(sols[h], mids[h])
        return carry

    lax.fori_loop(1, levels, refine, 0)

    wides = []
    for h in range(PAIR):
        q, k, v, beta = heads[h]
        inv = halves(sol_ref[h])
        inv_ref[h] = sol_ref[h]
        right = jnp.concatenate([beta * k.astype(f32), beta * v.astype(f32)], axis=1)
        wides.append(halves(product(inv, halves(right))))
    carries, bases, kws, ends = [], [], [], []
    for h in range(PAIR):
        q, k, v, beta = heads[h]
        scores = halves(jnp.where(at_row >= at_col, product(q, k, 1, 1), 0.0))
        seen = product(scores, wides[h])
        carry = q.astype(f32) - seen[:, :HD]
        carry_ref[0, :, h * HD : (h + 1) * HD] = carry
        carries.append(halves(carry))
        bases.append(seen[:, HD:])
        kwu = product(k, wides[h], 0, 0)
        kw_ref[h] = kwu[:, :HD]
        kws.append(halves(kwu[:, :HD]))
        ends.append(kwu[:, HD:])

    @pl.when(me > 0)
    def _():
        hop(step).wait_recv()

    states = [recv_ref[step, h] for h in range(PAIR)]
    for h in range(PAIR):
        out_state = ends[h] + states[h].astype(f32) - product(kws[h], states[h])
        send_ref[step, h] = out_state.astype(bf16)

    @pl.when(me < n - 1)
    def _():
        hop(step).start()

    for h in range(PAIR):
        cut = slice(h * HD, (h + 1) * HD)
        state_ref[h] = states[h]
        mix = bases[h] + product(carries[h], states[h])
        mix_ref[0, :, cut] = mix
        scale = lax.rsqrt(jnp.mean(mix * mix, axis=-1, keepdims=True) + epsilon)
        normed_ref[0, :, cut] = (mix * scale * gain_ref[...]).astype(bf16)

    @pl.when(step == steps - 1)
    def _():
        @pl.when(me < n - 1)
        def _():
            def done(at, carry):
                hop(at).wait_send()
                return carry

            lax.fori_loop(0, steps, done, 0)


def mixer(projected, strength, filters, gain):
    n = lax.axis_size("dp")
    seqs, extended, width = projected.shape
    rows = extended - RIM
    local = width // 3
    pairs = local // (PAIR * HD)
    wide = PAIR * HD

    def part(column):
        return pl.BlockSpec((1, extended, wide), lambda s, p: (s, 0, column * pairs + p))

    def flat():
        return pl.BlockSpec((1, rows, wide), lambda s, p: (s, 0, p))

    def square(size):
        return pl.BlockSpec((PAIR, size, size), lambda s, p: (s * pairs + p, 0, 0))

    total = seqs * pairs * PAIR
    return pl.pallas_call(
        functools.partial(mixer_kernel, n, rows),
        grid=(seqs, pairs),
        in_specs=[
            part(0), part(1), part(2),
            pl.BlockSpec((1, rows, strength.shape[2]), lambda s, p: (s, 0, 0)),
            pl.BlockSpec((3 * KCONV, wide), lambda s, p: (0, p)),
            pl.BlockSpec((1, HD), lambda s, p: (0, 0)),
        ],
        out_specs=[flat(), flat(), flat(), square(rows), square(HD), square(HD)],
        out_shape=[
            jax.ShapeDtypeStruct((seqs, rows, local), bf16),
            jax.ShapeDtypeStruct((seqs, rows, local), f32),
            jax.ShapeDtypeStruct((seqs, rows, local), f32),
            jax.ShapeDtypeStruct((total, rows, rows), f32),
            jax.ShapeDtypeStruct((total, HD, HD), f32),
            jax.ShapeDtypeStruct((total, HD, HD), bf16),
        ],
        scratch_shapes=[
            pltpu.VMEM((extended, wide), f32),
            pltpu.VMEM((PAIR, rows, rows), f32),
            pltpu.VMEM((PAIR, rows, rows), f32),
            pltpu.VMEM((seqs * pairs, PAIR, HD, HD), bf16),
            pltpu.VMEM((seqs * pairs, PAIR, HD, HD), bf16),
            pltpu.SemaphoreType.DMA((seqs * pairs,)),
            pltpu.SemaphoreType.DMA((seqs * pairs,)),
        ],
        compiler_params=pltpu.CompilerParams(
            collective_id=0, has_side_effects=True, vmem_limit_bytes=VMEM_LIMIT,
            dimension_semantics=("arbitrary", "arbitrary"),
        ),
        name="mixer",
    )(projected, projected, projected, strength, filters, gain)


def mixer_back_kernel(
    n, rows,
    pq_ref, pk_ref, pv_ref, strength_ref, filt_ref, gain_ref,
    back_ref, mix_ref, carry_ref, inv_ref, kw_ref, state_ref,
    proj_ref, last_ref, rim_ref, logit_ref, conv_ref, head_ref,
    xq_ref, xk_ref, xv_ref, bc_ref, recv_ref, send_ref, send_sem, recv_sem,
):
    me = lax.axis_index("dp")
    seq, pair = pl.program_id(0), pl.program_id(1)
    pairs = pl.num_programs(1)
    step = seq * pairs + pair
    steps = pl.num_programs(0) * pairs
    wide = PAIR * HD
    local = proj_ref.shape[2] // 3

    def hop(at):
        return pltpu.make_async_remote_copy(
            src_ref=send_ref.at[at],
            dst_ref=recv_ref.at[at],
            send_sem=send_sem.at[at],
            recv_sem=recv_sem.at[at],
            device_id={"dp": lax.rem(me + n - 1, n)},
            device_id_type=MESH,
        )

    @pl.when(step == 0)
    def _():
        barrier = pltpu.get_barrier_semaphore()

        @pl.when(me < n - 1)
        def _():
            pl.semaphore_signal(barrier, inc=1, device_id={"dp": lax.rem(me + 1, n)}, device_id_type=MESH)

        @pl.when(me == n - 1)
        def _():
            recv_ref[...] = jnp.zeros_like(recv_ref)

        @pl.when(me > 0)
        def _():
            pl.semaphore_wait(barrier, 1)

        head_ref[...] = jnp.zeros_like(head_ref)
        bc_ref[...] = jnp.zeros_like(bc_ref)
        conv_ref[...] = jnp.zeros_like(conv_ref)

    @pl.when(pair == 0)
    def _():
        logit_ref[...] = jnp.zeros_like(logit_ref)

    outs, kws, adds = [], [], []
    head_sum = jnp.zeros((1, HD), f32)
    for h in range(PAIR):
        cut = slice(h * HD, (h + 1) * HD)
        mix, back = mix_ref[0, :, cut], back_ref[0, :, cut]
        scale = lax.rsqrt(jnp.mean(mix * mix, axis=-1, keepdims=True) + epsilon)
        unit = mix * scale
        head_sum = head_sum + jnp.sum(back * unit, axis=0, keepdims=True)
        scaled = back * gain_ref[...]
        out = scale * (scaled - unit * jnp.mean(scaled * unit, axis=-1, keepdims=True))
        outs.append(halves(out))
        adds.append(product(halves(carry_ref[0, :, cut]), outs[h], 0, 0))
        kws.append(halves(kw_ref[h]))
    head_ref[...] += jnp.broadcast_to(head_sum, head_ref.shape) * jnp.where(
        lax.broadcasted_iota(jnp.int32, head_ref.shape, 0) == 0, 1.0, 0.0
    )

    @pl.when(me < n - 1)
    def _():
        hop(step).wait_recv()

    ends = [recv_ref[step, h] for h in range(PAIR)]
    for h in range(PAIR):
        before = adds[h] + ends[h].astype(f32) - product(kws[h], ends[h], 0, 0)
        send_ref[step, h] = before.astype(bf16)

    @pl.when(me > 0)
    def _():
        hop(step).start()

    at_row, at_col = masks(rows)
    strengths = strength_ref[0]
    lane = lax.broadcasted_iota(jnp.int32, strengths.shape, 1)
    run_q, gate_q = conv_act(xq_ref, pq_ref[0], filt_ref, 0, rows)
    run_k, gate_k = conv_act(xk_ref, pk_ref[0], filt_ref, 1, rows)
    run_v, gate_v = conv_act(xv_ref, pv_ref[0], filt_ref, 2, rows)
    act_q, act_k, act_v = run_q * gate_q, run_k * gate_k, run_v * gate_v
    back_acts = ([], [], [])
    for h in range(PAIR):
        cut = slice(h * HD, (h + 1) * HD)
        scale_q, scale_k = unit_scale(act_q[:, cut]), unit_scale(act_k[:, cut])
        unit_q, unit_k = act_q[:, cut] * scale_q, act_k[:, cut] * scale_k
        q, k, v = unit_q.astype(bf16), unit_k.astype(bf16), act_v[:, cut].astype(bf16)
        chosen = lane == pair * PAIR + h
        beta = jnp.sum(jnp.where(chosen, strengths, 0.0), axis=-1, keepdims=True)
        gram = product(k, k, 1, 1)
        scores = halves(jnp.where(at_row >= at_col, product(q, k, 1, 1), 0.0))
        state, end, out = state_ref[h], ends[h], outs[h]
        inv = halves(inv_ref[h])
        rest = v.astype(f32) - product(k, state)
        update = halves(product(inv, halves(beta * rest)))
        back_update = product(scores, out, 0, 0) + product(k, end)
        back_scores = halves(jnp.where(at_row >= at_col, product(out, update, 1, 1), 0.0))
        solved = product(inv, halves(back_update), 0, 0)
        solved_terms = halves(solved)
        back_low = jnp.where(at_row > at_col, -product(solved_terms, update, 1, 1), 0.0)
        back_beta = jnp.sum(back_low * gram, axis=-1, keepdims=True) + jnp.sum(
            solved * rest, axis=-1, keepdims=True
        )
        back_gram = beta * back_low
        back_gram = halves(back_gram + back_gram.T)
        back_value = beta * solved
        back_q = product(out, state, 1, 1) + product(back_scores, k)
        back_k = (
            product(back_scores, q, 0, 0)
            + product(update, end, 1, 1)
            + product(back_gram, k)
            - product(halves(back_value), state, 1, 1)
        )
        logit_ref[0] += jnp.where(chosen, back_beta * beta * (1.0 - beta), 0.0)
        back_acts[0].append(
            (back_q - unit_q * jnp.sum(unit_q * back_q, axis=-1, keepdims=True)) * scale_q
        )
        back_acts[1].append(
            (back_k - unit_k * jnp.sum(unit_k * back_k, axis=-1, keepdims=True)) * scale_k
        )
        back_acts[2].append(back_value)

    for column, (running, gate, x_ref) in enumerate(
        ((run_q, gate_q, xq_ref), (run_k, gate_k, xk_ref), (run_v, gate_v, xv_ref))
    ):
        back_conv = jnp.concatenate(back_acts[column], axis=1) * gate * (1.0 + running * (1.0 - gate))
        bc_ref[pl.ds(RIM, rows), :] = back_conv
        back_x, back_rim = None, None
        for tap in range(KCONV):
            weight = filt_ref[pl.ds(column * KCONV + tap, 1), :]
            term = weight * bc_ref[pl.ds(RIM + KCONV - 1 - tap, rows), :]
            edge = weight * bc_ref[pl.ds(KCONV - 1 - tap, RIM), :]
            back_x = term if back_x is None else back_x + term
            back_rim = edge if back_rim is None else back_rim + edge
            grad = jnp.sum(
                back_conv * x_ref[pl.ds(RIM - KCONV + 1 + tap, rows), :], axis=0, keepdims=True
            )
            conv_ref[pair, pl.ds(column * KCONV + tap, 1), :] += grad
        lanes = pl.ds(pl.multiple_of(column * local + pair * wide, wide), wide)
        proj_ref[0, :, lanes] = back_x.astype(bf16)
        last_ref[0, :, lanes] = back_x[rows - RIM :, :]
        rim_ref[0, :, lanes] = back_rim.astype(bf16)

    @pl.when(step == steps - 1)
    def _():
        @pl.when(me > 0)
        def _():
            def done(at, carry):
                hop(at).wait_send()
                return carry

            lax.fori_loop(0, steps, done, 0)


def mixer_back(projected, strength, filters, gain, back_normed, mix, carry, inverse, kw, state):
    n = lax.axis_size("dp")
    seqs, extended, width = projected.shape
    rows = extended - RIM
    local = width // 3
    pairs = local // (PAIR * HD)
    wide = PAIR * HD

    def part(column):
        return pl.BlockSpec((1, extended, wide), lambda s, p: (s, 0, column * pairs + p))

    def flat():
        return pl.BlockSpec((1, rows, wide), lambda s, p: (s, 0, p))

    def square(size):
        return pl.BlockSpec((PAIR, size, size), lambda s, p: (s * pairs + p, 0, 0))

    def whole(size, span):
        return pl.BlockSpec((1, size, span), lambda s, p: (s, 0, 0))

    heads = strength.shape[2]
    return pl.pallas_call(
        functools.partial(mixer_back_kernel, n, rows),
        grid=(seqs, pairs),
        in_specs=[
            part(0), part(1), part(2),
            whole(rows, heads),
            pl.BlockSpec((3 * KCONV, wide), lambda s, p: (0, p)),
            pl.BlockSpec((1, HD), lambda s, p: (0, 0)),
            flat(), flat(), flat(), square(rows), square(HD), square(HD),
        ],
        out_specs=[
            whole(rows, width), whole(RIM, width), whole(RIM, width), whole(rows, heads),
            pl.BlockSpec((pairs, 3 * KCONV, wide), lambda s, p: (0, 0, 0)),
            pl.BlockSpec((8, HD), lambda s, p: (0, 0)),
        ],
        out_shape=[
            jax.ShapeDtypeStruct((seqs, rows, width), bf16),
            jax.ShapeDtypeStruct((seqs, RIM, width), f32),
            jax.ShapeDtypeStruct((seqs, RIM, width), bf16),
            jax.ShapeDtypeStruct((seqs, rows, heads), f32),
            jax.ShapeDtypeStruct((pairs, 3 * KCONV, wide), f32),
            jax.ShapeDtypeStruct((8, HD), f32),
        ],
        scratch_shapes=[
            pltpu.VMEM((extended, wide), f32),
            pltpu.VMEM((extended, wide), f32),
            pltpu.VMEM((extended, wide), f32),
            pltpu.VMEM((rows + 2 * RIM, wide), f32),
            pltpu.VMEM((seqs * pairs, PAIR, HD, HD), bf16),
            pltpu.VMEM((seqs * pairs, PAIR, HD, HD), bf16),
            pltpu.SemaphoreType.DMA((seqs * pairs,)),
            pltpu.SemaphoreType.DMA((seqs * pairs,)),
        ],
        compiler_params=pltpu.CompilerParams(
            collective_id=1, has_side_effects=True, vmem_limit_bytes=VMEM_LIMIT,
            dimension_semantics=("arbitrary", "arbitrary"),
        ),
        name="mixer_back",
    )(
        projected, projected, projected, strength, filters, gain,
        back_normed, mix, carry, inverse, kw, state,
    )


def from_behind(block, axis, distance):
    devices = range(lax.axis_size(axis))
    route = [(i - distance, i) for i in devices if i - distance in devices]
    return lax.ppermute(block, axis, route)


def rms_unit(values):
    scale = lax.rsqrt(jnp.mean(values * values, axis=-1, keepdims=True) + epsilon)
    return values * scale, scale


def rms_back(back, unit, scale, gain):
    scaled = back * gain
    return scale * (scaled - unit * jnp.mean(scaled * unit, axis=-1, keepdims=True))


def matmul(spec, left, right):
    return jnp.einsum(spec, left, right, preferred_element_type=f32)


def shards(
    tokens,
    cotangent,
    query_weight,
    key_weight,
    value_weight,
    beta_weight,
    conv_filter,
    norm_gain,
    head_gain,
    out_weight,
    gate_weight,
    up_weight,
    down_weight,
):
    n = lax.axis_size("dp")
    tensor = lax.axis_size("tensor")
    seqs, own_len, width = tokens.shape
    local = query_weight.shape[1]
    heads = local // HD
    hidden = gate_weight.shape[1]

    full_small = lax.all_gather(
        jnp.concatenate(
            [conv_filter.reshape(-1), norm_gain.reshape(-1), head_gain, beta_weight.reshape(-1)]
        ),
        "dp",
    )
    full_qkv = lax.all_gather(
        jnp.concatenate([query_weight, key_weight, value_weight], axis=1), "dp", axis=0, tiled=True
    )
    full_out = lax.all_gather(out_weight.T, "dp", axis=0, tiled=True)
    full_gate_up = lax.all_gather(
        jnp.concatenate([gate_weight, up_weight], axis=1), "dp", axis=0, tiled=True
    )
    full_down = lax.all_gather(down_weight.T, "dp", axis=0, tiled=True)
    sizes = [conv_filter.size, norm_gain.size, head_gain.size, beta_weight.size]
    ends = [sum(sizes[: i + 1]) for i in range(4)]
    filters = (
        full_small[:, : ends[0]]
        .reshape(n, 3 * KCONV, heads, HD // n)
        .transpose(1, 2, 0, 3)
        .reshape(3 * KCONV, local)
        .astype(f32)
    )
    gains = (
        full_small[:, ends[0] : ends[1]].reshape(n, 2, width // n).transpose(1, 0, 2).reshape(2, width)
    ).astype(f32)
    head_row = full_small[:, ends[1] : ends[2]].reshape(1, HD).astype(f32)
    full_beta = full_small[:, ends[2] :].reshape(width, heads)

    rows_tokens = lax.all_gather(tokens, "tensor", axis=1, tiled=True)
    rows_cotangent = lax.all_gather(cotangent, "tensor", axis=1, tiled=True)
    rim_tokens = from_behind(rows_tokens[:, -RIM:], "dp", 1)
    extended = jnp.concatenate([rim_tokens, rows_tokens], axis=1).astype(f32)
    unit_ext, _ = rms_unit(extended)
    normed_ext = (unit_ext * gains[0]).astype(bf16)
    normed_first = normed_ext[:, RIM:]
    projected = matmul("std,dm->stm", normed_ext, full_qkv).astype(bf16)
    strength = jax.nn.sigmoid(matmul("std,dh->sth", normed_first, full_beta))
    normed_mix, mix, carry, inverse, kw, state = mixer(projected, strength, filters, head_row)

    branch_part = matmul("stk,dk->std", normed_mix, full_out)
    branch = lax.psum_scatter(branch_part.astype(bf16), "tensor", scatter_dimension=1, tiled=True)
    own_tokens = tokens.astype(f32)
    hidden_state = own_tokens + branch.astype(f32)
    unit_second, scale_second = rms_unit(hidden_state)
    normed_second = lax.all_gather(
        (unit_second * gains[1]).astype(bf16), "tensor", axis=1, tiled=True
    )
    gate_up = matmul("std,df->stf", normed_second, full_gate_up)
    gate_pre, up_pre = gate_up[..., :hidden], gate_up[..., hidden:]
    gate_sigmoid = jax.nn.sigmoid(gate_pre)
    ffn_hidden = (gate_pre * gate_sigmoid * up_pre).astype(bf16)
    ffn_part = matmul("stf,df->std", ffn_hidden, full_down)
    ffn_branch = lax.psum_scatter(
        ffn_part.astype(bf16), "tensor", scatter_dimension=1, tiled=True
    ).astype(f32)
    layer_out = (hidden_state + ffn_branch).astype(bf16)

    back_hidden = matmul("std,df->stf", rows_cotangent, full_down)
    back_gate = (
        back_hidden * up_pre * gate_sigmoid * (1.0 + gate_pre * (1.0 - gate_sigmoid))
    ).astype(bf16)
    back_up = (back_hidden * gate_pre * gate_sigmoid).astype(bf16)
    back_gate_up = jnp.concatenate([back_gate, back_up], axis=2)
    back_second = matmul("stf,df->std", back_gate_up, full_gate_up)
    back_second_rows = lax.psum_scatter(
        back_second.astype(bf16), "tensor", scatter_dimension=1, tiled=True
    ).astype(f32)
    grad_down = matmul("std,stf->df", rows_cotangent, ffn_hidden)
    grad_gate_up = matmul("std,stf->df", normed_second, back_gate_up)
    gain_second = jnp.sum(back_second_rows * unit_second, axis=(0, 1))
    back_state = cotangent.astype(f32) + rms_back(back_second_rows, unit_second, scale_second, gains[1])
    rows_back = lax.all_gather(back_state.astype(bf16), "tensor", axis=1, tiled=True)
    grad_out = matmul("std,stk->dk", rows_back, normed_mix)
    back_normed = matmul("std,dk->stk", rows_back, full_out)
    back_proj, last, rim, back_logit, conv_part, head_part = mixer_back(
        projected, strength, filters, head_row, back_normed, mix, carry, inverse, kw, state
    )
    rim = from_behind(rim, "dp", -1).astype(f32)
    back_proj = lax.dynamic_update_slice_in_dim(
        back_proj, (last + rim).astype(bf16), back_proj.shape[1] - RIM, 1
    )
    back_logit = back_logit.astype(bf16)
    grad_qkv = matmul("std,stm->dm", normed_first, back_proj)
    grad_beta = matmul("std,sth->dh", normed_first, back_logit)
    back_first = matmul("stm,dm->std", back_proj, full_qkv) + matmul(
        "sth,dh->std", back_logit, full_beta
    )
    back_first_rows = lax.psum_scatter(
        back_first.astype(bf16), "tensor", scatter_dimension=1, tiled=True
    ).astype(f32)
    unit_first, scale_first = rms_unit(own_tokens)
    gain_first = jnp.sum(back_first_rows * unit_first, axis=(0, 1))
    d_tokens = (back_state + rms_back(back_first_rows, unit_first, scale_first, gains[0])).astype(bf16)

    grad_conv = conv_part.transpose(1, 0, 2).reshape(3 * KCONV, local)
    shared = lax.psum(jnp.concatenate([gain_first, gain_second, head_part[0]]), "tensor")

    def scatter(grad):
        return lax.psum_scatter(grad.astype(bf16), "dp", scatter_dimension=0, tiled=True).astype(f32)

    small = jnp.concatenate(
        [
            grad_conv.reshape(3 * KCONV, heads, n, HD // n).transpose(2, 0, 1, 3).reshape(n, -1),
            shared[: 2 * width].reshape(2, n, width // n).transpose(1, 0, 2).reshape(n, -1),
            shared[2 * width :].reshape(n, HD // n),
            grad_beta.reshape(n, -1),
        ],
        axis=1,
    )
    small = scatter(small)[0]
    grad_down = scatter(grad_down).T
    grad_gate_up = scatter(grad_gate_up)
    grad_out = scatter(grad_out).T
    grad_qkv = scatter(grad_qkv)
    return (
        layer_out,
        d_tokens,
        grad_qkv[:, :local],
        grad_qkv[:, local : 2 * local],
        grad_qkv[:, 2 * local :],
        small[ends[2] :].reshape(beta_weight.shape),
        small[: ends[0]].reshape(conv_filter.shape),
        small[ends[0] : ends[1]].reshape(norm_gain.shape),
        small[ends[1] : ends[2]],
        grad_out,
        grad_gate_up[:, :hidden],
        grad_gate_up[:, hidden:],
        grad_down,
    )


def solution(mesh):
    both = P(None, ("dp", "tensor"), None)
    rows, cols = P("dp", "tensor"), P("tensor", "dp")
    conv, gain, head = P(None, "tensor", "dp"), P(None, "dp"), P("dp")
    return jax.shard_map(
        shards,
        mesh=mesh,
        in_specs=(both, both, rows, rows, rows, rows, conv, gain, head, cols, rows, rows, cols),
        out_specs=(both, both, rows, rows, rows, rows, conv, gain, head, cols, rows, rows, cols),
        check_vma=False,
    )
```

time: 3160 us -> 1380 us (0.44)
  other arithmetic: 1080 us -> 29.3 us
  waiting for transfers between devices: 1300 us -> 895 us
  matrix products: 489 us -> 151 us
  Pallas kernels: 0 us -> 147 us
  local copies, waits for them, and re-layouts: 98.9 us -> 29.9 us
  blocking collectives: 142 us -> 87.1 us
    another operation x48 -> x0, other arithmetic: 975 us -> none  [the longest x40 970 us: block_step(): jax.scipy.linalg.solve_triangular(system, block_strength[..., None] * blo...]
    all_gather x15 -> x8, waiting for transfers between devices: 789 us -> 412 us  [the longest x1 160 us: shards(): lax.all_gather(jnp.concatenate([gate_weight, up_weight], axis=1), 'dp', a...]
    dot_general x105 -> x15, matrix products: 421 us -> 151 us  [matmul(): return jnp.einsum(spec, left, right, preferred_element_type=f32)]
    pallas_call x0 -> x2, Pallas kernels: none -> 147 us  [the longest x1 83 us: mixer_back(): pl.pallas_call(functools.partial(mixer_back_kernel, n, rows), grid=(seqs,...]
    all_gather x3 -> x0, blocking collectives: 79 us -> none  [the longest x1 32.3 us: shards(): lax.all_gather(conv_filter, 'dp', axis=2, tiled=True)]
    unnamed x32 -> x16, waiting for transfers between devices: 80 us -> 1.61 us
    another operation x24 -> x0, matrix products: 68.1 us -> none  [block_step(): jax.scipy.linalg.solve_triangular(system, block_strength[..., None] * blo...]
    reduce_scatter x11 -> x8, waiting for transfers between devices: 434 us -> 477 us  [the longest x4 330 us: scatter(): lax.psum_scatter(grad.astype(bf16), 'dp', scatter_dimension=0, tiled=True)]
  transfers between devices with their start and end apart: 31 -> 18, of which waited for: 23 -> 14; matrix products, arithmetic and copies ran while one was open for 36% -> 11% of each run, Pallas kernels for 0% -> 11%
where the time goes in v1:
time: 1380 us; the launch traced here: 1370 us
  waiting for transfers between devices  895 us (65%)
  matrix products  151 us (11%)
  Pallas kernels  147 us (11%)
  blocking collectives  87.1 us (6%)
  local copies, waits for them, and re-layouts  29.9 us (2%)
  other arithmetic  29.3 us (2%)
  between operations  15.5 us (1%)
  starting transfers between devices  13.8 us (1%)
    reduce_scatter x4, waiting for transfers between devices, scatter(): lax.psum_scatter(grad.astype(bf16), 'dp', scatter_dimension=0, tiled=True)  330 us
    all_gather x1, waiting for transfers between devices, shards(): lax.all_gather(jnp.concatenate([gate_weight, up_weight], axis=1), 'dp', a...  160 us
    dot_general x15, matrix products, matmul(): return jnp.einsum(spec, left, right, preferred_element_type=f32)  151 us
    all_gather x1, waiting for transfers between devices, shards(): full_down = lax.all_gather(down_weight.T, 'dp', axis=0, tiled=True)  95.7 us
    pallas_call x1, Pallas kernels, mixer_back(): pl.pallas_call(functools.partial(mixer_back_kernel, n, rows), grid=(seqs,...  83 us
    all_gather x1, waiting for transfers between devices, shards(): lax.all_gather(jnp.concatenate([query_weight, key_weight, value_weight],...  80.2 us
    unnamed x2, blocking collectives  76.8 us
    reduce_scatter x1, waiting for transfers between devices, shards(): lax.psum_scatter(branch_part.astype(bf16), 'tensor', scatter_dimension=1,...  71.5 us
  transfers between devices with their start and end apart: 18, of which 14 were waited for; matrix products, arithmetic and copies ran while one was open for 11% of the time, Pallas kernels for 11%

profile of v1, /device:TPU:0, one launch (start us, length us, event | category | flops | bytes accessed | tf_op | source)
XLA Modules:
  0.0 1368.7 jit_solution(9637217598610071506)
XLA Ops:
  14.1 39.2 %all-reduce = bf16[18560]{0:T(1024)(128)(2,1)S(1)} all-reduce(bf16[18560]{0:T(1024)(128)(2,1)S(1)} %dynamic-update-slice), channel_id=2, replica_groups=mesh['dp'=8,'tensor'=4] {'dp'}, use_global_device_ids=true, to_apply=%add | all-reduce | flops 18560 | bytes 74240
  68.5 80.2 %all-gather.12.cloned.1.call-done = bf16[2048,1536]{1,0:T(8,128)(2,1)} async-done(((bf16[256,1536]{1,0:T(8,128)(2,1)}), bf16[2048,1536]{1,0:T(8,128)(2,1)}) %all-gather.12.cloned.1.call-update) | async-done | bytes 6291472 | tf_op jit(solution)/shard_map/all_gather | solution.py:511
  148.7 11.5 fusion.16.pq_ref.pk_ref.pv_ref
  160.2 64.4 %mixer.1 = (bf16[4,256,512]{2,1,0:T(8,128)(2,1)}, f32[4,256,512]{2,1,0:T(8,128)}, f32[4,256,512]{2,1,0:T(8,128)}, f32[16,256,256]{2,1,0:T(8,128)}, f32[16,128,12...) custom-call(bf16[4,264,1536]{2,1,0:T(8,128)(2,1)} %fusion.16.pq_ref.pk_ref.pv_ref, ...), custom_call_target="tpu_custom_call" | custom-call | tf_op jit(solution)/shard_map/mixer/pallas_call | solution.py:204
  233.5 71.5 %reduce-scatter.9.cloned.1.call-done = bf16[4,64,2048]{2,1,0:T(8,128)(2,1)} async-done(((bf16[4,256,2048]{2,1,0:T(8,128)(2,1)}), bf16[4,64,2048]{2,1,0:T(8,128)(2,1)}) %reduce-scatter.9.cloned.1.call-update) | async-done | bytes 1048592 | tf_op jit(solution)/shard_map/reduce_scatter | solution.py:546
  311.6 160.0 %all-gather.18.cloned.1.call-done = bf16[2048,2816]{1,0:T(8,128)(2,1)} async-done(((bf16[256,2816]{1,0:T(8,128)(2,1)}), bf16[2048,2816]{1,0:T(8,128)(2,1)}) %all-gather.18.cloned.1.call-update) | async-done | bytes 11534352 | tf_op jit(solution)/shard_map/all_gather | solution.py:515
  471.6 34.8 %all-gather.16.cloned.1.call-done = bf16[4,256,2048]{2,1,0:T(8,128)(2,1)} async-done(((bf16[4,64,2048]{2,1,0:T(8,128)(2,1)}), bf16[4,256,2048]{2,1,0:T(8,128)(2,1)}) %all-gather.16.cloned.1.call-update) | async-done | bytes 4194320 | tf_op jit(solution)/shard_map/all_gather | solution.py:550
  506.4 18.7 %fusion.2 = f32[4,256,2816]{2,1,0:T(8,128)} fusion(bf16[4,256,2048]{2,1,0:T(8,128)(2,1)} %all-gather.16.cloned.1.call-done, bf16[2048,2816]{1,0:T(8,128)(2,1)} %all-gather.18.cloned.1.call-done), kind=kOutput, calls=%fused_computation.5 | convolution fusion | flops 11811160064 | bytes 27262976 | tf_op jit(solution)/shard_map/std,df->stf/dot_general | solution.py:480
  525.1 17.4 %all-gather.22.cloned.1.call-done = bf16[4,256,2048]{2,1,0:T(8,128)(2,1)} async-done(((bf16[4,64,2048]{2,1,0:T(8,128)(2,1)}), bf16[4,256,2048]{2,1,0:T(8,128)(2,1)}) %all-gather.22.cloned.1.call-update) | async-done | bytes 4194320 | tf_op jit(solution)/shard_map/all_gather | solution.py:535
  542.5 95.7 %all-gather.20.cloned.1.call-done = bf16[2048,1408]{1,0:T(8,128)(2,1)} async-done(((bf16[256,1408]{1,0:T(8,128)(2,1)}), bf16[2048,1408]{1,0:T(8,128)(2,1)}) %all-gather.20.cloned.1.call-update) | async-done | bytes 5767184 | tf_op jit(solution)/shard_map/all_gather | solution.py:518
  638.2 14.7 %multiply_convert_fusion.1 = (bf16[4,256,1408]{2,1,0:T(8,128)(2,1)S(1)}, bf16[4,256,1408]{2,1,0:T(8,128)(2,1)S(1)}, bf16[4,256,1408]{2,1,0:T(8,128)(2,1)}) fusion(f32[4,256,2816]{2,1,0:T(8,128)} %fusion.2, bf16[4,256,2048]{2,1,0:T(8,128)(2,1)} %all-gather.22.cloned.1.call-done, bf16[2048,1408]{1,0:T(8,128)(2,1)} %all-gather.20.cloned.1.call-done), kind=kOutput, calls=%fused_computation.24 | convolution fusion | flops 5928648704 | bytes 30146560 | tf_op jit(solution)/shard_map/std,df->stf/dot_general | solution.py:480
  655.4 16.4 %fusion.22 = bf16[4,256,2048]{2,1,0:T(8,128)(2,1)} fusion(bf16[2048,2816]{1,0:T(8,128)(2,1)} %all-gather.18.cloned.1.call-done, bf16[4,256,1408]{2,1,0:T(8,128)(2,1)S(1)} %get-tuple-element.108, bf16[4,256,1408]{2,1,0:T(8,128)(2,1)S(1)} %get-tuple-element.107), kind=kOutput, calls=%fused_computation.32 | convolution fusion | flops 11824791552 | bytes 21495808 | tf_op jit(solution)/shard_map/stf,df->std/dot_general | solution.py:480
  681.7 33.0 %reduce-scatter.13.cloned.1.call-done = bf16[4,64,2048]{2,1,0:T(8,128)(2,1)} async-done(((bf16[4,256,2048]{2,1,0:T(8,128)(2,1)}), bf16[4,64,2048]{2,1,0:T(8,128)(2,1)}) %reduce-scatter.13.cloned.1.call-update) | async-done | bytes 1048592 | tf_op jit(solution)/shard_map/reduce_scatter | solution.py:570
  730.8 24.1 %all-gather.24.cloned.1.call-done = bf16[4,256,2048]{2,1,0:T(8,128)(2,1)} async-done(((bf16[4,64,2048]{2,1,0:T(8,128)(2,1)}), bf16[4,256,2048]{2,1,0:T(8,128)(2,1)}) %all-gather.24.cloned.1.call-update) | async-done | bytes 4194320 | tf_op jit(solution)/shard_map/all_gather | solution.py:577
  761.2 18.4 %bitcast_convert_fusion = bf16[2048,2816]{1,0:T(8,128)(2,1)} fusion(bf16[4,256,2048]{2,1,0:T(8,128)(2,1)} %all-gather.16.cloned.1.call-done, bf16[4,256,1408]{2,1,0:T(8,128)(2,1)} %copy-done.22, bf16[4,256,1408]{2,1,0:T(8,128)(2,1)} %copy-done.21), kind=kOutput, calls=%fused_computation | convolution fusion | flops 11828461568 | bytes 21495808 | tf_op jit(solution)/shard_map/std,stf->df/dot_general | solution.py:480
  786.4 83.0 %mixer_back.1 = (bf16[4,256,1536]{2,1,0:T(8,128)(2,1)}, f32[4,8,1536]{2,1,0:T(8,128)}, bf16[4,8,1536]{2,1,0:T(8,128)(2,1)}, f32[4,256,4]{2,1,0:T(8,128)}, f32[2,12,256]{2,1,0:T(8,128)}, /*index=5*/f32[8,128]{1,0:T(8,128)}) custom-call(bf16[4,264,1536]{2,1,0:T(8,128)(2,1)} %fusion.16.pq_ref.pk_ref.pv_ref, bf16[4,264,1536]{2,1,0:T(8,128)(2,1)} %fusion.16.pq_ref.pk_ref.pv_ref, ...), custom_call_target="tpu_custom_call" | custom-call | tf_op jit(solution)/shard_map/mixer_back/pallas_call | solution.py:419
  877.8 11.1 add_convert_fusion
  889.1 11.0 fusion.19
  900.4 11.7 bitcast_convert_fusion.1
  921.5 28.2 %reduce-scatter.19.cloned.1.call-done = bf16[256,512]{1,0:T(8,128)(2,1)} async-done(((bf16[2048,512]{1,0:T(8,128)(2,1)}), bf16[256,512]{1,0:T(8,128)(2,1)}) %reduce-scatter.19.cloned.1.call-update) | async-done | bytes 262160 | tf_op jit(solution)/shard_map/reduce_scatter | solution.py:604
  953.6 191.4 %reduce-scatter.21.cloned.1.call-done = bf16[256,2816]{1,0:T(8,128)(2,1)} async-done(((bf16[2048,2816]{1,0:T(8,128)(2,1)}), bf16[256,2816]{1,0:T(8,128)(2,1)}) %reduce-scatter.21.cloned.1.call-update) | async-done | bytes 1441808 | tf_op jit(solution)/shard_map/reduce_scatter | solution.py:604
  1148.1 42.9 %reduce-scatter.15.cloned.1.call-done = bf16[4,64,2048]{2,1,0:T(8,128)(2,1)} async-done(((bf16[4,256,2048]{2,1,0:T(8,128)(2,1)}), bf16[4,64,2048]{2,1,0:T(8,128)(2,1)}) %reduce-scatter.15.cloned.1.call-update) | async-done | bytes 1048592 | tf_op jit(solution)/shard_map/reduce_scatter | solution.py:593
  1203.4 37.6 %all-reduce.1 = bf16[8,2320]{1,0:T(8,128)(2,1)S(1)} all-reduce(bf16[8,2320]{1,0:T(8,128)(2,1)S(1)} %concatenate.28), channel_id=8, replica_groups=mesh['dp'=8,'tensor'=4] {'dp'}, use_global_device_ids=true, to_apply=%region_13.0.clone | all-reduce | flops 18560 | bytes 74240
  1249.3 110.2 %reduce-scatter.17.cloned.1.call-done = bf16[256,1536]{1,0:T(8,128)(2,1)} async-done(((bf16[2048,1536]{1,0:T(8,128)(2,1)}), bf16[256,1536]{1,0:T(8,128)(2,1)}) %reduce-scatter.17.cloned.1.call-update) | async-done | bytes 786448 | tf_op jit(solution)/shard_map/reduce_scatter | solution.py:604
  (163 shorter events, 126.1 us)
Async XLA Ops:
  7.2 46.9 %all-gather.10.cloned.1.call-start = ((), (), s32[]{:S(2)}) async-start(), calls=%async_computation.8 | async-start | bytes 5242880 | tf_op jit(solution)/shard_map/all_gather | solution.py:534
  8.0 140.7 %all-gather.12.cloned.1.call-start = ((), (), s32[]{:S(2)}) async-start(), calls=%async_computation.9 | async-start | bytes 7077888 | tf_op jit(solution)/shard_map/all_gather | solution.py:511
  10.1 214.6 %all-gather.14.cloned.1.call-start = ((), (), s32[]{:S(2)}) async-start(), calls=%async_computation.10 | async-start | bytes 2359296 | tf_op jit(solution)/shard_map/all_gather | solution.py:514
  12.0 293.1 %reduce-scatter.9.cloned.1.call-start = ((), (), s32[]{:S(2)}) async-start(), calls=%async_computation.11 | async-start | bytes 5242880 | tf_op jit(solution)/shard_map/reduce_scatter | solution.py:546
  55.1 4.8 collective-permute-start
  230.9 74.1 %copy-start = (bf16[4,64,2048]{2,1,0:T(8,128)(2,1)S(1)}, bf16[4,64,2048]{2,1,0:T(8,128)(2,1)}, u32[]{:S(2)}) copy-start(bf16[4,64,2048]{2,1,0:T(8,128)(2,1)} %param.13) | copy-start | bytes 3145732
  230.9 240.6 %all-gather.18.cloned.1.call-start = ((), (), s32[]{:S(2)}) async-start(), calls=%async_computation.13 | async-start | bytes 12976128 | tf_op jit(solution)/shard_map/all_gather | solution.py:515
  233.4 77.0 %copy-start.7 = (bf16[1408,256]{1,0:T(8,128)(2,1)S(1)}, bf16[1408,256]{1,0:T(8,128)(2,1)}, u32[]{:S(2)}) copy-start(bf16[1408,256]{1,0:T(8,128)(2,1)} %param.25) | copy-start | bytes 2162692
  233.5 272.9 %all-gather.16.cloned.1.call-start = ((), (), s32[]{:S(2)}) async-start(), calls=%async_computation.12 | async-start | bytes 5242880 | tf_op jit(solution)/shard_map/all_gather | solution.py:550
  309.3 233.2 %all-gather.22.cloned.1.call-start = ((), (), s32[]{:S(2)}) async-start(), calls=%async_computation.16 | async-start | bytes 5242880 | tf_op jit(solution)/shard_map/all_gather | solution.py:535
  310.1 328.1 %all-gather.20.cloned.1.call-start = ((), (), s32[]{:S(2)}) async-start(), calls=%async_computation.14 | async-start | bytes 6488064 | tf_op jit(solution)/shard_map/all_gather | solution.py:518
  311.6 403.1 %reduce-scatter.13.cloned.1.call-start = ((), (), s32[]{:S(2)}) async-start(), calls=%async_computation.17 | async-start | bytes 5242880 | tf_op jit(solution)/shard_map/reduce_scatter | solution.py:570
  671.8 42.9 %copy-start.1 = (bf16[4,64,2048]{2,1,0:T(8,128)(2,1)S(1)}, bf16[4,64,2048]{2,1,0:T(8,128)(2,1)}, u32[]{:S(2)}) copy-start(bf16[4,64,2048]{2,1,0:T(8,128)(2,1)} %reduce-scatter.9.cloned.1.call-done) | copy-start | bytes 3145732
  671.8 45.2 %copy-start.3 = (bf16[4,64,2048]{2,1,0:T(8,128)(2,1)S(1)}, bf16[4,64,2048]{2,1,0:T(8,128)(2,1)}, u32[]{:S(2)}) copy-start(bf16[4,64,2048]{2,1,0:T(8,128)(2,1)} %param.14) | copy-start | bytes 3145732
  671.8 83.1 %all-gather.24.cloned.1.call-start = ((), (), s32[]{:S(2)}) async-start(), calls=%async_computation.18 | async-start | bytes 5242880 | tf_op jit(solution)/shard_map/all_gather | solution.py:577
  720.3 191.9 %reduce-scatter.23.cloned.1.call-start = ((), (), s32[]{:S(2)}) async-start(), calls=%async_computation.23 | async-start | bytes 6488064 | tf_op jit(solution)/shard_map/reduce_scatter | solution.py:604
  730.8 219.0 %reduce-scatter.19.cloned.1.call-start = ((), (), s32[]{:S(2)}) async-start(), calls=%async_computation.21 | async-start | bytes 2359296 | tf_op jit(solution)/shard_map/reduce_scatter | solution.py:604
  761.1 383.9 %reduce-scatter.21.cloned.1.call-start = ((), (), s32[]{:S(2)}) async-start(), calls=%async_computation.22 | async-start | bytes 12976128 | tf_op jit(solution)/shard_map/reduce_scatter | solution.py:604
  779.5 411.4 %reduce-scatter.15.cloned.1.call-start = ((), (), s32[]{:S(2)}) async-start(), calls=%async_computation.19 | async-start | bytes 5242880 | tf_op jit(solution)/shard_map/reduce_scatter | solution.py:593
  786.4 84.3 %copy-start.6 = (bf16[2048,4]{1,0:T(8,128)(2,1)S(1)}, bf16[2048,4]{1,0:T(8,128)(2,1)}, u32[]{:S(2)}) copy-start(bf16[2048,4]{1,0:T(8,128)(2,1)} %copy-done.5) | copy-start | bytes 49156
  869.4 6.7 collective-permute-start.1
  889.0 355.4 %reduce-scatter.11.cloned.1.call-start = ((), (), s32[]{:S(2)}) async-start(), calls=%async_computation.15 | async-start | bytes 5242880 | tf_op jit(solution)/shard_map/reduce_scatter | solution.py:558
  900.1 459.3 %reduce-scatter.17.cloned.1.call-start = ((), (), s32[]{:S(2)}) async-start(), calls=%async_computation.20 | async-start | bytes 7077888 | tf_op jit(solution)/shard_map/reduce_scatter | solution.py:604
  918.9 272.0 %copy-start.12 = (f32[1,2,8,128]{3,1,2,0:T(2,128)S(1)}, f32[1,2,8,128]{3,1,2,0:T(2,128)}, u32[]{:S(2)}) copy-start(f32[1,2,8,128]{3,1,2,0:T(2,128)} %copy-done.11) | copy-start | bytes 24580
  (17 other events, 70.5 us)
Sparse Core Ops, SparseCore 0:
  9.6 37.1 all-gather.9
  49.6 99.0 all-gather.11
  151.4 49.6 all-gather.13
  231.1 73.9 reduce-scatter.8
  307.9 163.6 all-gather.17
  473.7 32.6 all-gather.15
  508.0 34.4 all-gather.21
  545.5 92.6 all-gather.19
  671.9 42.6 reduce-scatter.12
  720.4 34.4 all-gather.23
  758.6 122.6 reduce-scatter.22
  884.6 65.0 reduce-scatter.18
  953.3 191.6 reduce-scatter.20
  1147.4 43.5 reduce-scatter.14
  1193.5 44.4 reduce-scatter.10
  1241.5 117.9 reduce-scatter.16

commit v2 on v1

--- a/solution.py
+++ b/solution.py
@@ -460,6 +460,503 @@
     )
 
 
+OUTER = 4
+SUBS = 2
+
+
+def ring_walk(place, n):
+    inner = n // OUTER
+    if inner == 1:
+        return place
+    late = jnp.maximum(place - OUTER, 0)
+    turn, along = lax.div(late, inner - 1), lax.rem(late, inner - 1)
+    odd = lax.rem(turn, 2)
+    back = (OUTER - 1 - turn) * inner + (1 - odd) * (along + 1) + odd * (inner - 1 - along)
+    return jnp.where(place < OUTER, place * inner, back)
+
+
+def ring_place(index, n):
+    inner = n // OUTER
+    if inner == 1:
+        return index
+    out, along = lax.div(index, inner), lax.rem(index, inner)
+    odd = lax.rem(OUTER - 1 - out, 2)
+    turn = (1 - odd) * (along - 1) + odd * (inner - 1 - along)
+    return jnp.where(along == 0, out, OUTER + (OUTER - 1 - out) * (inner - 1) + turn)
+
+
+def remote(source, target, send, recv, **device):
+    return pltpu.make_async_remote_copy(
+        src_ref=source, dst_ref=target, send_sem=send, recv_sem=recv,
+        device_id=device, device_id_type=MESH,
+    )
+
+
+def swap_pair(index):
+    return index + 1 - 2 * lax.rem(index, 2)
+
+
+def swap_half(index, count):
+    return lax.rem(index + count // 2, count)
+
+
+def opening_kernel(
+    n, tensor,
+    q_ref, k_ref, v_ref, small_ref, tokens_ref, cot_ref,
+    qkv_ref, small_out, ext_ref, cot_out,
+    zero_ref, local_sem, ring_send, ring_recv, side_send, side_recv, rim_send, rim_recv,
+):
+    me, t = lax.axis_index("dp"), lax.axis_index("tensor")
+    place = ring_place(me, n)
+    near = (ring_walk(lax.rem(place + 1, n), n), ring_walk(lax.rem(place + n - 1, n), n))
+    core, cross = swap_pair(t), swap_half(t, tensor)
+    rows, local = q_ref.shape
+    own_len = tokens_ref.shape[1]
+    slab = rows // (2 * SUBS)
+
+    barrier = pltpu.get_barrier_semaphore()
+    for device in ({"dp": near[0]}, {"dp": near[1]}, {"tensor": core}, {"tensor": cross}):
+        pl.semaphore_signal(barrier, inc=1, device_id=device, device_id_type=MESH)
+
+    @pl.when(me > 0)
+    def _():
+        pl.semaphore_signal(
+            barrier, inc=1, device_id={"dp": lax.rem(me + n - 1, n), "tensor": tensor - 1},
+            device_id_type=MESH,
+        )
+
+    def chunk(ref, at, offset):
+        return ref.at[:, pl.ds(pl.multiple_of(offset + at * own_len, 8), own_len), :]
+
+    mine = [
+        pltpu.make_async_copy(ref, qkv_ref.at[me, :, pl.ds(c * local, local)], local_sem.at[c])
+        for c, ref in enumerate((q_ref, k_ref, v_ref))
+    ] + [
+        pltpu.make_async_copy(small_ref, small_out.at[me], local_sem.at[3]),
+        pltpu.make_async_copy(tokens_ref, chunk(ext_ref, t, RIM), local_sem.at[4]),
+        pltpu.make_async_copy(cot_ref, chunk(cot_out, t, 0), local_sem.at[5]),
+    ]
+    for copy in mine:
+        copy.start()
+
+    @pl.when(me == 0)
+    def _():
+        zero_ref[...] = jnp.zeros_like(zero_ref)
+        blank = pltpu.make_async_copy(zero_ref, ext_ref.at[:, pl.ds(0, RIM), :], local_sem.at[6])
+        blank.start()
+        blank.wait()
+
+    sends_rim = (me < n - 1) & (t == tensor - 1)
+
+    @pl.when(sends_rim)
+    def _():
+        pl.semaphore_wait(barrier, 4 + tensor)
+
+    @pl.when(jnp.logical_not(sends_rim))
+    def _():
+        pl.semaphore_wait(barrier, 4)
+
+    def to_rim(peer):
+        return remote(
+            tokens_ref.at[:, pl.ds(own_len - RIM, RIM), :], ext_ref.at[:, pl.ds(0, RIM), :],
+            rim_send.at[peer], rim_recv, dp=lax.rem(me + 1, n), tensor=peer,
+        )
+
+    sides = []
+    for i, (own, full, offset) in enumerate(((tokens_ref, ext_ref, RIM), (cot_ref, cot_out, 0))):
+        to_core = remote(own, chunk(full, t, offset), side_send.at[i, 0], side_recv.at[i, 0], tensor=core)
+        to_cross = remote(own, chunk(full, t, offset), side_send.at[i, 1], side_recv.at[i, 1], tensor=cross)
+        onward = remote(
+            chunk(full, cross, offset), chunk(full, cross, offset),
+            side_send.at[i, 2], side_recv.at[i, 2], tensor=core,
+        )
+        sides.append((to_core, to_cross, onward))
+        to_core.start()
+        to_cross.start()
+
+    for copy in mine:
+        copy.wait()
+
+    @pl.when(sends_rim)
+    def _():
+        for peer in range(tensor):
+            to_rim(peer).start()
+
+    def ring(hop, lane):
+        if lane == 2 * SUBS:
+            owner = ring_walk(lax.rem(place + n - hop + 1, n), n)
+            return remote(
+                small_out.at[owner], small_out.at[owner],
+                ring_send.at[hop, lane], ring_recv.at[hop, lane], dp=near[0],
+            )
+        way = lane % 2
+        owner = ring_walk(lax.rem(place + n + (2 * way - 1) * (hop - 1), n), n)
+        piece = qkv_ref.at[owner, pl.ds(lane * slab, slab), :]
+        return remote(piece, piece, ring_send.at[hop, lane], ring_recv.at[hop, lane], dp=near[way])
+
+    lanes = range(2 * SUBS + 1)
+
+    def advance(hop, carry):
+        for lane in lanes:
+            @pl.when(hop > 1)
+            def _():
+                ring(hop - 1, lane).wait_recv()
+
+            ring(hop, lane).start()
+        for i, at in ((0, n // 2), (1, n - 1)):
+            @pl.when(hop == at)
+            def _():
+                sides[i][1].wait_recv()
+                sides[i][2].start()
+
+        return carry
+
+    lax.fori_loop(1, n, advance, 0)
+    for lane in lanes:
+        ring(n - 1, lane).wait_recv()
+
+    def drain(hop, carry):
+        for lane in lanes:
+            ring(hop, lane).wait_send()
+        return carry
+
+    lax.fori_loop(1, n, drain, 0)
+    for to_core, to_cross, onward in sides:
+        to_core.wait()
+        to_cross.wait_send()
+        onward.wait()
+
+    @pl.when(sends_rim)
+    def _():
+        for peer in range(tensor):
+            to_rim(peer).wait_send()
+
+    @pl.when(me > 0)
+    def _():
+        to_rim(0).wait_recv()
+
+
+def opening(query_weight, key_weight, value_weight, small, tokens, cotangent):
+    n, tensor = lax.axis_size("dp"), lax.axis_size("tensor")
+    rows, local = query_weight.shape
+    seqs, own_len, width = tokens.shape
+    vmem, anywhere = pl.BlockSpec(memory_space=pltpu.VMEM), pl.BlockSpec(memory_space=pl.ANY)
+    lanes = 2 * SUBS + 1
+    return pl.pallas_call(
+        functools.partial(opening_kernel, n, tensor),
+        in_specs=[vmem] * 6,
+        out_specs=[anywhere] * 4,
+        out_shape=[
+            jax.ShapeDtypeStruct((n, rows, 3 * local), bf16),
+            jax.ShapeDtypeStruct((n,) + small.shape, bf16),
+            jax.ShapeDtypeStruct((seqs, RIM + tensor * own_len, width), bf16),
+            jax.ShapeDtypeStruct((seqs, tensor * own_len, width), bf16),
+        ],
+        scratch_shapes=[
+            pltpu.VMEM((seqs, RIM, width), bf16),
+            pltpu.SemaphoreType.DMA((7,)),
+            pltpu.SemaphoreType.DMA((n, lanes)),
+            pltpu.SemaphoreType.DMA((n, lanes)),
+            pltpu.SemaphoreType.DMA((2, 3)),
+            pltpu.SemaphoreType.DMA((2, 3)),
+            pltpu.SemaphoreType.DMA((tensor,)),
+            pltpu.SemaphoreType.DMA,
+        ],
+        compiler_params=pltpu.CompilerParams(
+            collective_id=2, has_side_effects=True, vmem_limit_bytes=VMEM_LIMIT
+        ),
+        name="opening",
+    )(query_weight, key_weight, value_weight, small, tokens, cotangent)
+
+
+def fold_kernel(
+    n_seqs, tensor, backward,
+    part_ref, own_ref, gain_ref, hidden_ref,
+    rows_ref, keep_ref, sum_ref,
+    near_ref, far_ref, send_ref, own_sum_ref, a_send, a_recv, x_send, x_recv, g_send, g_recv,
+):
+    t = lax.axis_index("tensor")
+    core, cross = swap_pair(t), swap_half(t, tensor)
+    both = swap_half(core, tensor)
+    own_len = own_ref.shape[1]
+
+    barrier = pltpu.get_barrier_semaphore()
+    for device in (core, cross):
+        pl.semaphore_signal(barrier, inc=1, device_id={"tensor": device}, device_id_type=MESH)
+    pl.semaphore_wait(barrier, 2)
+
+    def span(at):
+        return pl.ds(pl.multiple_of(at * own_len, own_len), own_len)
+
+    def to_core(s, i):
+        return remote(
+            part_ref.at[s, span((core, both)[i]), :], near_ref.at[s, i],
+            a_send.at[s, i], a_recv.at[s, i], tensor=core,
+        )
+
+    def to_cross(s):
+        return remote(send_ref.at[s], far_ref.at[s], x_send.at[s], x_recv.at[s], tensor=cross)
+
+    def gather(s, i):
+        if i == 2:
+            piece, peer = rows_ref.at[s, span(cross), :], core
+        else:
+            piece, peer = rows_ref.at[s, span(t), :], (cross, core)[i]
+        return remote(piece, piece, g_send.at[s, i], g_recv.at[s, i], tensor=peer)
+
+    for s in range(n_seqs):
+        for i in (1, 0):
+            to_core(s, i).start()
+
+    def first(s, carry):
+        to_core(s, 1).wait_recv()
+        send_ref[s] = (
+            part_ref[s, span(cross), :].astype(f32) + near_ref[s, 1].astype(f32)
+        ).astype(bf16)
+        to_cross(s).start()
+        to_core(s, 0).wait_recv()
+        own_sum_ref[s] = part_ref[s, span(t), :].astype(f32) + near_ref[s, 0].astype(f32)
+        return carry
+
+    lax.fori_loop(0, n_seqs, first, 0)
+    sum_ref[...] = jnp.zeros_like(sum_ref)
+
+    def second(s, carry):
+        to_cross(s).wait_recv()
+        total = own_sum_ref[s] + far_ref[s].astype(f32)
+        gain = gain_ref[...]
+        own = own_ref[s].astype(f32)
+        if backward:
+            hidden = hidden_ref[s]
+            scale = lax.rsqrt(jnp.mean(hidden * hidden, axis=-1, keepdims=True) + epsilon)
+            unit = hidden * scale
+            sum_ref[...] += jnp.sum(total * unit, axis=0, keepdims=True)
+            scaled = total * gain
+            kept = own + scale * (scaled - unit * jnp.mean(scaled * unit, axis=-1, keepdims=True))
+            keep_ref[s] = kept
+            rows_ref[s, span(t), :] = kept.astype(bf16)
+        else:
+            kept = own + total
+            keep_ref[s] = kept
+            scale = lax.rsqrt(jnp.mean(kept * kept, axis=-1, keepdims=True) + epsilon)
+            rows_ref[s, span(t), :] = (kept * scale * gain).astype(bf16)
+        gather(s, 0).start()
+        gather(s, 1).start()
+        return carry
+
+    lax.fori_loop(0, n_seqs, second, 0)
+
+    def third(s, carry):
+        gather(s, 0).wait_recv()
+        gather(s, 2).start()
+        return carry
+
+    lax.fori_loop(0, n_seqs, third, 0)
+
+    def last(s, carry):
+        gather(s, 1).wait_recv()
+        gather(s, 2).wait_recv()
+        for i in range(2):
+            to_core(s, i).wait_send()
+        to_cross(s).wait_send()
+        for i in range(3):
+            gather(s, i).wait_send()
+        return carry
+
+    lax.fori_loop(0, n_seqs, last, 0)
+
+
+def fold(part, own, gain, hidden=None):
+    tensor = lax.axis_size("tensor")
+    seqs, own_len, width = own.shape
+    backward = hidden is not None
+    vmem = pl.BlockSpec(memory_space=pltpu.VMEM)
+    if hidden is None:
+        hidden = jnp.zeros((8, 128), f32)
+    return pl.pallas_call(
+        functools.partial(fold_kernel, seqs, tensor, backward),
+        in_specs=[vmem] * 4,
+        out_specs=[vmem] * 3,
+        out_shape=[
+            jax.ShapeDtypeStruct((seqs, tensor * own_len, width), bf16),
+            jax.ShapeDtypeStruct((seqs, own_len, width), f32),
+            jax.ShapeDtypeStruct((1, width), f32),
+        ],
+        scratch_shapes=[
+            pltpu.VMEM((seqs, 2, own_len, width), bf16),
+            pltpu.VMEM((seqs, own_len, width), bf16),
+            pltpu.VMEM((seqs, own_len, width), bf16),
+            pltpu.VMEM((seqs, own_len, width), f32),
+            pltpu.SemaphoreType.DMA((seqs, 2)),
+            pltpu.SemaphoreType.DMA((seqs, 2)),
+            pltpu.SemaphoreType.DMA((seqs,)),
+            pltpu.SemaphoreType.DMA((seqs,)),
+            pltpu.SemaphoreType.DMA((seqs, 3)),
+            pltpu.SemaphoreType.DMA((seqs, 3)),
+        ],
+        compiler_params=pltpu.CompilerParams(
+            collective_id=4 if backward else 3, has_side_effects=True, vmem_limit_bytes=VMEM_LIMIT
+        ),
+        name="fold_back" if backward else "fold",
+    )(part, own, gain, hidden)
+
+
+def closing_kernel(
+    n, n_seqs, tensor,
+    part_ref, own_ref, tokens_ref, gain_ref, grad_ref,
+    d_ref, sum_ref,
+    near_ref, far_ref, send_ref, own_sum_ref, in_ref, out_ref,
+    a_send, a_recv, x_send, x_recv, ring_send, ring_recv,
+):
+    me, t = lax.axis_index("dp"), lax.axis_index("tensor")
+    place = ring_place(me, n)
+    near = (ring_walk(lax.rem(place + 1, n), n), ring_walk(lax.rem(place + n - 1, n), n))
+    core, cross = swap_pair(t), swap_half(t, tensor)
+    both = swap_half(core, tensor)
+    own_len = tokens_ref.shape[1]
+    slab = grad_ref.shape[1] // (2 * SUBS)
+
+    barrier = pltpu.get_barrier_semaphore()
+    for device in ({"dp": near[0]}, {"dp": near[1]}, {"tensor": core}, {"tensor": cross}):
+        pl.semaphore_signal(barrier, inc=1, device_id=device, device_id_type=MESH)
+    pl.semaphore_wait(barrier, 4)
+
+    def span(at):
+        return pl.ds(pl.multiple_of(at * own_len, own_len), own_len)
+
+    def to_core(s, i):
+        return remote(
+            part_ref.at[s, span((core, both)[i]), :], near_ref.at[s, i],
+            a_send.at[s, i], a_recv.at[s, i], tensor=core,
+        )
+
+    def to_cross(s):
+        return remote(send_ref.at[s], far_ref.at[s], x_send.at[s], x_recv.at[s], tensor=cross)
+
+    def owner(hop, way):
+        return ring_walk(lax.rem(place + n + (2 * way - 1) * hop, n), n)
+
+    def strip(lane):
+        return pl.ds(lane * slab, slab)
+
+    def opened(lane):
+        way = lane % 2
+        return remote(
+            grad_ref.at[owner(1, way), strip(lane), :], in_ref.at[1, strip(lane), :],
+            ring_send.at[1, lane], ring_recv.at[1, lane], dp=near[way],
+        )
+
+    def ring(hop, lane):
+        return remote(
+            out_ref.at[hop, strip(lane), :], in_ref.at[hop, strip(lane), :],
+            ring_send.at[hop, lane], ring_recv.at[hop, lane], dp=near[lane % 2],
+        )
+
+    lanes = range(2 * SUBS)
+    for lane in lanes:
+        opened(lane).start()
+    for s in range(n_seqs):
+        for i in (1, 0):
+            to_core(s, i).start()
+
+    def first(s, carry):
+        to_core(s, 1).wait_recv()
+        send_ref[s] = (
+            part_ref[s, span(cross), :].astype(f32) + near_ref[s, 1].astype(f32)
+        ).astype(bf16)
+        to_cross(s).start()
+        to_core(s, 0).wait_recv()
+        own_sum_ref[s] = part_ref[s, span(t), :].astype(f32) + near_ref[s, 0].astype(f32)
+        return carry
+
+    lax.fori_loop(0, n_seqs, first, 0)
+
+    def finish(s):
+        to_cross(s).wait_recv()
+        total = own_sum_ref[s] + far_ref[s].astype(f32)
+        tokens = tokens_ref[s].astype(f32)
+        scale = lax.rsqrt(jnp.mean(tokens * tokens, axis=-1, keepdims=True) + epsilon)
+        unit = tokens * scale
+        scaled = total * gain_ref[...]
+        d_ref[s] = (
+            own_ref[s] + scale * (scaled - unit * jnp.mean(scaled * unit, axis=-1, keepdims=True))
+        ).astype(bf16)
+
+    def advance(hop, carry):
+        for lane in lanes:
+            ring(hop - 1, lane).wait_recv()
+            out_ref[hop, strip(lane), :] = (
+                in_ref[hop - 1, strip(lane), :].astype(f32)
+                + grad_ref[owner(hop, lane % 2), strip(lane), :].astype(f32)
+            ).astype(bf16)
+            ring(hop, lane).start()
+
+        @pl.when(hop == n // 2)
+        def _():
+            for s in range(n_seqs):
+                finish(s)
+
+        return carry
+
+    lax.fori_loop(2, n, advance, 0)
+    for lane in lanes:
+        ring(n - 1, lane).wait_recv()
+        sum_ref[strip(lane), :] = in_ref[n - 1, strip(lane), :].astype(f32) + grad_ref[
+            me, strip(lane), :
+        ].astype(f32)
+        opened(lane).wait_send()
+
+    def drain(hop, carry):
+        for lane in lanes:
+            ring(hop, lane).wait_send()
+        return carry
+
+    lax.fori_loop(2, n, drain, 0)
+
+    def last(s, carry):
+        for i in range(2):
+            to_core(s, i).wait_send()
+        to_cross(s).wait_send()
+        return carry
+
+    lax.fori_loop(0, n_seqs, last, 0)
+
+
+def closing(part, own, tokens, gain, grads):
+    n, tensor = lax.axis_size("dp"), lax.axis_size("tensor")
+    seqs, own_len, width = tokens.shape
+    _, rows, columns = grads.shape
+    vmem = pl.BlockSpec(memory_space=pltpu.VMEM)
+    lanes = 2 * SUBS
+    return pl.pallas_call(
+        functools.partial(closing_kernel, n, seqs, tensor),
+        in_specs=[vmem] * 5,
+        out_specs=[vmem] * 2,
+        out_shape=[
+            jax.ShapeDtypeStruct((seqs, own_len, width), bf16),
+            jax.ShapeDtypeStruct((rows, columns), f32),
+        ],
+        scratch_shapes=[
+            pltpu.VMEM((seqs, 2, own_len, width), bf16),
+            pltpu.VMEM((seqs, own_len, width), bf16),
+            pltpu.VMEM((seqs, own_len, width), bf16),
+            pltpu.VMEM((seqs, own_len, width), f32),
+            pltpu.VMEM((n, rows, columns), bf16),
+            pltpu.VMEM((n, rows, columns), bf16),
+            pltpu.SemaphoreType.DMA((seqs, 2)),
+            pltpu.SemaphoreType.DMA((seqs, 2)),
+            pltpu.SemaphoreType.DMA((seqs,)),
+            pltpu.SemaphoreType.DMA((seqs,)),
+            pltpu.SemaphoreType.DMA((n, lanes)),
+            pltpu.SemaphoreType.DMA((n, lanes)),
+        ],
+        compiler_params=pltpu.CompilerParams(
+            collective_id=5, has_side_effects=True, vmem_limit_bytes=VMEM_LIMIT
+        ),
+        name="closing",
+    )(part, own, tokens, gain, grads)
+
+
 def from_behind(block, axis, distance):
     devices = range(lax.axis_size(axis))
     route = [(i - distance, i) for i in devices if i - distance in devices]
@@ -478,6 +975,41 @@
 
 def matmul(spec, left, right):
     return jnp.einsum(spec, left, right, preferred_element_type=f32)
+
+
+def swap(block, axis, half):
+    count = lax.axis_size(axis)
+    route = [(i, (i + count // 2) % count if half else i ^ 1) for i in range(count)]
+    return lax.ppermute(block, axis, route)
+
+
+def tensor_scatter(part):
+    tensor, t = lax.axis_size("tensor"), lax.axis_index("tensor")
+    seqs, rows, width = part.shape
+    chunks = part.reshape(seqs, tensor, rows // tensor, width)
+
+    def chunk(at):
+        return lax.dynamic_index_in_dim(chunks, at, 1, keepdims=False)
+
+    core, cross = swap_pair(t), swap_half(t, tensor)
+    both = swap_half(core, tensor)
+    near_own, near_cross = swap(chunk(core), "tensor", False), swap(chunk(both), "tensor", False)
+    far = swap((chunk(cross).astype(f32) + near_cross.astype(f32)).astype(bf16), "tensor", True)
+    return chunk(t).astype(f32) + near_own.astype(f32) + far.astype(f32)
+
+
+def tensor_sum(value):
+    value = value + swap(value, "tensor", False)
+    return value + swap(value, "tensor", True)
+
+
+def direct_scatter(grads):
+    n, me = lax.axis_size("dp"), lax.axis_index("dp")
+    total = lax.dynamic_index_in_dim(grads, me, 0, keepdims=False).astype(f32)
+    for step in range(1, n):
+        block = lax.dynamic_index_in_dim(grads, lax.rem(me + step, n), 0, keepdims=False)
+        total = total + lax.ppermute(block, "dp", [(i, (i + step) % n) for i in range(n)]).astype(f32)
+    return total
 
 
 def shards(
@@ -502,19 +1034,19 @@
     heads = local // HD
     hidden = gate_weight.shape[1]
 
-    full_small = lax.all_gather(
-        jnp.concatenate(
-            [conv_filter.reshape(-1), norm_gain.reshape(-1), head_gain, beta_weight.reshape(-1)]
-        ),
-        "dp",
-    )
-    full_qkv = lax.all_gather(
-        jnp.concatenate([query_weight, key_weight, value_weight], axis=1), "dp", axis=0, tiled=True
-    )
+    packed = jnp.concatenate(
+        [conv_filter.reshape(-1), norm_gain.reshape(-1), head_gain, beta_weight.reshape(-1)]
+    )
+    block = -(-packed.size // 2048) * 2048
+    small = jnp.pad(packed, (0, block - packed.size)).reshape(-1, 128)
+    full_qkv, full_small, extended, rows_cotangent = opening(
+        query_weight, key_weight, value_weight, small, tokens, cotangent
+    )
+    full_qkv = full_qkv.reshape(width, 3 * local)
+    full_small = full_small.reshape(n, block)
     full_out = lax.all_gather(out_weight.T, "dp", axis=0, tiled=True)
-    full_gate_up = lax.all_gather(
-        jnp.concatenate([gate_weight, up_weight], axis=1), "dp", axis=0, tiled=True
-    )
+    full_gate = lax.all_gather(gate_weight, "dp", axis=0, tiled=True)
+    full_up = lax.all_gather(up_weight, "dp", axis=0, tiled=True)
     full_down = lax.all_gather(down_weight.T, "dp", axis=0, tiled=True)
     sizes = [conv_filter.size, norm_gain.size, head_gain.size, beta_weight.size]
     ends = [sum(sizes[: i + 1]) for i in range(4)]
@@ -529,52 +1061,36 @@
         full_small[:, ends[0] : ends[1]].reshape(n, 2, width // n).transpose(1, 0, 2).reshape(2, width)
     ).astype(f32)
     head_row = full_small[:, ends[1] : ends[2]].reshape(1, HD).astype(f32)
-    full_beta = full_small[:, ends[2] :].reshape(width, heads)
-
-    rows_tokens = lax.all_gather(tokens, "tensor", axis=1, tiled=True)
-    rows_cotangent = lax.all_gather(cotangent, "tensor", axis=1, tiled=True)
-    rim_tokens = from_behind(rows_tokens[:, -RIM:], "dp", 1)
-    extended = jnp.concatenate([rim_tokens, rows_tokens], axis=1).astype(f32)
-    unit_ext, _ = rms_unit(extended)
+    full_beta = full_small[:, ends[2] : ends[3]].reshape(width, heads)
+
+    unit_ext, _ = rms_unit(extended.astype(f32))
     normed_ext = (unit_ext * gains[0]).astype(bf16)
     normed_first = normed_ext[:, RIM:]
     projected = matmul("std,dm->stm", normed_ext, full_qkv).astype(bf16)
     strength = jax.nn.sigmoid(matmul("std,dh->sth", normed_first, full_beta))
     normed_mix, mix, carry, inverse, kw, state = mixer(projected, strength, filters, head_row)
 
-    branch_part = matmul("stk,dk->std", normed_mix, full_out)
-    branch = lax.psum_scatter(branch_part.astype(bf16), "tensor", scatter_dimension=1, tiled=True)
-    own_tokens = tokens.astype(f32)
-    hidden_state = own_tokens + branch.astype(f32)
-    unit_second, scale_second = rms_unit(hidden_state)
-    normed_second = lax.all_gather(
-        (unit_second * gains[1]).astype(bf16), "tensor", axis=1, tiled=True
-    )
-    gate_up = matmul("std,df->stf", normed_second, full_gate_up)
-    gate_pre, up_pre = gate_up[..., :hidden], gate_up[..., hidden:]
+    branch_part = matmul("stk,dk->std", normed_mix, full_out).astype(bf16)
+    normed_second, hidden_state, _ = fold(branch_part, tokens, gains[1:2])
+    gate_pre = matmul("std,df->stf", normed_second, full_gate)
+    up_pre = matmul("std,df->stf", normed_second, full_up)
     gate_sigmoid = jax.nn.sigmoid(gate_pre)
     ffn_hidden = (gate_pre * gate_sigmoid * up_pre).astype(bf16)
-    ffn_part = matmul("stf,df->std", ffn_hidden, full_down)
-    ffn_branch = lax.psum_scatter(
-        ffn_part.astype(bf16), "tensor", scatter_dimension=1, tiled=True
-    ).astype(f32)
-    layer_out = (hidden_state + ffn_branch).astype(bf16)
 
     back_hidden = matmul("std,df->stf", rows_cotangent, full_down)
     back_gate = (
         back_hidden * up_pre * gate_sigmoid * (1.0 + gate_pre * (1.0 - gate_sigmoid))
     ).astype(bf16)
     back_up = (back_hidden * gate_pre * gate_sigmoid).astype(bf16)
-    back_gate_up = jnp.concatenate([back_gate, back_up], axis=2)
-    back_second = matmul("stf,df->std", back_gate_up, full_gate_up)
-    back_second_rows = lax.psum_scatter(
-        back_second.astype(bf16), "tensor", scatter_dimension=1, tiled=True
-    ).astype(f32)
+    back_second = matmul("stf,df->std", back_gate, full_gate) + matmul("stf,df->std", back_up, full_up)
+    rows_back, back_state, gain_second = fold(
+        back_second.astype(bf16), cotangent, gains[1:2], hidden_state
+    )
     grad_down = matmul("std,stf->df", rows_cotangent, ffn_hidden)
-    grad_gate_up = matmul("std,stf->df", normed_second, back_gate_up)
-    gain_second = jnp.sum(back_second_rows * unit_second, axis=(0, 1))
-    back_state = cotangent.astype(f32) + rms_back(back_second_rows, unit_second, scale_second, gains[1])
-    rows_back = lax.all_gather(back_state.astype(bf16), "tensor", axis=1, tiled=True)
+    grad_gate = matmul("std,stf->df", normed_second, back_gate)
+    grad_up = matmul("std,stf->df", normed_second, back_up)
+    ffn_part = matmul("stf,df->std", ffn_hidden, full_down).astype(bf16)
+    layer_out = (hidden_state + tensor_scatter(ffn_part)).astype(bf16)
     grad_out = matmul("std,stk->dk", rows_back, normed_mix)
     back_normed = matmul("std,dk->stk", rows_back, full_out)
     back_proj, last, rim, back_logit, conv_part, head_part = mixer_back(
@@ -590,46 +1106,45 @@
     back_first = matmul("stm,dm->std", back_proj, full_qkv) + matmul(
         "sth,dh->std", back_logit, full_beta
     )
-    back_first_rows = lax.psum_scatter(
-        back_first.astype(bf16), "tensor", scatter_dimension=1, tiled=True
-    ).astype(f32)
-    unit_first, scale_first = rms_unit(own_tokens)
-    gain_first = jnp.sum(back_first_rows * unit_first, axis=(0, 1))
-    d_tokens = (back_state + rms_back(back_first_rows, unit_first, scale_first, gains[0])).astype(bf16)
+    gain_first = jnp.sum(back_first * unit_ext[:, RIM:], axis=(0, 1))
+    grads = jnp.concatenate([grad_qkv.astype(bf16), grad_out.astype(bf16)], axis=1)
+    d_tokens, grad_main = closing(
+        back_first.astype(bf16), back_state, tokens, gains[0:1], grads.reshape(n, width // n, -1)
+    )
 
     grad_conv = conv_part.transpose(1, 0, 2).reshape(3 * KCONV, local)
-    shared = lax.psum(jnp.concatenate([gain_first, gain_second, head_part[0]]), "tensor")
+    gain_grads = jnp.stack([gain_first, gain_second[0]])
+    small_grads = jnp.concatenate(
+        [
+            grad_conv.reshape(3 * KCONV, heads, n, HD // n).transpose(2, 0, 1, 3).reshape(n, -1),
+            gain_grads.reshape(2, n, width // n).transpose(1, 0, 2).reshape(n, -1),
+            head_part[0].reshape(n, HD // n),
+            grad_beta.reshape(n, -1),
+        ],
+        axis=1,
+    )
+    small_grads = direct_scatter(small_grads.astype(bf16))
+    shared = tensor_sum(small_grads[ends[0] : ends[2]])
 
     def scatter(grad):
         return lax.psum_scatter(grad.astype(bf16), "dp", scatter_dimension=0, tiled=True).astype(f32)
 
-    small = jnp.concatenate(
-        [
-            grad_conv.reshape(3 * KCONV, heads, n, HD // n).transpose(2, 0, 1, 3).reshape(n, -1),
-            shared[: 2 * width].reshape(2, n, width // n).transpose(1, 0, 2).reshape(n, -1),
-            shared[2 * width :].reshape(n, HD // n),
-            grad_beta.reshape(n, -1),
-        ],
-        axis=1,
-    )
-    small = scatter(small)[0]
     grad_down = scatter(grad_down).T
-    grad_gate_up = scatter(grad_gate_up)
-    grad_out = scatter(grad_out).T
-    grad_qkv = scatter(grad_qkv)
+    grad_gate = scatter(grad_gate)
+    grad_up = scatter(grad_up)
     return (
         layer_out,
         d_tokens,
-        grad_qkv[:, :local],
-        grad_qkv[:, local : 2 * local],
-        grad_qkv[:, 2 * local :],
-        small[ends[2] :].reshape(beta_weight.shape),
-        small[: ends[0]].reshape(conv_filter.shape),
-        small[ends[0] : ends[1]].reshape(norm_gain.shape),
-        small[ends[1] : ends[2]],
-        grad_out,
-        grad_gate_up[:, :hidden],
-        grad_gate_up[:, hidden:],
+        grad_main[:, :local],
+        grad_main[:, local : 2 * local],
+        grad_main[:, 2 * local : 3 * local],
+        small_grads[ends[2] :].reshape(beta_weight.shape),
+        small_grads[: ends[0]].reshape(conv_filter.shape),
+        shared[: ends[1] - ends[0]].reshape(norm_gain.shape),
+        shared[ends[1] - ends[0] :],
+        grad_main[:, 3 * local :].T,
+        grad_gate,
+        grad_up,
         grad_down,
     )
 

time: 1380 us -> 852 us (0.62)
  waiting for transfers between devices: 895 us -> 82.6 us
  Pallas kernels: 147 us -> 504 us
  blocking collectives: 87.1 us -> 0 us
    pallas_call x0 -> x4, Pallas kernels: none -> 349 us  [the longest x1 124 us: closing(): pl.pallas_call(functools.partial(closing_kernel, n, seqs, tensor), in_spe...]
    reduce_scatter x4 -> x3, waiting for transfers between devices: 330 us -> 0.01 us  [scatter(): lax.psum_scatter(grad.astype(bf16), 'dp', scatter_dimension=0, tiled=True)]
    all_gather x6 -> x2, waiting for transfers between devices: 316 us -> 81.2 us  [the longest x1 81.2 us: shards(): full_gate = lax.all_gather(gate_weight, 'dp', axis=0, tiled=True)]
    reduce_scatter x4 -> x0, waiting for transfers between devices: 147 us -> none  [the longest x1 71.5 us: shards(): lax.psum_scatter(branch_part.astype(bf16), 'tensor', scatter_dimension=1,...]
    all_gather x1, waiting for transfers between devices: 95.7 us -> 0.02 us  [shards(): full_down = lax.all_gather(down_weight.T, 'dp', axis=0, tiled=True)]
    unnamed x2 -> x0, blocking collectives: 76.8 us -> none
    dot_general x15 -> x18, matrix products: 151 us -> 157 us  [matmul(): return jnp.einsum(spec, left, right, preferred_element_type=f32)]
  transfers between devices with their start and end apart: 18 -> 20, of which waited for: 14 -> 1; matrix products, arithmetic and copies ran while one was open for 11% -> 23% of each run, Pallas kernels for 11% -> 60%
where the time goes in v2:
time: 852 us; the launch traced here: 842 us
  Pallas kernels  504 us (59%)
  matrix products  157 us (18%)
  waiting for transfers between devices  82.6 us (10%)
  local copies, waits for them, and re-layouts  40.2 us (5%)
  other arithmetic  29.8 us (3%)
  between operations  14.9 us (2%)
  starting transfers between devices  13.5 us (2%)
    dot_general x18, matrix products, matmul(): return jnp.einsum(spec, left, right, preferred_element_type=f32)  157 us
    pallas_call x1, Pallas kernels, closing(): pl.pallas_call(functools.partial(closing_kernel, n, seqs, tensor), in_spe...  124 us
    pallas_call x2, Pallas kernels, fold(): pl.pallas_call(functools.partial(fold_kernel, seqs, tensor, backward), in...  116 us
    pallas_call x1, Pallas kernels, opening(): pl.pallas_call(functools.partial(opening_kernel, n, tensor), in_specs=[vm...  109 us
    pallas_call x1, Pallas kernels, mixer_back(): pl.pallas_call(functools.partial(mixer_back_kernel, n, rows), grid=(seqs,...  84.8 us
    all_gather x1, waiting for transfers between devices, shards(): full_gate = lax.all_gather(gate_weight, 'dp', axis=0, tiled=True)  81.2 us
    pallas_call x1, Pallas kernels, mixer(): pl.pallas_call(functools.partial(mixer_kernel, n, rows), grid=(seqs, pair...  69.9 us
  transfers between devices with their start and end apart: 20, of which 1 were waited for; matrix products, arithmetic and copies ran while one was open for 23% of the time, Pallas kernels for 60%

profile of v2, /device:TPU:0, one launch (start us, length us, event | category | flops | bytes accessed | tf_op | source)
XLA Modules:
  0.0 842.2 jit_solution(1057746427616845312)
XLA Ops:
  13.9 109.4 %opening.1 = (bf16[8,256,1536]{2,1,0:T(8,128)(2,1)}, bf16[8,32,128]{2,1,0:T(8,128)(2,1)}, bf16[4,264,2048]{2,1,0:T(8,128)(2,1)}, bf16[4,256,2048]{2,1,0:T(8,128)(2,1)}) custom-call(bf16[256,512]{1,0:T(8,128)(2,1)} %q_ref.1, bf16[256,512]{1,0:T(8,128)(2,1)} %k_ref.1, bf16[256,512]{1,0:T(8,128)(2,1)} %v_ref.1, bf16[32,128]{1,0:T(8,128)(2,1)} %pad_bitcast_fusion.small_ref, ...), custom_call_target="tpu_custom_call" | custom-call | tf_op jit(solution)/shard_map/opening/pallas_call | solution.py:645
  137.8 8.5 %convolution_convert_fusion.pq_ref.pk_ref.pv_ref = bf16[4,264,1536]{2,1,0:T(8,128)(2,1)} fusion(bf16[4,264,2048]{2,1,0:T(8,128)(2,1)S(1)} %get-tuple-element.111, bf16[2048,1536,1]{1,0,2:T(8,128)(2,1)S(1)} %bitcast.148), kind=kOutput, calls=%fused_computation.29 | convolution fusion | flops 6645399552 | bytes 13860864 | tf_op jit(solution)/shard_map/std,dm->stm/dot_general | solution.py:977
  146.3 69.9 %mixer.1 = (bf16[4,256,512]{2,1,0:T(8,128)(2,1)}, f32[4,256,512]{2,1,0:T(8,128)}, f32[4,256,512]{2,1,0:T(8,128)}, f32[16,256,256]{2,1,0:T(8,128)}, f32[16,128,12...) custom-call(bf16[4,264,1536]{2,1,0:T(8,128)(2,1)} %convolution_convert_fusion.pq_ref.pk_ref.pv_ref, ...), custom_call_target="tpu_custom_call" | custom-call | tf_op jit(solution)/shard_map/mixer/pallas_call | solution.py:204
  216.2 6.2 convolution_convert_fusion.1.part_ref
  223.0 59.0 %fold.1 = (bf16[4,256,2048]{2,1,0:T(8,128)(2,1)}, f32[4,64,2048]{2,1,0:T(8,128)}, f32[1,2048]{1,0:T(1,128)}) custom-call(bf16[4,256,2048]{2,1,0:T(8,128)(2,1)} %convolution_convert_fusion.1.part_ref, bf16[4,64,2048]{2,1,0:T(8,128)(2,1)} %tokens_ref.3, f32[1,2048]{1,0:T(1,128)} %bitcast.136, f32[8,128]{1,0:T(8,128)} %broadcast_in_dim.4.hidden_ref), custom_call_target="tpu_custom_call" | custom-call | tf_op jit(solution)/shard_map/fold/pallas_call | solution.py:776
  282.1 11.7 %fusion.2 = f32[4,256,1408]{2,1,0:T(8,128)} fusion(bf16[4,256,2048]{2,1,0:T(8,128)(2,1)} %get-tuple-element.42, bf16[2048,1408]{1,0:T(8,128)(2,1)} %all-gather.11.cloned.1.call-done), kind=kOutput, calls=%fused_computation.12 | convolution fusion | flops 5905580032 | bytes 15728640 | tf_op jit(solution)/shard_map/std,df->stf/dot_general | solution.py:977
  293.8 11.7 %fusion.8 = f32[4,256,1408]{2,1,0:T(8,128)} fusion(bf16[4,256,2048]{2,1,0:T(8,128)(2,1)} %get-tuple-element.41, bf16[2048,1408]{1,0:T(8,128)(2,1)} %all-gather.9.cloned.1.call-done), kind=kOutput, calls=%fused_computation.18 | convolution fusion | flops 5905580032 | bytes 15728640 | tf_op jit(solution)/shard_map/std,df->stf/dot_general | solution.py:977
  305.4 81.2 %all-gather.7.cloned.1.call-done = bf16[2048,1408]{1,0:T(8,128)(2,1)} async-done(((bf16[256,1408]{1,0:T(8,128)(2,1)}), bf16[2048,1408]{1,0:T(8,128)(2,1)}) %all-gather.7.cloned.1.call-update) | async-done | bytes 5767184 | tf_op jit(solution)/shard_map/all_gather | solution.py:1048
  386.6 15.8 %multiply_convert_fusion.2 = (bf16[4,256,1408]{2,1,0:T(8,128)(2,1)}, bf16[4,256,1408]{2,1,0:T(8,128)(2,1)S(1)}, bf16[4,256,1408]{2,1,0:T(8,128)(2,1)}) fusion(f32[4,256,1408]{2,1,0:T(8,128)} %fusion.2, f32[4,256,1408]{2,1,0:T(8,128)} %fusion.8, bf16[4,256,2048]{2,1,0:T(8,128)(2,1)} %get-tuple-element.41, bf16[2048,1408]{1,0:T(8,128)(2,1)} %all-gather.7.cloned.1.call-done), kind=kOutput, calls=%fused_computation.25 | convolution fusion | flops 5928648704 | bytes 30146560 | tf_op jit(solution)/shard_map/std,df->stf/dot_general | solution.py:977
  404.0 8.7 %bitcast_convert_fusion.1 = bf16[2048,1408]{1,0:T(8,128)(2,1)} fusion(bf16[4,256,2048]{2,1,0:T(8,128)(2,1)S(1)} %copy-done.11, bf16[4,256,1408]{2,1,0:T(8,128)(2,1)S(1)} %get-tuple-element.106), kind=kOutput, calls=%fused_computation.1 | convolution fusion | flops 5908463616 | bytes 12845056 | tf_op jit(solution)/shard_map/std,stf->df/dot_general | solution.py:977
  412.7 11.1 %bitcast_convert_fusion.3 = bf16[2048,1408]{1,0:T(8,128)(2,1)} fusion(bf16[4,256,2048]{2,1,0:T(8,128)(2,1)} %get-tuple-element.41, bf16[4,256,1408]{2,1,0:T(8,128)(2,1)} %get-tuple-element.105), kind=kOutput, calls=%fused_computation.3 | convolution fusion | flops 5908463616 | bytes 12845056 | tf_op jit(solution)/shard_map/std,stf->df/dot_general | solution.py:977
  424.6 11.0 %bitcast_convert_fusion.2 = bf16[2048,1408]{1,0:T(8,128)(2,1)} fusion(bf16[4,256,2048]{2,1,0:T(8,128)(2,1)} %get-tuple-element.41, bf16[4,256,1408]{2,1,0:T(8,128)(2,1)} %get-tuple-element.107), kind=kOutput, calls=%fused_computation.2 | convolution fusion | flops 5908463616 | bytes 12845056 | tf_op jit(solution)/shard_map/std,stf->df/dot_general | solution.py:977
  437.5 8.9 %fusion.6 = f32[4,256,2048]{2,1,0:T(8,128)S(1)} fusion(bf16[4,256,1408]{2,1,0:T(8,128)(2,1)S(1)} %copy-done.17, bf16[2048,1408]{1,0:T(8,128)(2,1)} %all-gather.9.cloned.1.call-done), kind=kOutput, calls=%fused_computation.16 | convolution fusion | flops 5905580032 | bytes 17039360 | tf_op jit(solution)/shard_map/stf,df->std/dot_general | solution.py:977
  446.4 11.0 %add_convert_fusion.part_ref = bf16[4,256,2048]{2,1,0:T(8,128)(2,1)} fusion(f32[4,256,2048]{2,1,0:T(8,128)S(1)} %fusion.6, bf16[4,256,1408]{2,1,0:T(8,128)(2,1)S(1)} %copy-done.16, bf16[2048,1408]{1,0:T(8,128)(2,1)} %all-gather.7.cloned.1.call-done), kind=kOutput, calls=%fused_computation.11 | convolution fusion | flops 5909774336 | bytes 21233664 | tf_op jit(solution)/shard_map/stf,df->std/dot_general | solution.py:977
  457.4 57.1 %fold_back.1 = (bf16[4,256,2048]{2,1,0:T(8,128)(2,1)}, f32[4,64,2048]{2,1,0:T(8,128)}, f32[1,2048]{1,0:T(1,128)}) custom-call(bf16[4,256,2048]{2,1,0:T(8,128)(2,1)} %add_convert_fusion.part_ref, bf16[4,64,2048]{2,1,0:T(8,128)(2,1)} %own_ref.3, f32[1,2048]{1,0:T(1,128)} %bitcast.137, f32[4,64,2048]{2,1,0:T(8,128)} %get-tuple-element.40.hidden_ref), custom_call_target="tpu_custom_call" | custom-call | tf_op jit(solution)/shard_map/fold_back/pallas_call | solution.py:776
  514.5 5.9 fusion.34.back_ref
  520.3 84.8 %mixer_back.1 = (bf16[4,256,1536]{2,1,0:T(8,128)(2,1)}, f32[4,8,1536]{2,1,0:T(8,128)}, bf16[4,8,1536]{2,1,0:T(8,128)(2,1)}, f32[4,256,4]{2,1,0:T(8,128)}, f32[2,12,256]{2,1,0:T(8,128)}, /*index=5*/f32[8,128]{1,0:T(8,128)}) custom-call(bf16[4,264,1536]{2,1,0:T(8,128)(2,1)} %convolution_convert_fusion.pq_ref.pk_ref.pv_ref, ...), custom_call_target="tpu_custom_call" | custom-call | tf_op jit(solution)/shard_map/mixer_back/pallas_call | solution.py:419
  611.4 5.5 fusion.49
  619.7 8.7 %fusion.14 = bf16[4,256,2048]{2,1,0:T(8,128)(2,1)} fusion(bf16[4,256,1408]{2,1,0:T(8,128)(2,1)S(1)} %copy-done.19, bf16[2048,1408]{1,0:T(8,128)(2,1)S(1)} %bitcast.150), kind=kOutput, calls=%fused_computation.31 | convolution fusion | flops 5907677184 | bytes 12845056 | tf_op jit(solution)/shard_map/stf,df->std/dot_general | solution.py:977
  630.3 13.7 %fusion.1 = (bf16[2048]{0:T(1024)(128)(2,1)S(1)}, bf16[4,256,2048]{2,1,0:T(8,128)(2,1)}) fusion(f32[4,264,2048]{2,1,0:T(8,128)} %get-tuple-element.110, f32[4,256,2048]{2,1,0:T(8,128)} %fusion.49, bf16[4,256,1536]{2,1,0:T(8,128)(2,1)} %fusion.54, bf16[2048,1536,1]{1,0,2:T(8,128)(2,1)} %bitcast.145), kind=kOutput, calls=%fused_computation.9 | convolution fusion | flops 6450837504 | bytes 30412800 | tf_op jit(solution)/shard_map/stm,dm->std/dot_general | solution.py:977
  656.4 11.6 %bitcast_convert_fusion = bf16[2048,1536]{0,1:T(8,128)(2,1)} fusion(bf16[4,256,1536]{2,1,0:T(8,128)(2,1)S(1)} %copy-done.13, bf16[4,264,2048]{2,1,0:T(8,128)(2,1)} %copy-done.2), kind=kOutput, calls=%fused_computation | convolution fusion | flops 6445596672 | bytes 13631488 | tf_op jit(solution)/shard_map/std,stm->dm/dot_general | solution.py:977
  672.3 7.7 pad_maximum_fusion
  680.0 12.3 %copy.77 = bf16[2048,2048]{1,0:T(8,128)(2,1)} copy(bf16[2048,2048]{0,1:T(8,128)(2,1)} %pad_maximum_fusion) | data formatting | bytes 16777216 | tf_op jit(solution)/shard_map/concatenate | solution.py:1110
  692.3 123.7 %closing.1 = (bf16[4,64,2048]{2,1,0:T(8,128)(2,1)}, f32[256,2048]{1,0:T(8,128)}) custom-call(bf16[4,256,2048]{2,1,0:T(8,128)(2,1)} %get-tuple-element.109.part_ref, f32[4,64,2048]{2,1,0:T(8,128)} %get-tuple-element.53.own_ref, bf16[4,64,2048]{2,1,0:T(8,128)(2,1)} %tokens_ref.3, f32[1,2048]{1,0:T(1,128)} %bitcast.139, bf16[8,256,2048]{2,1,0:T(8,128)(2,1)} %bitcast.124), custom_call_target="tpu_custom_call" | custom-call | tf_op jit(solution)/shard_map/closing/pallas_call | solution.py:931
  (166 shorter events, 72.5 us)
Async XLA Ops:
  7.2 209.0 %all-gather.5.cloned.1.call-start = ((), (), s32[]{:S(2)}) async-start(), calls=%async_computation.3 | async-start | bytes 2359296 | tf_op jit(solution)/shard_map/all_gather | solution.py:1047
  9.1 273.0 %all-gather.11.cloned.1.call-start = ((), (), s32[]{:S(2)}) async-start(), calls=%async_computation.6 | async-start | bytes 6488064 | tf_op jit(solution)/shard_map/all_gather | solution.py:1050
  11.4 282.4 %all-gather.9.cloned.1.call-start = ((), (), s32[]{:S(2)}) async-start(), calls=%async_computation.5 | async-start | bytes 6488064 | tf_op jit(solution)/shard_map/all_gather | solution.py:1049
  12.1 374.5 %all-gather.7.cloned.1.call-start = ((), (), s32[]{:S(2)}) async-start(), calls=%async_computation.4 | async-start | bytes 6488064 | tf_op jit(solution)/shard_map/all_gather | solution.py:1048
  12.7 814.0 %reduce-scatter.8.cloned.1.call-start = ((), (), s32[]{:S(2)}) async-start(), calls=%async_computation.9 | async-start | bytes 6488064 | tf_op jit(solution)/shard_map/reduce_scatter | solution.py:1130
  386.6 17.4 %copy-start.11 = (bf16[4,256,2048]{2,1,0:T(8,128)(2,1)S(1)}, bf16[4,256,2048]{2,1,0:T(8,128)(2,1)}, u32[]{:S(2)}) copy-start(bf16[4,256,2048]{2,1,0:T(8,128)(2,1)} %get-tuple-element.42) | copy-start | bytes 12582916
  412.7 416.9 %reduce-scatter.4.cloned.1.call-start = ((), (), s32[]{:S(2)}) async-start(), calls=%async_computation.7 | async-start | bytes 6488064 | tf_op jit(solution)/shard_map/reduce_scatter | solution.py:1130
  423.9 408.0 %reduce-scatter.6.cloned.1.call-start = ((), (), s32[]{:S(2)}) async-start(), calls=%async_computation.8 | async-start | bytes 6488064 | tf_op jit(solution)/shard_map/reduce_scatter | solution.py:1130
  457.4 57.1 %copy-start.14 = (bf16[2048,512]{1,0:T(8,128)(2,1)S(1)}, bf16[2048,512]{1,0:T(8,128)(2,1)}, u32[]{:S(2)}) copy-start(bf16[2048,512]{1,0:T(8,128)(2,1)} %all-gather.5.cloned.1.call-done) | copy-start | bytes 6291460
  520.3 87.4 %copy-start.7 = (f32[1,2048]{1,0:T(1,128)S(1)}, f32[1,2048]{1,0:T(1,128)}, u32[]{:S(2)}) copy-start(f32[1,2048]{1,0:T(1,128)} %get-tuple-element.57) | copy-start | bytes 24580
  605.2 24.5 %collective-permute-start.3 = (bf16[4,8,1536]{2,1,0:T(8,128)(2,1)}, bf16[4,8,1536]{2,1,0:T(8,128)(2,1)S(1)}, u32[]{:S(2)}, u32[]{:S(2)}) collective-permute-start(bf16[4,8,1536]{2,1,0:T(8,128)(2,1)} %get-tuple-element.51), channel_id=1, source_target_pairs={{4,0},{8,4},{12,8},{16,12},{20,16},{24,20},{28,24},{5,1},{9,5},{13... | collective-permute-start | bytes 294920 | tf_op jit(solution)/shard_map/ppermute | solution.py:963
  644.1 12.2 %copy-start.13 = (bf16[4,256,1536]{2,1,0:T(8,128)(2,1)S(1)}, bf16[4,256,1536]{2,1,0:T(8,128)(2,1)}, u32[]{:S(2)}) copy-start(bf16[4,256,1536]{2,1,0:T(8,128)(2,1)} %fusion.54) | copy-start | bytes 9437188
  644.4 8.5 %collective-permute-start.10 = (bf16[2320]{0:T(1024)(128)(2,1)S(1)}, bf16[2320]{0:T(1024)(128)(2,1)S(1)}, u32[]{:S(2)}, u32[]{:S(2)}) collective-permute-start(bf16[2320]{0:T(1024)(128)(2,1)S(1)} %get-tuple-element.99), channel_id=1, source_target_pairs={{0,28},{4,0},{8,4},{12,8},{16,12},{20,16},{24,20},{28,24},{1,29},{... | collective-permute-start | bytes 13928 | tf_op jit(solution)/shard_map/ppermute | solution.py:1011
  644.4 11.3 %collective-permute-start.9 = (bf16[2320]{0:T(1024)(128)(2,1)S(1)}, bf16[2320]{0:T(1024)(128)(2,1)S(1)}, u32[]{:S(2)}, u32[]{:S(2)}) collective-permute-start(bf16[2320]{0:T(1024)(128)(2,1)S(1)} %get-tuple-element.100), channel_id=1, source_target_pairs={{0,24},{4,28},{8,0},{12,4},{16,8},{20,12},{24,16},{28,20},{1,25},{... | collective-permute-start | bytes 13928 | tf_op jit(solution)/shard_map/ppermute | solution.py:1011
  644.5 11.3 %collective-permute-start.8 = (bf16[2320]{0:T(1024)(128)(2,1)S(1)}, bf16[2320]{0:T(1024)(128)(2,1)S(1)}, u32[]{:S(2)}, u32[]{:S(2)}) collective-permute-start(bf16[2320]{0:T(1024)(128)(2,1)S(1)} %get-tuple-element.101), channel_id=1, source_target_pairs={{0,20},{4,24},{8,28},{12,0},{16,4},{20,8},{24,12},{28,16},{1,21},{... | collective-permute-start | bytes 13928 | tf_op jit(solution)/shard_map/ppermute | solution.py:1011
  649.7 18.9 %collective-permute-start.1 = (bf16[4,64,2048]{2,1,0:T(8,128)(2,1)S(1)}, bf16[4,64,2048]{2,1,0:T(8,128)(2,1)S(1)}, u32[]{:S(2)}, u32[]{:S(2)}) collective-permute-start(bf16[4,64,2048]{2,1,0:T(8,128)(2,1)S(1)} %get-tuple-element.113), channel_id=1, source_target_pairs={{0,1},{1,0},{2,3},{3,2},{4,5},{5,4},{6,7},{7,6},{8,9},{9,8},{10,11... | collective-permute-start | bytes 3145736 | tf_op jit(solution)/shard_map/ppermute | solution.py:983
  649.7 18.2 %collective-permute-start.7 = (bf16[2320]{0:T(1024)(128)(2,1)S(1)}, bf16[2320]{0:T(1024)(128)(2,1)S(1)}, u32[]{:S(2)}, u32[]{:S(2)}) collective-permute-start(bf16[2320]{0:T(1024)(128)(2,1)S(1)} %get-tuple-element.102), channel_id=1, source_target_pairs={{0,16},{4,20},{8,24},{12,28},{16,0},{20,4},{24,8},{28,12},{1,17},{... | collective-permute-start | bytes 13928 | tf_op jit(solution)/shard_map/ppermute | solution.py:1011
  652.8 15.2 %collective-permute-start.6 = (bf16[2320]{0:T(1024)(128)(2,1)S(1)}, bf16[2320]{0:T(1024)(128)(2,1)S(1)}, u32[]{:S(2)}, u32[]{:S(2)}) collective-permute-start(bf16[2320]{0:T(1024)(128)(2,1)S(1)} %get-tuple-element.103), channel_id=1, source_target_pairs={{0,12},{4,16},{8,20},{12,24},{16,28},{20,0},{24,4},{28,8},{1,13},{... | collective-permute-start | bytes 13928 | tf_op jit(solution)/shard_map/ppermute | solution.py:1011
  655.7 12.3 %collective-permute-start.5 = (bf16[2320]{0:T(1024)(128)(2,1)S(1)}, bf16[2320]{0:T(1024)(128)(2,1)S(1)}, u32[]{:S(2)}, u32[]{:S(2)}) collective-permute-start(bf16[2320]{0:T(1024)(128)(2,1)S(1)} %get-tuple-element.104), channel_id=1, source_target_pairs={{0,8},{4,12},{8,16},{12,20},{16,24},{20,28},{24,0},{28,4},{1,9},{5... | collective-permute-start | bytes 13928 | tf_op jit(solution)/shard_map/ppermute | solution.py:1011
  655.8 12.3 %collective-permute-start.4 = (bf16[2320]{0:T(1024)(128)(2,1)S(1)}, bf16[2320]{0:T(1024)(128)(2,1)S(1)}, u32[]{:S(2)}, u32[]{:S(2)}) collective-permute-start(bf16[2320]{0:T(1024)(128)(2,1)S(1)} %get-tuple-element.98), channel_id=1, source_target_pairs={{0,4},{4,8},{8,12},{12,16},{16,20},{20,24},{24,28},{28,0},{1,5},{5... | collective-permute-start | bytes 13928 | tf_op jit(solution)/shard_map/ppermute | solution.py:1011
  668.0 155.3 %collective-permute-start = (bf16[4,64,2048]{2,1,0:T(8,128)(2,1)}, bf16[4,64,2048]{2,1,0:T(8,128)(2,1)}, u32[]{:S(2)}, u32[]{:S(2)}) collective-permute-start(bf16[4,64,2048]{2,1,0:T(8,128)(2,1)} %get-tuple-element.112), channel_id=1, source_target_pairs={{0,1},{1,0},{2,3},{3,2},{4,5},{5,4},{6,7},{7,6},{8,9},{9,8},{10,11... | collective-permute-start | bytes 3145736 | tf_op jit(solution)/shard_map/ppermute | solution.py:983
  668.1 147.9 %collective-permute-start.11 = (f32[528]{0:T(1024)S(1)}, f32[528]{0:T(1024)S(1)}, u32[]{:S(2)}, u32[]{:S(2)}) collective-permute-start(f32[528]{0:T(1024)S(1)} %slice.104), channel_id=1, source_target_pairs={{0,1},{1,0},{2,3},{3,2},{4,5},{5,4},{6,7},{7,6},{8,9},{9,8},{10,11... | collective-permute-start | bytes 6344 | tf_op jit(solution)/shard_map/ppermute | solution.py:983
  671.3 152.0 %collective-permute-start.2 = (bf16[4,64,2048]{2,1,0:T(8,128)(2,1)}, bf16[4,64,2048]{2,1,0:T(8,128)(2,1)}, u32[]{:S(2)}, u32[]{:S(2)}) collective-permute-start(bf16[4,64,2048]{2,1,0:T(8,128)(2,1)} %fusion.30), channel_id=1, source_target_pairs={{0,2},{1,3},{2,0},{3,1},{4,6},{5,7},{6,4},{7,5},{8,10},{9,11},{10,... | collective-permute-start | bytes 3145736 | tf_op jit(solution)/shard_map/ppermute | solution.py:983
  816.0 6.1 collective-permute-start.12
  (20 other events, 113.7 us)
Sparse Core Ops, SparseCore 0:
  10.8 70.4 all-gather.4
  84.0 106.8 all-gather.10
  193.1 98.9 all-gather.8
  294.1 92.4 all-gather.6
  412.8 108.1 reduce-scatter.7
  524.5 122.2 reduce-scatter.3
  650.4 146.2 reduce-scatter.5

commit v3 on v2

v3 whole, which is shorter than its diff:
```python
import functools

import jax
import jax.numpy as jnp
from jax import lax
from jax.experimental import pallas as pl
from jax.experimental.pallas import tpu as pltpu
from jax.sharding import PartitionSpec as P

HD = 128
KCONV = 4
RIM = 8
PAIR = 2
OUTER = 4
SUBS = 2

epsilon = 1e-06
f32 = jnp.float32
bf16 = jnp.bfloat16
MESH = pl.DeviceIdType.MESH
VMEM_LIMIT = 60 * 1024 * 1024


def ring_walk(place, n):
    inner = n // OUTER
    if inner == 1:
        return place
    late = jnp.maximum(place - OUTER, 0)
    turn, along = lax.div(late, inner - 1), lax.rem(late, inner - 1)
    odd = lax.rem(turn, 2)
    back = (OUTER - 1 - turn) * inner + (1 - odd) * (along + 1) + odd * (inner - 1 - along)
    return jnp.where(place < OUTER, place * inner, back)


def ring_place(index, n):
    inner = n // OUTER
    if inner == 1:
        return index
    out, along = lax.div(index, inner), lax.rem(index, inner)
    odd = lax.rem(OUTER - 1 - out, 2)
    turn = (1 - odd) * (along - 1) + odd * (inner - 1 - along)
    return jnp.where(along == 0, out, OUTER + (OUTER - 1 - out) * (inner - 1) + turn)


def remote(source, target, send, recv, **device):
    return pltpu.make_async_remote_copy(
        src_ref=source, dst_ref=target, send_sem=send, recv_sem=recv,
        device_id=device, device_id_type=MESH,
    )


def swap_pair(index):
    return index + 1 - 2 * lax.rem(index, 2)


def swap_half(index, count):
    return lax.rem(index + count // 2, count)


class Ring:
    def __init__(self, n, rows, lanes, send, recv):
        self.n, self.lanes, self.send, self.recv = n, range(lanes), send, recv
        self.me = lax.axis_index("dp")
        self.place = ring_place(self.me, n)
        self.near = (
            ring_walk(lax.rem(self.place + 1, n), n),
            ring_walk(lax.rem(self.place + n - 1, n), n),
        )
        self.slab = rows // lanes

    def greet(self, barrier):
        for device in self.near:
            pl.semaphore_signal(barrier, inc=1, device_id={"dp": device}, device_id_type=MESH)

    def strip(self, lane):
        return pl.ds(lane * self.slab, self.slab)

    def owner(self, hop, lane):
        return ring_walk(lax.rem(self.place + self.n + (2 * (lane % 2) - 1) * hop, self.n), self.n)

    def copy(self, source, target, hop, lane):
        return remote(
            source, target, self.send.at[hop, lane], self.recv.at[hop, lane], dp=self.near[lane % 2]
        )


class RingGather(Ring):
    def __init__(self, n, rows, full, send, recv, own=None, local=None, lanes=2 * SUBS):
        super().__init__(n, rows, lanes, send, recv)
        self.own, self.full, self.local = own, full, local

    def first(self, lane):
        strip = self.strip(lane)
        return self.copy(self.own.at[strip, :], self.full.at[self.me, strip, :], 1, lane)

    def later(self, hop, lane):
        piece = self.full.at[self.owner(hop - 1, lane), self.strip(lane), :]
        return self.copy(piece, piece, hop, lane)

    def stay(self):
        return pltpu.make_async_copy(self.own, self.full.at[self.me], self.local)

    def start(self):
        self.stay().start()
        for lane in self.lanes:
            self.first(lane).start()

    def resume(self, hop):
        for lane in self.lanes:
            self.later(hop, lane).start()

    def advance(self, hop):
        for lane in self.lanes:
            self.later(hop - 1, lane).wait_recv()
            self.later(hop, lane).start()

    def settle(self, begin, end):
        for lane in self.lanes:
            self.later(end, lane).wait_recv()
            if begin == 1:
                self.first(lane).wait_send()

        def drain(hop, carry):
            for lane in self.lanes:
                self.later(hop, lane).wait_send()
            return carry

        lax.fori_loop(max(begin, 2), end + 1, drain, 0)
        if begin == 1:
            self.stay().wait()


class RingScatter(Ring):
    def __init__(self, n, rows, part, inward, total, send, recv, lanes=2 * SUBS):
        super().__init__(n, rows, lanes, send, recv)
        self.part, self.inward, self.total = part, inward, total
        self.half = rows // 2

    def strip(self, lane):
        return pl.ds((lane % 2) * self.half + (lane // 2) * self.slab, self.slab)

    def sender(self, hop, lane):
        strip = self.strip(lane)
        return self.copy(self.inward.at[hop - 1, strip, :], self.inward.at[hop, strip, :], hop, lane)

    def ways(self, value_of):
        for way in range(2):
            value = value_of(way)
            for lane in self.lanes[way::2]:
                at = (lane // 2) * self.slab
                yield lane, value[at : at + self.slab]

    def start(self):
        for lane, value in self.ways(lambda way: self.part(self.owner(1, way), way)):
            self.inward[0, self.strip(lane), :] = value.astype(bf16)
            self.sender(1, lane).start()

    def summed(self, hop, lane, value):
        self.sender(hop, lane).wait_recv()
        return self.inward[hop, self.strip(lane), :].astype(f32) + value

    def advance(self, hop):
        for lane, value in self.ways(lambda way: self.part(self.owner(hop, way), way)):
            self.inward[hop - 1, self.strip(lane), :] = self.summed(hop - 1, lane, value).astype(bf16)
            self.sender(hop, lane).start()

    def finish(self):
        for lane, value in self.ways(lambda way: self.part(self.me, way)):
            self.total[self.strip(lane), :] = self.summed(self.n - 1, lane, value)

        def drain(hop, carry):
            for lane in self.lanes:
                self.sender(hop, lane).wait_send()
            return carry

        lax.fori_loop(1, self.n, drain, 0)


def held_part(ref):
    half = ref.shape[1] // 2
    return lambda owner, way: ref[owner, way * half : (way + 1) * half, :].astype(f32)


def grad_part(rows, left_ref, right_ref, spare_ref=None):
    half = rows // 2

    def part(owner, way):
        at = owner * rows + way * half
        if half % 128 == 0:
            return dot(left_ref[:, pl.ds(pl.multiple_of(at, half), half)], right_ref[...], 0, 0)
        block = lax.div(at, 128) * 128
        spare_ref[...] = dot(left_ref[:, pl.ds(pl.multiple_of(block, 128), 128)], right_ref[...], 0, 0)
        return spare_ref[pl.ds(pl.multiple_of(at - block, half), half), :]

    return part


def spare(rows, columns):
    return pltpu.VMEM((8, 128) if (rows // 2) % 128 == 0 else (128, columns), f32)


def ring_semaphores(n, lanes=2 * SUBS):
    return [pltpu.SemaphoreType.DMA((n, lanes)), pltpu.SemaphoreType.DMA((n, lanes))]


def halves(value):
    high = value.astype(bf16)
    return (high, (value - high.astype(f32)).astype(bf16))


def dot(left, right, left_dim=1, right_dim=0):
    return lax.dot_general(
        left, right, (((left_dim,), (right_dim,)), ((), ())), preferred_element_type=f32
    )


def beside(*parts):
    return jnp.concatenate(parts, axis=1)


def full_product(left, right, left_dim=1, right_dim=0):
    return (
        dot(left[0], right[0], left_dim, right_dim)
        + dot(left[1], right[0], left_dim, right_dim)
        + dot(left[0], right[1], left_dim, right_dim)
    )


def narrow_product(left, right, left_dim=1):
    both = dot(left[0], beside(*right), left_dim, 0)
    width = right[0].shape[1]
    return both[:, :width] + both[:, width:] + dot(left[1], right[0], left_dim, 0)


def short_product(left, right):
    return dot(beside(*left), jnp.concatenate([right, right], axis=0))


def short_product_t(left, right):
    return dot(beside(*left), beside(right, right), 1, 1)


def square_product(left, right):
    lower = beside(right[0], jnp.zeros_like(right[0]))
    both = dot(beside(*left), jnp.concatenate([beside(*right), lower], axis=0))
    return both[:, :HD] + both[:, HD:]


def conv_act(x_ref, x_in, filt_ref, column, rows):
    x_ref[...] = x_in.astype(f32)
    running = None
    for tap in range(KCONV):
        term = filt_ref[pl.ds(column * KCONV + tap, 1), :] * x_ref[pl.ds(RIM - KCONV + 1 + tap, rows), :]
        running = term if running is None else running + term
    gate = jax.nn.sigmoid(running)
    return running, gate


def unit_scale(act):
    return lax.rsqrt(jnp.sum(act * act, axis=-1, keepdims=True) + epsilon)


def masks(rows):
    at_row = lax.broadcasted_iota(jnp.int32, (rows, rows), 0)
    at_col = lax.broadcasted_iota(jnp.int32, (rows, rows), 1)
    return at_row, at_col


def chain_lag(me, limit):
    return jnp.minimum(lax.div(3 * me + 4, 5), limit)


def mixer_kernel(
    n, rows, steps, pairs, limit,
    pq_ref, pk_ref, pv_ref, strength_ref, filt_ref, gain_ref, own_ref,
    normed_ref, mix_ref, carry_ref, inv_ref, kw_ref, state_ref, full_ref,
    x_ref, low_ref, sol_ref, end_ref, recv_ref, send_ref,
    send_sem, recv_sem, ring_send, ring_recv, local_sem,
):
    me = lax.axis_index("dp")
    step = pl.program_id(0)
    lag = chain_lag(me, limit)
    ring = RingGather(n, own_ref.shape[0], full_ref, ring_send, ring_recv, own_ref, local_sem)

    def hop(at, h):
        return remote(
            send_ref.at[at, h], recv_ref.at[at, h], send_sem.at[at, h], recv_sem.at[at, h],
            dp=lax.rem(me + 1, n),
        )

    @pl.when(step == 0)
    def _():
        barrier = pltpu.get_barrier_semaphore()
        ring.greet(barrier)

        @pl.when(me > 0)
        def _():
            pl.semaphore_signal(
                barrier, inc=1, device_id={"dp": lax.rem(me + n - 1, n)}, device_id_type=MESH
            )

        @pl.when(me == 0)
        def _():
            recv_ref[...] = jnp.zeros_like(recv_ref)

        @pl.when(me < n - 1)
        def _():
            pl.semaphore_wait(barrier, 3)

        @pl.when(me == n - 1)
        def _():
            pl.semaphore_wait(barrier, 2)

        ring.start()

    each = -(-(n - 2) // (steps - 1))

    @pl.when(step > 0)
    def _():
        for i in range(each):
            at = (step - 1) * each + i + 2

            @pl.when(at < n)
            def _():
                ring.advance(at)

    @pl.when(step < steps)
    def _():
        pair = lax.rem(step, pairs)
        at_row, at_col = masks(HD)
        all_row, all_col = masks(rows)
        acts = []
        for column, ref in enumerate((pq_ref, pk_ref, pv_ref)):
            running, gate = conv_act(x_ref, ref[0], filt_ref, column, rows)
            acts.append(running * gate)
        strengths = strength_ref[0]
        lane = lax.broadcasted_iota(jnp.int32, strengths.shape, 1)
        heads = []
        for h in range(PAIR):
            cut = slice(h * HD, (h + 1) * HD)
            act_q, act_k = acts[0][:, cut], acts[1][:, cut]
            q = (act_q * unit_scale(act_q)).astype(bf16)
            k = (act_k * unit_scale(act_k)).astype(bf16)
            v = acts[2][:, cut].astype(bf16)
            beta = jnp.sum(jnp.where(lane == pair * PAIR + h, strengths, 0.0), axis=-1, keepdims=True)
            low = jnp.where(all_row > all_col, beta * dot(k, k, 1, 1), 0.0)
            low_ref[h] = low
            first = (at_row & 1 == 1) & (at_row - 1 == at_col)
            for b in range(2):
                block = low[b * HD : (b + 1) * HD, b * HD : (b + 1) * HD]
                sol_ref[h, b] = jnp.where(at_row == at_col, 1.0, 0.0) - jnp.where(first, block, 0.0)
            heads.append((q, k, v, beta))
        blocks = [(h, b) for h in range(PAIR) for b in range(2)]

        def refine(level, carry):
            band_row, band_col = at_row >> level, at_col >> level
            band = (band_row & 1 == 1) & (band_row - 1 == band_col)
            sols = [halves(sol_ref[h, b]) for h, b in blocks]
            mids = [
                halves(
                    square_product(
                        halves(
                            jnp.where(
                                band, low_ref[h, b * HD : (b + 1) * HD, b * HD : (b + 1) * HD], 0.0
                            )
                        ),
                        sol,
                    )
                )
                for (h, b), sol in zip(blocks, sols)
            ]
            for (h, b), sol, mid in zip(blocks, sols, mids):
                sol_ref[h, b] = sol_ref[h, b] - square_product(sol, mid)
            return carry

        lax.fori_loop(1, (HD - 1).bit_length(), refine, 0)

        wides = []
        for h in range(PAIR):
            q, k, v, beta = heads[h]
            top, low = halves(sol_ref[h, 0]), halves(sol_ref[h, 1])
            mid = halves(square_product(halves(low_ref[h, HD:, :HD]), top))
            corner = -square_product(low, mid)
            inv = jnp.concatenate(
                [
                    beside(sol_ref[h, 0], jnp.zeros((HD, HD), f32)),
                    beside(corner, sol_ref[h, 1]),
                ],
                axis=0,
            )
            inv_ref[h] = inv
            right = beside(beta * k.astype(f32), beta * v.astype(f32))
            wides.append(halves(full_product(halves(inv), halves(right))))
        for h in range(PAIR):
            q, k, v, beta = heads[h]
            scores = halves(jnp.where(all_row >= all_col, dot(q, k, 1, 1), 0.0))
            seen = full_product(scores, wides[h])
            carry_ref[step, h] = q.astype(f32) - seen[:, :HD]
            mix_ref[step, h] = seen[:, HD:]
            kwu = dot(k, wides[h][0], 0, 0) + dot(k, wides[h][1], 0, 0)
            kw_ref[step, h] = kwu[:, :HD]
            end_ref[step, h] = kwu[:, HD:]

    at = step - lag

    @pl.when((at >= 0) & (at < steps))
    def _():
        for h in range(PAIR):
            @pl.when(me > 0)
            def _():
                hop(at, h).wait_recv()

            state = recv_ref[at, h]
            out_state = end_ref[at, h] + state.astype(f32) - short_product(halves(kw_ref[at, h]), state)
            send_ref[at, h] = out_state.astype(bf16)

            @pl.when(me < n - 1)
            def _():
                hop(at, h).start()

        seq, pair = lax.div(at, pairs), lax.rem(at, pairs)
        for h in range(PAIR):
            state = recv_ref[at, h]
            state_ref[at, h] = state
            mix = mix_ref[at, h] + short_product(halves(carry_ref[at, h]), state)
            mix_ref[at, h] = mix
            scale = lax.rsqrt(jnp.mean(mix * mix, axis=-1, keepdims=True) + epsilon)
            lanes = pl.ds(pl.multiple_of((pair * PAIR + h) * HD, HD), HD)
            normed_ref[seq, :, lanes] = (mix * scale * gain_ref[...]).astype(bf16)

    @pl.when(step == steps + limit - 1)
    def _():
        ring.settle(1, n - 1)

        @pl.when(me < n - 1)
        def _():
            def done(at, carry):
                for h in range(PAIR):
                    hop(at, h).wait_send()
                return carry

            lax.fori_loop(0, steps, done, 0)


def mixer(projected, strength, filters, gain, weight):
    n = lax.axis_size("dp")
    seqs, extended, width = projected.shape
    rows = extended - RIM
    local = width // 3
    pairs = local // (PAIR * HD)
    wide = PAIR * HD
    steps = seqs * pairs
    limit = min((3 * (n - 1) + 4) // 5, steps)
    assert rows == 2 * HD
    vmem, anywhere = pl.BlockSpec(memory_space=pltpu.VMEM), pl.BlockSpec(memory_space=pl.ANY)

    def now(i):
        return jnp.minimum(i, steps - 1)

    def part(column):
        return pl.BlockSpec(
            (1, extended, wide),
            lambda i: (lax.div(now(i), pairs), 0, column * pairs + lax.rem(now(i), pairs)),
        )

    def whole(*shape):
        return pl.BlockSpec(shape, lambda i: (0,) * len(shape))

    total = steps * PAIR
    return pl.pallas_call(
        functools.partial(mixer_kernel, n, rows, steps, pairs, limit),
        grid=(steps + limit,),
        in_specs=[
            part(0), part(1), part(2),
            pl.BlockSpec((1, rows, strength.shape[2]), lambda i: (lax.div(now(i), pairs), 0, 0)),
            pl.BlockSpec((3 * KCONV, wide), lambda i: (0, lax.rem(now(i), pairs))),
            whole(1, HD),
            vmem,
        ],
        out_specs=[
            whole(seqs, rows, local),
            whole(steps, PAIR, rows, HD),
            whole(steps, PAIR, rows, HD),
            pl.BlockSpec((PAIR, rows, rows), lambda i: (now(i), 0, 0)),
            whole(steps, PAIR, HD, HD),
            whole(steps, PAIR, HD, HD),
            anywhere,
        ],
        out_shape=[
            jax.ShapeDtypeStruct((seqs, rows, local), bf16),
            jax.ShapeDtypeStruct((steps, PAIR, rows, HD), f32),
            jax.ShapeDtypeStruct((steps, PAIR, rows, HD), f32),
            jax.ShapeDtypeStruct((total, rows, rows), f32),
            jax.ShapeDtypeStruct((steps, PAIR, HD, HD), f32),
            jax.ShapeDtypeStruct((steps, PAIR, HD, HD), bf16),
            jax.ShapeDtypeStruct((n,) + weight.shape, bf16),
        ],
        scratch_shapes=[
            pltpu.VMEM((extended, wide), f32),
            pltpu.VMEM((PAIR, rows, rows), f32),
            pltpu.VMEM((PAIR, 2, HD, HD), f32),
            pltpu.VMEM((steps, PAIR, HD, HD), f32),
            pltpu.VMEM((steps, PAIR, HD, HD), bf16),
            pltpu.VMEM((steps, PAIR, HD, HD), bf16),
            pltpu.SemaphoreType.DMA((steps, PAIR)),
            pltpu.SemaphoreType.DMA((steps, PAIR)),
        ]
        + ring_semaphores(n)
        + [pltpu.SemaphoreType.DMA],
        compiler_params=pltpu.CompilerParams(
            collective_id=0, has_side_effects=True, vmem_limit_bytes=VMEM_LIMIT,
            dimension_semantics=("arbitrary",),
        ),
        name="mixer",
    )(projected, projected, projected, strength, filters, gain, weight)


def mixer_back_kernel(
    n, rows, steps, pairs,
    pq_ref, pk_ref, pv_ref, strength_ref, filt_ref, gain_ref,
    back_ref, mix_ref, carry_ref, inv_ref, kw_ref, state_ref,
    proj_ref, logit_ref, conv_ref, head_ref,
    xq_ref, xk_ref, xv_ref, bc_ref, high_ref, low_ref, recv_ref, send_ref, last_ref, rim_ref, next_ref,
    send_sem, recv_sem, rim_send, rim_recv,
):
    me = lax.axis_index("dp")
    step = pl.program_id(0)
    wide = PAIR * HD
    local = proj_ref.shape[2] // 3

    def to_rim(seq):
        return remote(
            rim_ref.at[seq], next_ref.at[seq], rim_send.at[seq], rim_recv.at[seq],
            dp=lax.rem(me + n - 1, n),
        )

    def hop(at, h):
        return remote(
            send_ref.at[at, h], recv_ref.at[at, h], send_sem.at[at, h], recv_sem.at[at, h],
            dp=lax.rem(me + n - 1, n),
        )

    @pl.when(step == 0)
    def _():
        barrier = pltpu.get_barrier_semaphore()

        @pl.when(me < n - 1)
        def _():
            pl.semaphore_signal(barrier, inc=1, device_id={"dp": lax.rem(me + 1, n)}, device_id_type=MESH)

        @pl.when(me == n - 1)
        def _():
            recv_ref[...] = jnp.zeros_like(recv_ref)
            next_ref[...] = jnp.zeros_like(next_ref)

        @pl.when(me > 0)
        def _():
            pl.semaphore_wait(barrier, 1)

        head_ref[...] = jnp.zeros_like(head_ref)
        bc_ref[...] = jnp.zeros_like(bc_ref)
        conv_ref[...] = jnp.zeros_like(conv_ref)

    @pl.when(step < steps)
    def _():
        adds = []
        head_sum = jnp.zeros((1, HD), f32)
        for h in range(PAIR):
            mix, back = mix_ref[0, h], back_ref[0, :, h * HD : (h + 1) * HD]
            scale = lax.rsqrt(jnp.mean(mix * mix, axis=-1, keepdims=True) + epsilon)
            unit = mix * scale
            head_sum = head_sum + jnp.sum(back * unit, axis=0, keepdims=True)
            scaled = back * gain_ref[...]
            out = halves(scale * (scaled - unit * jnp.mean(scaled * unit, axis=-1, keepdims=True)))
            high_ref[step, h], low_ref[step, h] = out
            adds.append(narrow_product(halves(carry_ref[0, h]), out, 0))
        head_ref[...] += jnp.where(
            lax.broadcasted_iota(jnp.int32, head_ref.shape, 0) == 0, head_sum, 0.0
        )

        for h in range(PAIR):
            @pl.when(me < n - 1)
            def _():
                hop(step, h).wait_recv()

            end, kw = recv_ref[step, h], halves(kw_ref[0, h])
            before = adds[h] + end.astype(f32) - dot(kw[0], end, 0, 0) - dot(kw[1], end, 0, 0)
            send_ref[step, h] = before.astype(bf16)

            @pl.when(me > 0)
            def _():
                hop(step, h).start()

    @pl.when(step >= steps)
    def _():
        now = step - steps
        seq, pair = lax.div(now, pairs), lax.rem(now, pairs)
        @pl.when(pair == 0)
        def _():
            logit_ref[...] = jnp.zeros_like(logit_ref)

        at_row, at_col = masks(rows)
        strengths = strength_ref[0]
        lane = lax.broadcasted_iota(jnp.int32, strengths.shape, 1)
        run_q, gate_q = conv_act(xq_ref, pq_ref[0], filt_ref, 0, rows)
        run_k, gate_k = conv_act(xk_ref, pk_ref[0], filt_ref, 1, rows)
        run_v, gate_v = conv_act(xv_ref, pv_ref[0], filt_ref, 2, rows)
        act_q, act_k, act_v = run_q * gate_q, run_k * gate_k, run_v * gate_v
        back_acts = ([], [], [])
        for h in range(PAIR):
            cut = slice(h * HD, (h + 1) * HD)
            scale_q, scale_k = unit_scale(act_q[:, cut]), unit_scale(act_k[:, cut])
            unit_q, unit_k = act_q[:, cut] * scale_q, act_k[:, cut] * scale_k
            q, k, v = unit_q.astype(bf16), unit_k.astype(bf16), act_v[:, cut].astype(bf16)
            chosen = lane == pair * PAIR + h
            beta = jnp.sum(jnp.where(chosen, strengths, 0.0), axis=-1, keepdims=True)
            gram = dot(k, k, 1, 1)
            scores = halves(jnp.where(at_row >= at_col, dot(q, k, 1, 1), 0.0))
            state, end = state_ref[0, h], recv_ref[now, h]
            out = (high_ref[now, h], low_ref[now, h])
            inv = halves(inv_ref[h])
            through = dot(k, beside(state, end))
            rest = v.astype(f32) - through[:, :HD]
            update = halves(narrow_product(inv, halves(beta * rest)))
            back_update = halves(narrow_product(scores, out, 0) + through[:, HD:])
            back_scores = short_product_t(out, update[0]) + dot(out[0], update[1], 1, 1)
            back_scores = halves(jnp.where(at_row >= at_col, back_scores, 0.0))
            solved = narrow_product(inv, back_update, 0)
            terms = halves(solved)
            back_low = short_product_t(terms, update[0]) + dot(terms[0], update[1], 1, 1)
            back_low = jnp.where(at_row > at_col, -back_low, 0.0)
            back_beta = jnp.sum(back_low * gram, axis=-1, keepdims=True) + jnp.sum(
                solved * rest, axis=-1, keepdims=True
            )
            back_gram = beta * back_low
            back_gram = halves(back_gram + back_gram.T)
            back_value = beta * solved
            back_q = short_product_t(out, state) + dot(back_scores[0], k) + dot(back_scores[1], k)
            back_k = (
                dot(back_scores[0], q, 0, 0)
                + dot(back_scores[1], q, 0, 0)
                + short_product_t(update, end)
                + dot(back_gram[0], k)
                + dot(back_gram[1], k)
                - short_product_t(halves(back_value), state)
            )
            logit_ref[0] += jnp.where(chosen, back_beta * beta * (1.0 - beta), 0.0)
            back_acts[0].append(
                (back_q - unit_q * jnp.sum(unit_q * back_q, axis=-1, keepdims=True)) * scale_q
            )
            back_acts[1].append(
                (back_k - unit_k * jnp.sum(unit_k * back_k, axis=-1, keepdims=True)) * scale_k
            )
            back_acts[2].append(back_value)

        for column, (running, gate, x_ref) in enumerate(
            ((run_q, gate_q, xq_ref), (run_k, gate_k, xk_ref), (run_v, gate_v, xv_ref))
        ):
            back_conv = beside(*back_acts[column]) * gate * (1.0 + running * (1.0 - gate))
            bc_ref[pl.ds(RIM, rows), :] = back_conv
            back_x, back_rim = None, None
            for tap in range(KCONV):
                weight = filt_ref[pl.ds(column * KCONV + tap, 1), :]
                term = weight * bc_ref[pl.ds(RIM + KCONV - 1 - tap, rows), :]
                edge = weight * bc_ref[pl.ds(KCONV - 1 - tap, RIM), :]
                back_x = term if back_x is None else back_x + term
                back_rim = edge if back_rim is None else back_rim + edge
                grad = jnp.sum(
                    back_conv * x_ref[pl.ds(RIM - KCONV + 1 + tap, rows), :], axis=0, keepdims=True
                )
                conv_ref[pair, pl.ds(column * KCONV + tap, 1), :] += grad
            lanes = pl.ds(pl.multiple_of(column * local + pair * wide, wide), wide)
            proj_ref[seq, :, lanes] = back_x.astype(bf16)
            last_ref[seq, :, lanes] = back_x[rows - RIM :, :]
            rim_ref[seq, :, lanes] = back_rim.astype(bf16)

        @pl.when((pair == pairs - 1) & (me > 0))
        def _():
            to_rim(seq).start()

    @pl.when(step == 2 * steps - 1)
    def _():
        seqs = steps // pairs

        @pl.when(me > 0)
        def _():
            def done(at, carry):
                for h in range(PAIR):
                    hop(at, h).wait_send()
                return carry

            lax.fori_loop(0, steps, done, 0)
            for seq in range(seqs):
                to_rim(seq).wait_send()

        @pl.when(me < n - 1)
        def _():
            for seq in range(seqs):
                to_rim(seq).wait_recv()

        for seq in range(seqs):
            edge = last_ref[seq] + next_ref[seq].astype(f32)
            proj_ref[seq, pl.ds(rows - RIM, RIM), :] = edge.astype(bf16)


def mixer_back(projected, strength, filters, gain, back_normed, mix, carry, inverse, kw, state):
    n = lax.axis_size("dp")
    seqs, extended, width = projected.shape
    rows = extended - RIM
    local = width // 3
    pairs = local // (PAIR * HD)
    wide = PAIR * HD
    steps = seqs * pairs
    def early(i):
        return jnp.minimum(i, steps - 1)

    def late(i):
        return jnp.maximum(i - steps, 0)

    def part(column):
        return pl.BlockSpec(
            (1, extended, wide),
            lambda i: (lax.div(late(i), pairs), 0, column * pairs + lax.rem(late(i), pairs)),
        )

    def tall(size, when):
        return pl.BlockSpec((1, PAIR, size, HD), lambda i: (when(i), 0, 0, 0))

    def seq(size, span):
        return pl.BlockSpec((1, size, span), lambda i: (lax.div(late(i), pairs), 0, 0))

    heads = strength.shape[2]
    return pl.pallas_call(
        functools.partial(mixer_back_kernel, n, rows, steps, pairs),
        grid=(2 * steps,),
        in_specs=[
            part(0), part(1), part(2),
            seq(rows, heads),
            pl.BlockSpec((3 * KCONV, wide), lambda i: (0, lax.rem(late(i), pairs))),
            pl.BlockSpec((1, HD), lambda i: (0, 0)),
            pl.BlockSpec(
                (1, rows, wide), lambda i: (lax.div(early(i), pairs), 0, lax.rem(early(i), pairs))
            ),
            tall(rows, early), tall(rows, early),
            pl.BlockSpec((PAIR, rows, rows), lambda i: (late(i), 0, 0)),
            tall(HD, early), tall(HD, late),
        ],
        out_specs=[
            pl.BlockSpec((seqs, rows, width), lambda i: (0, 0, 0)),
            seq(rows, heads),
            pl.BlockSpec((pairs, 3 * KCONV, wide), lambda i: (0, 0, 0)),
            pl.BlockSpec((8, HD), lambda i: (0, 0)),
        ],
        out_shape=[
            jax.ShapeDtypeStruct((seqs, rows, width), bf16),
            jax.ShapeDtypeStruct((seqs, rows, heads), f32),
            jax.ShapeDtypeStruct((pairs, 3 * KCONV, wide), f32),
            jax.ShapeDtypeStruct((8, HD), f32),
        ],
        scratch_shapes=[
            pltpu.VMEM((extended, wide), f32),
            pltpu.VMEM((extended, wide), f32),
            pltpu.VMEM((extended, wide), f32),
            pltpu.VMEM((rows + 2 * RIM, wide), f32),
            pltpu.VMEM((steps, PAIR, rows, HD), bf16),
            pltpu.VMEM((steps, PAIR, rows, HD), bf16),
            pltpu.VMEM((steps, PAIR, HD, HD), bf16),
            pltpu.VMEM((steps, PAIR, HD, HD), bf16),
            pltpu.VMEM((seqs, RIM, width), f32),
            pltpu.VMEM((seqs, RIM, width), bf16),
            pltpu.VMEM((seqs, RIM, width), bf16),
            pltpu.SemaphoreType.DMA((steps, PAIR)),
            pltpu.SemaphoreType.DMA((steps, PAIR)),
            pltpu.SemaphoreType.DMA((seqs,)),
            pltpu.SemaphoreType.DMA((seqs,)),
        ],
        compiler_params=pltpu.CompilerParams(
            collective_id=1, has_side_effects=True, vmem_limit_bytes=VMEM_LIMIT,
            dimension_semantics=("arbitrary",),
        ),
        name="mixer_back",
    )(
        projected, projected, projected, strength, filters, gain,
        back_normed, mix, carry, inverse, kw, state,
    )


def opening_kernel(
    n, tensor,
    q_ref, k_ref, v_ref, small_ref, tokens_ref, cot_ref, out_ref,
    qkv_ref, small_out, ext_ref, cot_out, full_out,
    zero_ref, local_sem, ring_send, ring_recv, side_send, side_recv, rim_send, rim_recv,
):
    me, t = lax.axis_index("dp"), lax.axis_index("tensor")
    place = ring_place(me, n)
    near = (ring_walk(lax.rem(place + 1, n), n), ring_walk(lax.rem(place + n - 1, n), n))
    core, cross = swap_pair(t), swap_half(t, tensor)
    rows, local = q_ref.shape
    own_len = tokens_ref.shape[1]
    slab = rows // (2 * SUBS)

    barrier = pltpu.get_barrier_semaphore()
    for device in ({"dp": near[0]}, {"dp": near[1]}, {"tensor": core}, {"tensor": cross}):
        pl.semaphore_signal(barrier, inc=1, device_id=device, device_id_type=MESH)

    @pl.when(me > 0)
    def _():
        pl.semaphore_signal(
            barrier, inc=1, device_id={"dp": lax.rem(me + n - 1, n), "tensor": tensor - 1},
            device_id_type=MESH,
        )

    def chunk(ref, at, offset):
        return ref.at[:, pl.ds(pl.multiple_of(offset + at * own_len, 8), own_len), :]

    mine = [
        pltpu.make_async_copy(ref, qkv_ref.at[me, :, pl.ds(c * local, local)], local_sem.at[c])
        for c, ref in enumerate((q_ref, k_ref, v_ref))
    ] + [
        pltpu.make_async_copy(small_ref, small_out.at[me], local_sem.at[3]),
        pltpu.make_async_copy(tokens_ref, chunk(ext_ref, t, RIM), local_sem.at[4]),
        pltpu.make_async_copy(cot_ref, chunk(cot_out, t, 0), local_sem.at[5]),
        pltpu.make_async_copy(out_ref, full_out.at[me], local_sem.at[7]),
    ]
    for copy in mine:
        copy.start()

    @pl.when(me == 0)
    def _():
        zero_ref[...] = jnp.zeros_like(zero_ref)
        blank = pltpu.make_async_copy(zero_ref, ext_ref.at[:, pl.ds(0, RIM), :], local_sem.at[6])
        blank.start()
        blank.wait()

    sends_rim = (me < n - 1) & (t == tensor - 1)

    @pl.when(sends_rim)
    def _():
        pl.semaphore_wait(barrier, 4 + tensor)

    @pl.when(jnp.logical_not(sends_rim))
    def _():
        pl.semaphore_wait(barrier, 4)

    def to_rim(peer):
        return remote(
            tokens_ref.at[:, pl.ds(own_len - RIM, RIM), :], ext_ref.at[:, pl.ds(0, RIM), :],
            rim_send.at[peer], rim_recv, dp=lax.rem(me + 1, n), tensor=peer,
        )

    sides = []
    for i, (own, full, offset) in enumerate(((tokens_ref, ext_ref, RIM), (cot_ref, cot_out, 0))):
        to_core = remote(own, chunk(full, t, offset), side_send.at[i, 0], side_recv.at[i, 0], tensor=core)
        to_cross = remote(own, chunk(full, t, offset), side_send.at[i, 1], side_recv.at[i, 1], tensor=cross)
        onward = remote(
            chunk(full, cross, offset), chunk(full, cross, offset),
            side_send.at[i, 2], side_recv.at[i, 2], tensor=core,
        )
        sides.append((to_core, to_cross, onward))
        to_core.start()
        to_cross.start()

    for copy in mine:
        copy.wait()

    @pl.when(sends_rim)
    def _():
        for peer in range(tensor):
            to_rim(peer).start()

    def ring(hop, lane):
        if lane == 2 * SUBS:
            owner = ring_walk(lax.rem(place + n - hop + 1, n), n)
            return remote(
                small_out.at[owner], small_out.at[owner],
                ring_send.at[hop, lane], ring_recv.at[hop, lane], dp=near[0],
            )
        way = lane % 2 if lane < 2 * SUBS else lane - 2 * SUBS - 1
        owner = ring_walk(lax.rem(place + n + (2 * way - 1) * (hop - 1), n), n)
        if lane > 2 * SUBS:
            piece = full_out.at[owner, pl.ds(way * (rows // 2), rows // 2), :]
            return remote(piece, piece, ring_send.at[hop, lane], ring_recv.at[hop, lane], dp=near[way])
        piece = qkv_ref.at[owner, pl.ds(lane * slab, slab), :]
        return remote(piece, piece, ring_send.at[hop, lane], ring_recv.at[hop, lane], dp=near[way])

    lanes = range(2 * SUBS + 3)

    def advance(hop, carry):
        for lane in lanes:
            @pl.when(hop > 1)
            def _():
                ring(hop - 1, lane).wait_recv()

            ring(hop, lane).start()
        for i, at in ((0, n // 2), (1, n - 1)):
            @pl.when(hop == at)
            def _():
                sides[i][1].wait_recv()
                sides[i][2].start()

        return carry

    lax.fori_loop(1, n, advance, 0)
    for lane in lanes:
        ring(n - 1, lane).wait_recv()

    def drain(hop, carry):
        for lane in lanes:
            ring(hop, lane).wait_send()
        return carry

    lax.fori_loop(1, n, drain, 0)
    for to_core, to_cross, onward in sides:
        to_core.wait()
        to_cross.wait_send()
        onward.wait()

    @pl.when(sends_rim)
    def _():
        for peer in range(tensor):
            to_rim(peer).wait_send()

    @pl.when(me > 0)
    def _():
        to_rim(0).wait_recv()


def opening(query_weight, key_weight, value_weight, small, tokens, cotangent, out_rows):
    n, tensor = lax.axis_size("dp"), lax.axis_size("tensor")
    rows, local = query_weight.shape
    seqs, own_len, width = tokens.shape
    vmem, anywhere = pl.BlockSpec(memory_space=pltpu.VMEM), pl.BlockSpec(memory_space=pl.ANY)
    lanes = 2 * SUBS + 3
    return pl.pallas_call(
        functools.partial(opening_kernel, n, tensor),
        in_specs=[vmem] * 7,
        out_specs=[anywhere] * 5,
        out_shape=[
            jax.ShapeDtypeStruct((n, rows, 3 * local), bf16),
            jax.ShapeDtypeStruct((n,) + small.shape, bf16),
            jax.ShapeDtypeStruct((seqs, RIM + tensor * own_len, width), bf16),
            jax.ShapeDtypeStruct((seqs, tensor * own_len, width), bf16),
            jax.ShapeDtypeStruct((n,) + out_rows.shape, bf16),
        ],
        scratch_shapes=[
            pltpu.VMEM((seqs, RIM, width), bf16),
            pltpu.SemaphoreType.DMA((8,)),
            pltpu.SemaphoreType.DMA((n, lanes)),
            pltpu.SemaphoreType.DMA((n, lanes)),
            pltpu.SemaphoreType.DMA((2, 3)),
            pltpu.SemaphoreType.DMA((2, 3)),
            pltpu.SemaphoreType.DMA((tensor,)),
            pltpu.SemaphoreType.DMA,
        ],
        compiler_params=pltpu.CompilerParams(
            collective_id=2, has_side_effects=True, vmem_limit_bytes=VMEM_LIMIT
        ),
        name="opening",
    )(query_weight, key_weight, value_weight, small, tokens, cotangent, out_rows)


def fold_kernel(
    n, n_seqs, tensor, backward, count,
    part_ref, own_ref, gain_ref, hidden_ref, *refs,
):
    t = lax.axis_index("tensor")
    core, cross = swap_pair(t), swap_half(t, tensor)
    both = swap_half(core, tensor)
    own_len = own_ref.shape[1]
    refs = list(refs)
    pieces, refs = refs[:count], refs[count:]
    outs = 1 if backward else count
    (rows_ref, keep_ref, sum_ref), made, refs = refs[:3], refs[3 : 3 + outs], refs[3 + outs :]
    (
        near_ref, far_ref, send_ref, own_sum_ref, a_send, a_recv, x_send, x_recv, g_send, g_recv,
        ring_send, ring_recv,
    ) = refs[:12]
    ring_refs = refs[12:]
    if backward:
        rings = [
            RingScatter(
                n, made[0].shape[0], grad_part(made[0].shape[0], *pieces, ring_refs[1]), ring_refs[0],
                made[0], ring_send.at[0], ring_recv.at[0],
            )
        ]
    else:
        rings = [
            RingGather(
                n, pieces[i].shape[0], made[i], ring_send.at[i], ring_recv.at[i], pieces[i], ring_refs[i]
            )
            for i in range(count)
        ]

    def advance(hop):
        if hop < n:
            for ring in rings:
                ring.advance(hop)

    barrier = pltpu.get_barrier_semaphore()
    rings[0].greet(barrier)
    for device in (core, cross):
        pl.semaphore_signal(barrier, inc=1, device_id={"tensor": device}, device_id_type=MESH)
    pl.semaphore_wait(barrier, 4)

    def span(at):
        return pl.ds(pl.multiple_of(at * own_len, own_len), own_len)

    def to_core(s, i):
        return remote(
            part_ref.at[s, span((core, both)[i]), :], near_ref.at[s, i],
            a_send.at[s, i], a_recv.at[s, i], tensor=core,
        )

    def to_cross(s):
        return remote(send_ref.at[s], far_ref.at[s], x_send.at[s], x_recv.at[s], tensor=cross)

    def gather(s, i):
        if i == 2:
            piece, peer = rows_ref.at[s, span(cross), :], core
        else:
            piece, peer = rows_ref.at[s, span(t), :], (cross, core)[i]
        return remote(piece, piece, g_send.at[s, i], g_recv.at[s, i], tensor=peer)

    for s in range(n_seqs):
        for i in (1, 0):
            to_core(s, i).start()
    for ring in rings:
        ring.start()

    def first(s, carry):
        to_core(s, 1).wait_recv()
        send_ref[s] = (
            part_ref[s, span(cross), :].astype(f32) + near_ref[s, 1].astype(f32)
        ).astype(bf16)
        to_cross(s).start()
        to_core(s, 0).wait_recv()
        own_sum_ref[s] = part_ref[s, span(t), :].astype(f32) + near_ref[s, 0].astype(f32)
        return carry

    lax.fori_loop(0, n_seqs, first, 0)
    sum_ref[...] = jnp.zeros_like(sum_ref)

    moments = (0, 1, 2, 3, 1) if backward else (0, 2, 0)

    def second(s, carry):
        to_cross(s).wait_recv()
        total = own_sum_ref[s] + far_ref[s].astype(f32)
        gain = gain_ref[...]
        own = own_ref[s].astype(f32)
        if backward:
            hidden = hidden_ref[s]
            scale = lax.rsqrt(jnp.mean(hidden * hidden, axis=-1, keepdims=True) + epsilon)
            unit = hidden * scale
            sum_ref[...] += jnp.sum(total * unit, axis=0, keepdims=True)
            scaled = total * gain
            kept = own + scale * (scaled - unit * jnp.mean(scaled * unit, axis=-1, keepdims=True))
            keep_ref[s] = kept
            rows_ref[s, span(t), :] = kept.astype(bf16)
        else:
            kept = own + total
            keep_ref[s] = kept
            scale = lax.rsqrt(jnp.mean(kept * kept, axis=-1, keepdims=True) + epsilon)
            rows_ref[s, span(t), :] = (kept * scale * gain).astype(bf16)
        gather(s, 0).start()
        gather(s, 1).start()

        for i, at in enumerate(moments[:-1]):
            @pl.when(s == at)
            def _():
                advance(2 + i)

        return carry

    lax.fori_loop(0, n_seqs, second, 0)

    def third(s, carry):
        gather(s, 0).wait_recv()
        gather(s, 2).start()

        @pl.when(s == moments[-1])
        def _():
            advance(1 + len(moments))

        return carry

    lax.fori_loop(0, n_seqs, third, 0)

    def rest(hop, carry):
        for ring in rings:
            ring.advance(hop)
        return carry

    lax.fori_loop(2 + len(moments), n, rest, 0)
    for ring in rings:
        if backward:
            ring.finish()
        else:
            ring.settle(1, n - 1)

    def last(s, carry):
        gather(s, 1).wait_recv()
        gather(s, 2).wait_recv()
        for i in range(2):
            to_core(s, i).wait_send()
        to_cross(s).wait_send()
        for i in range(3):
            gather(s, i).wait_send()
        return carry

    lax.fori_loop(0, n_seqs, last, 0)


def fold(part, own, gain, pieces, hidden=None):
    n, tensor = lax.axis_size("dp"), lax.axis_size("tensor")
    seqs, own_len, width = own.shape
    backward, count = hidden is not None, len(pieces)
    vmem, anywhere = pl.BlockSpec(memory_space=pltpu.VMEM), pl.BlockSpec(memory_space=pl.ANY)
    if backward:
        rows, columns = pieces[0].shape[1] // n, pieces[1].shape[1]
        made = [jax.ShapeDtypeStruct((rows, columns), f32)]
        ring_scratch = [pltpu.VMEM((n, rows, columns), bf16), spare(rows, columns)]
    else:
        hidden = jnp.zeros((8, 128), f32)
        made = [jax.ShapeDtypeStruct((n,) + piece.shape, bf16) for piece in pieces]
        ring_scratch = [pltpu.SemaphoreType.DMA for _ in pieces]
    return pl.pallas_call(
        functools.partial(fold_kernel, n, seqs, tensor, backward, count),
        in_specs=[vmem] * (4 + count),
        out_specs=[vmem] * 3 + [vmem if backward else anywhere] * len(made),
        out_shape=[
            jax.ShapeDtypeStruct((seqs, tensor * own_len, width), bf16),
            jax.ShapeDtypeStruct((seqs, own_len, width), f32),
            jax.ShapeDtypeStruct((1, width), f32),
        ]
        + made,
        scratch_shapes=[
            pltpu.VMEM((seqs, 2, own_len, width), bf16),
            pltpu.VMEM((seqs, own_len, width), bf16),
            pltpu.VMEM((seqs, own_len, width), bf16),
            pltpu.VMEM((seqs, own_len, width), f32),
            pltpu.SemaphoreType.DMA((seqs, 2)),
            pltpu.SemaphoreType.DMA((seqs, 2)),
            pltpu.SemaphoreType.DMA((seqs,)),
            pltpu.SemaphoreType.DMA((seqs,)),
            pltpu.SemaphoreType.DMA((seqs, 3)),
            pltpu.SemaphoreType.DMA((seqs, 3)),
            pltpu.SemaphoreType.DMA((count, n, 2 * SUBS)),
            pltpu.SemaphoreType.DMA((count, n, 2 * SUBS)),
        ]
        + ring_scratch,
        compiler_params=pltpu.CompilerParams(
            collective_id=4 if backward else 3, has_side_effects=True, vmem_limit_bytes=VMEM_LIMIT
        ),
        name="fold_back" if backward else "fold",
    )(part, own, gain, hidden, *pieces)


def closing_kernel(
    n, n_seqs, tensor,
    own_ref, tokens_ref, gain_ref, small_ref, *refs,
):
    hbm, refs = refs[:9], refs[9:]
    d_ref, gate_sum, out_sum, qkv_sum, small_sum, gain_sum, shared_ref = refs[:7]
    refs = refs[7:]
    held, refs = refs[:9], refs[9:]
    (
        gate_in, out_in, qkv_in, small_in, gain_in, spare_gate, spare_out, spare_qkv,
        part_ref, near_ref, far_ref, send_ref, total_ref, pass_ref, got_ref,
        load_sem, a_send, a_recv, x_send, x_recv, ring_send, ring_recv, s_send, s_recv,
    ) = refs
    second_ref, gate_ref, back_ref, mix_ref, proj_ref, weight_ref, logit_ref, beta_ref, first_ref = held
    me, t = lax.axis_index("dp"), lax.axis_index("tensor")
    core, cross = swap_pair(t), swap_half(t, tensor)
    both = swap_half(core, tensor)
    own_len = tokens_ref.shape[1]
    length = own_len * tensor
    rows, width = gate_sum.shape[0], gain_ref.shape[1]
    block = gain_sum.shape[1]

    loads = [
        pltpu.make_async_copy(source, target, load_sem.at[i])
        for i, (source, target) in enumerate(zip(hbm, held))
    ]
    for load in loads:
        load.start()

    def gain_part(owner, way):
        at = lax.div(owner * (width // n), block) * block
        return total_ref[pl.ds(way * 16, 16), pl.ds(pl.multiple_of(at, 128), block)]

    def ring(i, count, part, inward, total, lanes=2 * SUBS):
        return RingScatter(n, count, part, inward, total, ring_send.at[i], ring_recv.at[i], lanes)

    gate = ring(0, rows, grad_part(rows, second_ref, gate_ref, spare_gate), gate_in, gate_sum)
    out = ring(1, rows, grad_part(rows, back_ref, mix_ref, spare_out), out_in, out_sum)
    qkv = ring(2, rows, grad_part(rows, first_ref, proj_ref, spare_qkv), qkv_in, qkv_sum)
    small = ring(3, small_ref.shape[1], held_part(small_ref), small_in, small_sum, 2)
    gains = ring(4, 32, gain_part, gain_in, gain_sum, 2)

    barrier = pltpu.get_barrier_semaphore()
    gate.greet(barrier)
    for device in (core, cross):
        pl.semaphore_signal(barrier, inc=1, device_id={"tensor": device}, device_id_type=MESH)
    pl.semaphore_wait(barrier, 4)

    def span(at):
        return pl.ds(pl.multiple_of(at * own_len, own_len), own_len)

    def to_core(s, i):
        return remote(
            part_ref.at[s, span((core, both)[i]), :], near_ref.at[s, i],
            a_send.at[s, i], a_recv.at[s, i], tensor=core,
        )

    def to_cross(s):
        return remote(send_ref.at[s], far_ref.at[s], x_send.at[s], x_recv.at[s], tensor=cross)

    early = (gate, out, small)
    for load in loads[:4]:
        load.wait()
    for chain in early:
        chain.start()
    for load in loads[4:]:
        load.wait()

    def input_grad(s, carry):
        here = pl.ds(pl.multiple_of(s * length, length), length)
        part_ref[s] = (
            dot(proj_ref[here, :], weight_ref[...], 1, 1) + dot(logit_ref[here, :], beta_ref[...], 1, 1)
        ).astype(bf16)
        for i in (1, 0):
            to_core(s, i).start()
        for chain in early:
            chain.advance(2 + s)
        return carry

    lax.fori_loop(0, n_seqs, input_grad, 0)

    def first(s, carry):
        to_core(s, 1).wait_recv()
        send_ref[s] = (
            part_ref[s, span(cross), :].astype(f32) + near_ref[s, 1].astype(f32)
        ).astype(bf16)
        to_cross(s).start()
        return carry

    lax.fori_loop(0, n_seqs, first, 0)
    for chain in early:
        chain.advance(2 + n_seqs)
    total_ref[...] = jnp.zeros_like(total_ref)

    def second(s, carry):
        to_core(s, 0).wait_recv()
        to_cross(s).wait_recv()
        total = (
            part_ref[s, span(t), :].astype(f32) + near_ref[s, 0].astype(f32) + far_ref[s].astype(f32)
        )
        tokens = tokens_ref[s].astype(f32)
        scale = lax.rsqrt(jnp.mean(tokens * tokens, axis=-1, keepdims=True) + epsilon)
        unit = tokens * scale
        total_ref[...] += jnp.sum(total * unit, axis=0, keepdims=True)
        scaled = total * gain_ref[...]
        d_ref[s] = (
            own_ref[s] + scale * (scaled - unit * jnp.mean(scaled * unit, axis=-1, keepdims=True))
        ).astype(bf16)
        return carry

    lax.fori_loop(0, n_seqs, second, 0)

    def rest(hop, carry):
        for chain in early:
            chain.advance(hop)
        return carry

    lax.fori_loop(3 + n_seqs, n, rest, 0)
    qkv.start()
    gains.start()
    for chain in early:
        chain.finish()

    def final(hop, carry):
        for chain in (qkv, gains):
            chain.advance(hop)
        return carry

    lax.fori_loop(2, n, final, 0)
    gains.finish()
    shared_ref[0, :, :] = small_sum[...]
    shared_ref[1, :, :] = jnp.zeros_like(small_sum)
    for c in range(block // 128):
        shared_ref[1, pl.ds(c, 1), :] = gain_sum[pl.ds(0, 1), c * 128 : (c + 1) * 128]
    for i, peer in enumerate((core, cross)):
        pass_ref[i] = shared_ref[...]
        share = remote(pass_ref.at[i], got_ref.at[i], s_send.at[i], s_recv.at[i], tensor=peer)
        share.start()
        share.wait()
        shared_ref[...] += got_ref[i]
    qkv.finish()

    def last(s, carry):
        for i in range(2):
            to_core(s, i).wait_send()
        to_cross(s).wait_send()
        return carry

    lax.fori_loop(0, n_seqs, last, 0)


def closing(own, tokens, gain, small, factors):
    n, tensor = lax.axis_size("dp"), lax.axis_size("tensor")
    seqs, own_len, width = tokens.shape
    rows, block = width // n, max(128, width // n)
    columns = [factors[i].shape[1] for i in (1, 3, 4)]
    vmem, anywhere = pl.BlockSpec(memory_space=pltpu.VMEM), pl.BlockSpec(memory_space=pl.ANY)
    shared = (2,) + small.shape[1:]
    return pl.pallas_call(
        functools.partial(closing_kernel, n, seqs, tensor),
        in_specs=[vmem] * 4 + [anywhere] * 9,
        out_specs=[vmem] * 7,
        out_shape=[jax.ShapeDtypeStruct((seqs, own_len, width), bf16)]
        + [jax.ShapeDtypeStruct((rows, count), f32) for count in columns]
        + [
            jax.ShapeDtypeStruct(small.shape[1:], f32),
            jax.ShapeDtypeStruct((32, block), f32),
            jax.ShapeDtypeStruct(shared, f32),
        ],
        scratch_shapes=[pltpu.VMEM(factor.shape, bf16) for factor in factors]
        + [pltpu.VMEM((n, rows, count), bf16) for count in columns]
        + [pltpu.VMEM(small.shape, bf16), pltpu.VMEM((n, 32, block), bf16)]
        + [spare(rows, count) for count in columns]
        + [
            pltpu.VMEM((seqs, own_len * tensor, width), bf16),
            pltpu.VMEM((seqs, 2, own_len, width), bf16),
            pltpu.VMEM((seqs, own_len, width), bf16),
            pltpu.VMEM((seqs, own_len, width), bf16),
            pltpu.VMEM((32, width), f32),
            pltpu.VMEM((2,) + shared, f32),
            pltpu.VMEM((2,) + shared, f32),
            pltpu.SemaphoreType.DMA((9,)),
            pltpu.SemaphoreType.DMA((seqs, 2)),
            pltpu.SemaphoreType.DMA((seqs, 2)),
            pltpu.SemaphoreType.DMA((seqs,)),
            pltpu.SemaphoreType.DMA((seqs,)),
            pltpu.SemaphoreType.DMA((5, n, 2 * SUBS)),
            pltpu.SemaphoreType.DMA((5, n, 2 * SUBS)),
            pltpu.SemaphoreType.DMA((2,)),
            pltpu.SemaphoreType.DMA((2,)),
        ],
        compiler_params=pltpu.CompilerParams(
            collective_id=5, has_side_effects=True, vmem_limit_bytes=63 * 1024 * 1024
        ),
        name="closing",
    )(own, tokens, gain, small, *factors)


def rms_unit(values):
    scale = lax.rsqrt(jnp.mean(values * values, axis=-1, keepdims=True) + epsilon)
    return values * scale, scale


def rms_back(back, unit, scale, gain):
    scaled = back * gain
    return scale * (scaled - unit * jnp.mean(scaled * unit, axis=-1, keepdims=True))


def flat(array):
    return array.reshape(-1, array.shape[-1])


def matmul(spec, left, right):
    return jnp.einsum(spec, left, right, preferred_element_type=f32)


def swap(block, axis, half):
    count = lax.axis_size(axis)
    route = [(i, (i + count // 2) % count if half else i ^ 1) for i in range(count)]
    return lax.ppermute(block, axis, route)


def tensor_scatter(part):
    tensor, t = lax.axis_size("tensor"), lax.axis_index("tensor")
    seqs, rows, width = part.shape
    chunks = part.reshape(seqs, tensor, rows // tensor, width)

    def chunk(at):
        return lax.dynamic_index_in_dim(chunks, at, 1, keepdims=False)

    core, cross = swap_pair(t), swap_half(t, tensor)
    both = swap_half(core, tensor)
    near_own, near_cross = swap(chunk(core), "tensor", False), swap(chunk(both), "tensor", False)
    far = swap((chunk(cross).astype(f32) + near_cross.astype(f32)).astype(bf16), "tensor", True)
    return chunk(t).astype(f32) + near_own.astype(f32) + far.astype(f32)


def shards(
    tokens,
    cotangent,
    query_weight,
    key_weight,
    value_weight,
    beta_weight,
    conv_filter,
    norm_gain,
    head_gain,
    out_weight,
    gate_weight,
    up_weight,
    down_weight,
):
    n = lax.axis_size("dp")
    tensor = lax.axis_size("tensor")
    seqs, own_len, width = tokens.shape
    local = query_weight.shape[1]
    heads = local // HD
    hidden = gate_weight.shape[1]

    packed = jnp.concatenate(
        [conv_filter.reshape(-1), norm_gain.reshape(-1), head_gain, beta_weight.reshape(-1)]
    )
    block = -(-packed.size // 4096) * 4096
    small = jnp.pad(packed, (0, block - packed.size)).reshape(-1, 128)
    full_qkv, full_small, extended, rows_cotangent, full_out = opening(
        query_weight, key_weight, value_weight, small, tokens, cotangent, out_weight.T
    )
    full_out = full_out.reshape(width, local)
    full_qkv = full_qkv.reshape(width, 3 * local)
    full_small = full_small.reshape(n, block)
    sizes = [conv_filter.size, norm_gain.size, head_gain.size, beta_weight.size]
    ends = [sum(sizes[: i + 1]) for i in range(4)]
    filters = (
        full_small[:, : ends[0]]
        .reshape(n, 3 * KCONV, heads, HD // n)
        .transpose(1, 2, 0, 3)
        .reshape(3 * KCONV, local)
        .astype(f32)
    )
    gains = (
        full_small[:, ends[0] : ends[1]].reshape(n, 2, width // n).transpose(1, 0, 2).reshape(2, width)
    ).astype(f32)
    head_row = full_small[:, ends[1] : ends[2]].reshape(1, HD).astype(f32)
    full_beta = full_small[:, ends[2] : ends[3]].reshape(width, heads)

    unit_ext, _ = rms_unit(extended.astype(f32))
    normed_ext = (unit_ext * gains[0]).astype(bf16)
    normed_first = normed_ext[:, RIM:]
    projected = matmul("std,dm->stm", normed_ext, full_qkv).astype(bf16)
    strength = jax.nn.sigmoid(matmul("std,dh->sth", normed_first, full_beta))
    normed_mix, mix, carry, inverse, kw, state, full_gate = mixer(
        projected, strength, filters, head_row, gate_weight
    )
    full_gate = full_gate.reshape(width, hidden)

    branch_part = matmul("stk,dk->std", normed_mix, full_out).astype(bf16)
    normed_second, hidden_state, _, full_up, full_down = fold(
        branch_part, tokens, gains[1:2], [up_weight, down_weight.T]
    )
    full_up, full_down = full_up.reshape(width, hidden), full_down.reshape(width, hidden)
    gate_pre = matmul("std,df->stf", normed_second, full_gate)
    up_pre = matmul("std,df->stf", normed_second, full_up)
    gate_sigmoid = jax.nn.sigmoid(gate_pre)
    ffn_hidden = (gate_pre * gate_sigmoid * up_pre).astype(bf16)

    back_hidden = matmul("std,df->stf", rows_cotangent, full_down)
    back_gate = (
        back_hidden * up_pre * gate_sigmoid * (1.0 + gate_pre * (1.0 - gate_sigmoid))
    ).astype(bf16)
    back_up = (back_hidden * gate_pre * gate_sigmoid).astype(bf16)
    back_second = matmul("stf,df->std", back_gate, full_gate) + matmul("stf,df->std", back_up, full_up)
    rows_back, back_state, gain_second, grad_down = fold(
        back_second.astype(bf16), cotangent, gains[1:2],
        [flat(rows_cotangent), flat(ffn_hidden)], hidden_state,
    )
    rows_back, back_up, ffn_hidden = lax.optimization_barrier((rows_back, back_up, ffn_hidden))
    grad_up = matmul("std,stf->df", normed_second, back_up)
    ffn_part = matmul("stf,df->std", ffn_hidden, full_down).astype(bf16)
    layer_out = (hidden_state + tensor_scatter(ffn_part)).astype(bf16)
    back_normed = matmul("std,dk->stk", rows_back, full_out)
    back_proj, back_logit, conv_part, head_part = mixer_back(
        projected, strength, filters, head_row, back_normed, mix, carry, inverse, kw, state
    )
    back_logit = back_logit.astype(bf16)
    grad_beta = matmul("std,sth->dh", normed_first, back_logit)
    grad_conv = conv_part.transpose(1, 0, 2).reshape(3 * KCONV, local)
    gain_grads = jnp.concatenate([jnp.zeros_like(gain_second), gain_second])
    small_grads = jnp.concatenate(
        [
            grad_conv.reshape(3 * KCONV, heads, n, HD // n).transpose(2, 0, 1, 3).reshape(n, -1),
            gain_grads.reshape(2, n, width // n).transpose(1, 0, 2).reshape(n, -1),
            head_part[0].reshape(n, HD // n),
            grad_beta.reshape(n, -1),
        ],
        axis=1,
    )
    small_grads = jnp.pad(small_grads, ((0, 0), (0, block - small_grads.shape[1])))
    lanes = ((0, 0), (0, 128 - heads))
    d_tokens, grad_gate, grad_out, grad_qkv, small_grads, _, shared = closing(
        back_state, tokens, gains[0:1], small_grads.astype(bf16).reshape(n, -1, 128),
        [
            flat(normed_second), flat(back_gate), flat(rows_back), flat(normed_mix), flat(back_proj),
            full_qkv, jnp.pad(flat(back_logit), lanes), jnp.pad(full_beta, lanes), flat(normed_first),
        ],
    )
    gain_row = shared[1, : max(1, width // n // 128)].reshape(-1)
    if width // n < 128:
        start = lax.rem(lax.axis_index("dp") * (width // n), 128)
        gain_row = lax.dynamic_slice_in_dim(gain_row, start, width // n)
    shared = shared[0]
    small_grads, shared = small_grads.reshape(-1), shared.reshape(-1)

    def scatter(grad):
        return lax.psum_scatter(grad.astype(bf16), "dp", scatter_dimension=0, tiled=True).astype(f32)

    grad_up = scatter(grad_up)
    return (
        layer_out,
        d_tokens,
        grad_qkv[:, :local],
        grad_qkv[:, local : 2 * local],
        grad_qkv[:, 2 * local :],
        small_grads[ends[2] : ends[3]].reshape(beta_weight.shape),
        small_grads[: ends[0]].reshape(conv_filter.shape),
        jnp.stack([gain_row, shared[ends[0] + width // n : ends[1]]]),
        shared[ends[1] : ends[2]],
        grad_out.T,
        grad_gate,
        grad_up,
        grad_down.T,
    )


def solution(mesh):
    both = P(None, ("dp", "tensor"), None)
    rows, cols = P("dp", "tensor"), P("tensor", "dp")
    conv, gain, head = P(None, "tensor", "dp"), P(None, "dp"), P("dp")
    return jax.shard_map(
        shards,
        mesh=mesh,
        in_specs=(both, both, rows, rows, rows, rows, conv, gain, head, cols, rows, rows, cols),
        out_specs=(both, both, rows, rows, rows, rows, conv, gain, head, cols, rows, rows, cols),
        check_vma=False,
    )
```

time: 852 us -> 797 us (0.935)
  Pallas kernels: 504 us -> 615 us
  waiting for transfers between devices: 82.6 us -> 0.03 us
  matrix products: 157 us -> 95.9 us
  other arithmetic: 29.8 us -> 18.4 us
  starting transfers between devices: 13.5 us -> 2.56 us
    pallas_call x4, Pallas kernels: 271 us -> 374 us  [the longest x2 211 us: fold(): pl.pallas_call(functools.partial(fold_kernel, n, seqs, tensor, backward,...]
    all_gather x4 -> x0, waiting for transfers between devices: 81.3 us -> none  [the longest x1 81.2 us: shards(): full_gate = lax.all_gather(gate_weight, 'dp', axis=0, tiled=True)]
    dot_general x18 -> x12, matrix products: 157 us -> 95.9 us  [matmul(): return jnp.einsum(spec, left, right, preferred_element_type=f32)]
    pallas_call x1, Pallas kernels: 124 us -> 152 us  [closing(): pl.pallas_call(functools.partial(closing_kernel, n, seqs, tensor), in_spe...]
    pallas_call x1, Pallas kernels: 109 us -> 88.7 us  [opening(): pl.pallas_call(functools.partial(opening_kernel, n, tensor), in_specs=[vm...]
    concatenate x1, local copies, waits for them, and re-layouts: 12.3 us -> 0.02 us  [shards(): gain_grads = jnp.concatenate([jnp.zeros_like(gain_second), gain_second])]
    ppermute x8 -> x0, starting transfers between devices: 10.7 us -> none  [the longest x7 9.28 us: direct_scatter(): lax.ppermute(block, 'dp', [(i, (i + step) % n) for i in range(n)])]
    slice x5 -> x6, local copies, waits for them, and re-layouts: 0.73 us -> 10 us  [the longest x1 4.9 us: shards(): normed_first = normed_ext[:, RIM:]]
  transfers between devices with their start and end apart: 20 -> 4, of which waited for: 1 -> 0; matrix products, arithmetic and copies ran while one was open for 23% -> 6% of each run, Pallas kernels for 60% -> 31%
where the time goes in v3:
time: 797 us; the launch traced here: 789 us
  Pallas kernels  615 us (77%)
  matrix products  95.9 us (12%)
  local copies, waits for them, and re-layouts  42.2 us (5%)
  other arithmetic  18.4 us (2%)
  between operations  14.9 us (2%)
    pallas_call x2, Pallas kernels, fold(): pl.pallas_call(functools.partial(fold_kernel, n, seqs, tensor, backward,...  211 us
    pallas_call x1, Pallas kernels, closing(): pl.pallas_call(functools.partial(closing_kernel, n, seqs, tensor), in_spe...  152 us
    dot_general x12, matrix products, matmul(): return jnp.einsum(spec, left, right, preferred_element_type=f32)  95.9 us
    pallas_call x1, Pallas kernels, mixer_back(): pl.pallas_call(functools.partial(mixer_back_kernel, n, rows, steps, pairs...  90.9 us
    pallas_call x1, Pallas kernels, opening(): pl.pallas_call(functools.partial(opening_kernel, n, tensor), in_specs=[vm...  88.7 us
    pallas_call x1, Pallas kernels, mixer(): pl.pallas_call(functools.partial(mixer_kernel, n, rows, steps, pairs, lim...  71.9 us
    unnamed x61, local copies, waits for them, and re-layouts  20 us
  transfers between devices with their start and end apart: 4, of which 0 were waited for; matrix products, arithmetic and copies ran while one was open for 6% of the time, Pallas kernels for 31%

profile of v3, /device:TPU:0, one launch (start us, length us, event | category | flops | bytes accessed | tf_op | source)
XLA Modules:
  0.0 788.7 jit_solution(11521556129416100791)
XLA Ops:
  12.8 88.7 %opening.1 = (bf16[8,256,1536]{2,1,0:T(8,128)(2,1)}, bf16[8,32,128]{2,1,0:T(8,128)(2,1)}, bf16[4,264,2048]{2,1,0:T(8,128)(2,1)}, bf16[4,256,2048]{2,1,0:T(8,128)(2,1)}, bf16[8,256,512]{2,1,0:T(8,128)(2,1)}) custom-call(bf16[256,512]{1,0:T(8,128)(2,1)} %q_ref.1, bf16[256,512]{1,0:T(8,128)(2,1)} %k_ref.1, bf16[256,512]{1,0:T(8,128)(2,1)} %v_ref.1, ...), custom_call_target="tpu_custom_call" | custom-call | tf_op jit(solution)/shard_map/opening/pallas_call | solution.py:934
  102.5 3.3 fusion
  107.0 3.4 fusion.2
  110.4 8.6 %convolution_convert_fusion.pq_ref.pk_ref.pv_ref = bf16[4,264,1536]{2,1,0:T(8,128)(2,1)} fusion(bf16[4,264,2048]{2,1,0:T(8,128)(2,1)S(1)} %fusion.2, bf16[2048,1536,1]{1,0,2:T(8,128)(2,1)S(1)} %bitcast.122), kind=kOutput, calls=%fused_computation.11 | convolution fusion | flops 6645399552 | bytes 13860864 | tf_op jit(solution)/shard_map/std,dm->stm/dot_general | solution.py:1371
  124.5 71.9 %mixer.1 = (bf16[4,256,512]{2,1,0:T(8,128)(2,1)}, f32[8,2,256,128]{3,2,1,0:T(8,128)}, f32[8,2,256,128]{3,2,1,0:T(8,128)}, f32[16,256,256]{2,1,0:T(8,128)}, f32[8...) custom-call(bf16[4,264,1536]{2,1,0:T(8,128)(2,1)} %convolution_convert_fusion.pq_ref.pk_ref.pv, ...), custom_call_target="tpu_custom_call" | custom-call | tf_op jit(solution)/shard_map/mixer/pallas_call | solution.py:470
  196.4 5.7 convolution_convert_fusion.2.part_ref
  202.7 127.8 %fold.1 = (bf16[4,256,2048]{2,1,0:T(8,128)(2,1)}, f32[4,64,2048]{2,1,0:T(8,128)}, f32[1,2048]{1,0:T(1,128)}, bf16[8,256,1408]{2,1,0:T(8,128)(2,1)}, bf16[8,256,1408]{2,1,0:T(8,128)(2,1)}) custom-call(bf16[4,256,2048]{2,1,0:T(8,128)(2,1)} %convolution_convert_fusion.2.part_ref, bf16[4,64,2048]{2,1,0:T(8,128)(2,1)} %tokens_ref.3, f32[1,2048]{1,0:T(1,128)} %bitcast.145, ...), custom_call_target="tpu_custom_call" | custom-call | tf_op jit(solution)/shard_map/fold/pallas_call | solution.py:1126
  330.5 11.8 %fusion.17 = f32[4,256,1408]{2,1,0:T(8,128)} fusion(bf16[4,256,2048]{2,1,0:T(8,128)(2,1)} %get-tuple-element.54, bf16[2048,1408,1]{1,0,2:T(8,128)(2,1)} %bitcast.159), kind=kOutput, calls=%fused_computation.51 | convolution fusion | flops 5905580032 | bytes 15728640 | tf_op jit(solution)/shard_map/std,df->stf/dot_general | solution.py:1371
  342.4 8.4 %fusion.16 = f32[4,256,1408]{2,1,0:T(8,128)} fusion(bf16[4,256,2048]{2,1,0:T(8,128)(2,1)S(1)} %copy-done.2, bf16[2048,1408,1]{1,0,2:T(8,128)(2,1)S(1)} %bitcast.158), kind=kOutput, calls=%fused_computation.50 | convolution fusion | flops 5905580032 | bytes 15728640 | tf_op jit(solution)/shard_map/std,df->stf/dot_general | solution.py:1371
  350.8 13.1 %multiply_convert_fusion = (bf16[4,256,1408]{2,1,0:T(8,128)(2,1)}, bf16[4,256,1408]{2,1,0:T(8,128)(2,1)S(1)}, bf16[4,256,1408]{2,1,0:T(8,128)(2,1)}) fusion(f32[4,256,1408]{2,1,0:T(8,128)} %fusion.17, f32[4,256,1408]{2,1,0:T(8,128)} %fusion.16, bf16[4,256,2048]{2,1,0:T(8,128)(2,1)S(1)} %copy-done.4, bf16[2048,1408,1]{1,0,2:T(8,128)(2,1)S(1)} %bitcast.165), kind=kOutput, calls=%fused_computation.7 | convolution fusion | flops 5928648704 | bytes 30146560 | tf_op jit(solution)/shard_map/std,df->stf/dot_general | solution.py:1371
  364.0 9.4 %fusion.18 = f32[4,256,2048]{2,1,0:T(8,128)} fusion(bf16[4,256,1408]{2,1,0:T(8,128)(2,1)S(1)} %get-tuple-element.132, bf16[2048,1408,1]{1,0,2:T(8,128)(2,1)S(1)} %bitcast.162), kind=kOutput, calls=%fused_computation.52 | convolution fusion | flops 5905580032 | bytes 17039360 | tf_op jit(solution)/shard_map/stf,df->std/dot_general | solution.py:1371
  373.4 10.5 %add_convert_fusion.part_ref = bf16[4,256,2048]{2,1,0:T(8,128)(2,1)} fusion(f32[4,256,2048]{2,1,0:T(8,128)} %fusion.18, bf16[4,256,1408]{2,1,0:T(8,128)(2,1)S(1)} %copy-done.14, bf16[2048,1408,1]{1,0,2:T(8,128)(2,1)S(1)} %bitcast.166), kind=kOutput, calls=%fused_computation.6 | convolution fusion | flops 5909774336 | bytes 21233664 | tf_op jit(solution)/shard_map/stf,df->std/dot_general | solution.py:1371
  383.9 83.1 %fold_back.1 = (bf16[4,256,2048]{2,1,0:T(8,128)(2,1)}, f32[4,64,2048]{2,1,0:T(8,128)}, f32[1,2048]{1,0:T(1,128)}, f32[256,1408]{1,0:T(8,128)}) custom-call(bf16[4,256,2048]{2,1,0:T(8,128)(2,1)} %add_convert_fusion.part_ref, bf16[4,64,2048]{2,1,0:T(8,128)(2,1)} %own_ref.5, f32[1,2048]{1,0:T(1,128)} %bitcast.146, f32[4,64,2048]{2,1,0:T(8,128)} %get-tuple-element.51.hidden_ref, ...), custom_call_target="tpu_custom_call" | custom-call | tf_op jit(solution)/shard_map/fold_back/pallas_call | solution.py:1126
  467.0 11.0 %bitcast_convert_fusion = bf16[2048,1408]{1,0:T(8,128)(2,1)} fusion(bf16[4,256,2048]{2,1,0:T(8,128)(2,1)} %get-tuple-element.54, bf16[4,256,1408]{2,1,0:T(8,128)(2,1)S(1)} %copy-done.15), kind=kOutput, calls=%fused_computation | convolution fusion | flops 5908463616 | bytes 12845056 | tf_op jit(solution)/shard_map/std,stf->df/dot_general | solution.py:1371
  479.8 8.7 %convolution_convert_fusion.1 = bf16[4,256,2048]{2,1,0:T(8,128)(2,1)S(1)} fusion(bf16[4,256,1408]{2,1,0:T(8,128)(2,1)S(1)} %copy-done.7, bf16[2048,1408,1]{1,0,2:T(8,128)(2,1)} %bitcast.157), kind=kOutput, calls=%fused_computation.12 | convolution fusion | flops 5907677184 | bytes 12845056 | tf_op jit(solution)/shard_map/stf,df->std/dot_general | solution.py:1371
  492.2 4.9 slice.88
  497.7 3.7 fusion.19.back_ref
  501.3 90.9 %mixer_back.1 = (bf16[4,256,1536]{2,1,0:T(8,128)(2,1)}, f32[4,256,4]{2,1,0:T(8,128)}, f32[2,12,256]{2,1,0:T(8,128)}, f32[8,128]{1,0:T(8,128)}) custom-call(bf16[4,264,1536]{2,1,0:T(8,128)(2,1)} %convolution_convert_fusion.pq_ref.pk_ref.pv_ref, bf16[4,264,1536]{2,1,0:T(8,128)(2,1)} %convolution_convert_fusion.pq_ref.pk_ref.pv_ref, ...), custom_call_target="tpu_custom_call" | custom-call | tf_op jit(solution)/shard_map/mixer_back/pallas_call | solution.py:733
  596.0 2.9 fusion.3
  598.9 2.6 fusion.4
  606.3 152.3 %closing.1 = (bf16[4,64,2048]{2,1,0:T(8,128)(2,1)}, f32[256,1408]{1,0:T(8,128)}, f32[256,512]{1,0:T(8,128)}, f32[256,1536]{1,0:T(8,128)}, f32[32,128]{1,0:T(8,12...) custom-call(f32[4,64,2048]{2,1,0:T(8,128)} %get-tuple-element.59.own_ref, bf16[4,64,2048]{2,1,0:T(8,128)(2,1)} %tokens_ref.3, ...), custom_call_target="tpu_custom_call" | custom-call | tf_op jit(solution)/shard_map/closing/pallas_call | solution.py:1316
  765.4 2.9 copy.84
  769.6 2.5 fusion.14
  772.1 3.6 fusion.7
  (115 shorter events, 42.0 us)
Async XLA Ops:
  7.2 768.5 %reduce-scatter.2.cloned.1.call-start = ((), (), s32[]{:S(2)}) async-start(), calls=%async_computation.1 | async-start | bytes 6488064 | tf_op jit(solution)/shard_map/reduce_scatter | solution.py:1511
  102.5 7.9 %slice-start = ((s8[6291456]{0:T(1024)(128)(4,1)}), s8[2097152]{0:T(1024)(128)(4,1)S(1)}, s32[]{:S(2)}) async-start(s8[6291456]{0:T(1024)(128)(4,1)} %bitcast.120), calls=%async_computation.2 | async-start | bytes 4194304
  107.0 3.5 slice-start.1
  110.4 8.7 %copy-start = (bf16[4,264,2048]{2,1,0:T(8,128)(2,1)}, bf16[4,264,2048]{2,1,0:T(8,128)(2,1)S(1)}, u32[]{:S(2)}) copy-start(bf16[4,264,2048]{2,1,0:T(8,128)(2,1)S(1)} %fusion.2) | copy-start | bytes 12976132
  119.1 4.3 copy-start.9
  124.5 71.9 %copy-start.12 = (bf16[8,256,512]{2,1,0:T(8,128)(2,1)S(1)}, bf16[8,256,512]{2,1,0:T(8,128)(2,1)}, u32[]{:S(2)}) copy-start(bf16[8,256,512]{2,1,0:T(8,128)(2,1)} %get-tuple-element.50) | copy-start | bytes 6291460
  330.5 11.9 %copy-start.2 = (bf16[4,256,2048]{2,1,0:T(8,128)(2,1)S(1)}, bf16[4,256,2048]{2,1,0:T(8,128)(2,1)}, u32[]{:S(2)}) copy-start(bf16[4,256,2048]{2,1,0:T(8,128)(2,1)} %get-tuple-element.52) | copy-start | bytes 12582916
  330.5 11.8 %copy-start.11 = (bf16[8,256,1408]{2,1,0:T(8,128)(2,1)S(1)}, bf16[8,256,1408]{2,1,0:T(8,128)(2,1)}, u32[]{:S(2)}) copy-start(bf16[8,256,1408]{2,1,0:T(8,128)(2,1)} %get-tuple-element.53) | copy-start | bytes 17301508
  330.5 20.3 %slice-start.4 = ((s8[5767168]{0:T(1024)(128)(4,1)}), s8[4194304]{0:T(1024)(128)(4,1)S(1)}, s32[]{:S(2)}) async-start(s8[5767168]{0:T(1024)(128)(4,1)} %bitcast.163), calls=%async_computation.6 | async-start | bytes 8388608
  342.3 8.5 %slice-start.5 = ((s8[5767168]{0:T(1024)(128)(4,1)}), s8[1572864]{0:T(1024)(128)(4,1)S(1)}, s32[]{:S(2)}) async-start(s8[5767168]{0:T(1024)(128)(4,1)} %bitcast.163), calls=%async_computation.7 | async-start | bytes 3145728
  342.3 8.4 %copy-start.4 = (bf16[4,256,2048]{2,1,0:T(8,128)(2,1)S(1)}, bf16[4,256,2048]{2,1,0:T(8,128)(2,1)}, u32[]{:S(2)}) copy-start(bf16[4,256,2048]{2,1,0:T(8,128)(2,1)} %get-tuple-element.54) | copy-start | bytes 12582916
  342.3 21.6 %slice-start.2 = ((s8[5767168]{0:T(1024)(128)(4,1)}), s8[4194304]{0:T(1024)(128)(4,1)S(1)}, s32[]{:S(2)}) async-start(s8[5767168]{0:T(1024)(128)(4,1)} %bitcast.160), calls=%async_computation.4 | async-start | bytes 8388608
  350.8 13.1 %slice-start.3 = ((s8[5767168]{0:T(1024)(128)(4,1)}), s8[1572864]{0:T(1024)(128)(4,1)S(1)}, s32[]{:S(2)}) async-start(s8[5767168]{0:T(1024)(128)(4,1)} %bitcast.160), calls=%async_computation.5 | async-start | bytes 3145728
  363.9 9.5 %copy-start.6 = (bf16[4,256,1408]{2,1,0:T(8,128)(2,1)}, bf16[4,256,1408]{2,1,0:T(8,128)(2,1)S(1)}, u32[]{:S(2)}) copy-start(bf16[4,256,1408]{2,1,0:T(8,128)(2,1)S(1)} %get-tuple-element.132) | copy-start | bytes 8650756
  364.0 9.4 %copy-start.14 = (bf16[4,256,1408]{2,1,0:T(8,128)(2,1)S(1)}, bf16[4,256,1408]{2,1,0:T(8,128)(2,1)}, u32[]{:S(2)}) copy-start(bf16[4,256,1408]{2,1,0:T(8,128)(2,1)} %get-tuple-element.77) | copy-start | bytes 8650756
  383.9 83.1 %copy-start.15 = (bf16[4,256,1408]{2,1,0:T(8,128)(2,1)S(1)}, bf16[4,256,1408]{2,1,0:T(8,128)(2,1)}, u32[]{:S(2)}) copy-start(bf16[4,256,1408]{2,1,0:T(8,128)(2,1)} %get-tuple-element.77) | copy-start | bytes 8650756
  491.6 107.3 %collective-permute-start.1 = (bf16[4,64,2048]{2,1,0:T(8,128)(2,1)S(1)}, bf16[4,64,2048]{2,1,0:T(8,128)(2,1)S(1)}, u32[]{:S(2)}, u32[]{:S(2)}) collective-permute-start(bf16[4,64,2048]{2,1,0:T(8,128)(2,1)S(1)} %get-tuple-element.135), channel_id=1, source_target_pairs={{0,1},{1,0},{2,3},{3,2},{4,5},{5,4},{6,7},{7,6},{8,9},{9,8},{10,11... | collective-permute-start | bytes 3145736 | tf_op jit(solution)/shard_map/ppermute | solution.py:1377
  491.6 280.5 %collective-permute-start = (bf16[4,64,2048]{2,1,0:T(8,128)(2,1)}, bf16[4,64,2048]{2,1,0:T(8,128)(2,1)}, u32[]{:S(2)}, u32[]{:S(2)}) collective-permute-start(bf16[4,64,2048]{2,1,0:T(8,128)(2,1)} %get-tuple-element.134), channel_id=1, source_target_pairs={{0,1},{1,0},{2,3},{3,2},{4,5},{5,4},{6,7},{7,6},{8,9},{9,8},{10,11... | collective-permute-start | bytes 3145736 | tf_op jit(solution)/shard_map/ppermute | solution.py:1377
  492.1 5.5 copy-start.5
  492.1 5.5 copy-start.13
  501.3 92.0 %copy-start.10 = (f32[1,2048]{1,0:T(1,128)S(1)}, f32[1,2048]{1,0:T(1,128)}, u32[]{:S(2)}) copy-start(f32[1,2048]{1,0:T(1,128)} %get-tuple-element.67) | copy-start | bytes 24580
  601.5 170.6 %collective-permute-start.2 = (bf16[4,64,2048]{2,1,0:T(8,128)(2,1)}, bf16[4,64,2048]{2,1,0:T(8,128)(2,1)}, u32[]{:S(2)}, u32[]{:S(2)}) collective-permute-start(bf16[4,64,2048]{2,1,0:T(8,128)(2,1)} %fusion.4), channel_id=1, source_target_pairs={{0,2},{1,3},{2,0},{3,1},{4,6},{5,7},{6,4},{7,5},{8,10},{9,11},{10,... | collective-permute-start | bytes 3145736 | tf_op jit(solution)/shard_map/ppermute | solution.py:1377
  758.7 13.5 %copy-start.1 = (f32[4,64,2048]{2,1,0:T(8,128)S(1)}, f32[4,64,2048]{2,1,0:T(8,128)}, u32[]{:S(2)}) copy-start(f32[4,64,2048]{2,1,0:T(8,128)} %get-tuple-element.51.hidden_ref) | copy-start | bytes 6291460
  772.1 8.2 %copy-start.8 = (f32[256,1408]{1,0:T(8,128)S(1)}, f32[256,1408]{1,0:T(8,128)}, u32[]{:S(2)}) copy-start(f32[256,1408]{1,0:T(8,128)} %get-tuple-element.167) | copy-start | bytes 4325380
  (2 other events, 3.8 us)
Sparse Core Ops, SparseCore 0:
  478.2 121.8 reduce-scatter.1

commit v4 on v3

--- a/solution.py
+++ b/solution.py
@@ -105,12 +105,8 @@
         for lane in self.lanes:
             self.first(lane).start()
 
-    def resume(self, hop):
-        for lane in self.lanes:
-            self.later(hop, lane).start()
-
-    def advance(self, hop):
-        for lane in self.lanes:
+    def advance(self, hop, lanes=None):
+        for lane in self.lanes if lanes is None else lanes:
             self.later(hop - 1, lane).wait_recv()
             self.later(hop, lane).start()
 
@@ -161,8 +157,21 @@
 
     def advance(self, hop):
         for lane, value in self.ways(lambda way: self.part(self.owner(hop, way), way)):
-            self.inward[hop - 1, self.strip(lane), :] = self.summed(hop - 1, lane, value).astype(bf16)
-            self.sender(hop, lane).start()
+            self.forward(hop, lane, value)
+
+    def advance_first(self, hop, kept):
+        for way in range(2):
+            value = self.part(self.owner(hop, way), way)
+            kept[way] = value[self.slab :]
+            self.forward(hop, way, value[: self.slab])
+
+    def advance_second(self, hop, kept):
+        for way in range(2):
+            self.forward(hop, 2 + way, kept[way])
+
+    def forward(self, hop, lane, value):
+        self.inward[hop - 1, self.strip(lane), :] = self.summed(hop - 1, lane, value).astype(bf16)
+        self.sender(hop, lane).start()
 
     def finish(self):
         for lane, value in self.ways(lambda way: self.part(self.me, way)):
@@ -322,7 +331,7 @@
 
             @pl.when(at < n)
             def _():
-                ring.advance(at)
+                ring.advance(at, range(2) if each == 1 else None)
 
     @pl.when(step < steps)
     def _():
@@ -401,17 +410,23 @@
             kw_ref[step, h] = kwu[:, :HD]
             end_ref[step, h] = kwu[:, HD:]
 
+    if each == 1:
+        @pl.when((step > 0) & (step + 1 < n))
+        def _():
+            ring.advance(step + 1, range(2, 2 * SUBS))
+
     at = step - lag
 
     @pl.when((at >= 0) & (at < steps))
     def _():
+        kws = [halves(kw_ref[at, h]) for h in range(PAIR)]
         for h in range(PAIR):
             @pl.when(me > 0)
             def _():
                 hop(at, h).wait_recv()
 
             state = recv_ref[at, h]
-            out_state = end_ref[at, h] + state.astype(f32) - short_product(halves(kw_ref[at, h]), state)
+            out_state = end_ref[at, h] + state.astype(f32) - short_product(kws[h], state)
             send_ref[at, h] = out_state.astype(bf16)
 
             @pl.when(me < n - 1)
@@ -515,18 +530,140 @@
     )(projected, projected, projected, strength, filters, gain, weight)
 
 
-def mixer_back_kernel(
+def state_back_kernel(
     n, rows, steps, pairs,
-    pq_ref, pk_ref, pv_ref, strength_ref, filt_ref, gain_ref,
-    back_ref, mix_ref, carry_ref, inv_ref, kw_ref, state_ref,
-    proj_ref, logit_ref, conv_ref, head_ref,
-    xq_ref, xk_ref, xv_ref, bc_ref, high_ref, low_ref, recv_ref, send_ref, last_ref, rim_ref, next_ref,
-    send_sem, recv_sem, rim_send, rim_recv,
+    rows_ref, weight_ref, gain_ref, mix_ref, carry_ref, kw_ref,
+    high_ref, low_ref, end_ref, head_ref,
+    recv_ref, send_ref, send_sem, recv_sem,
 ):
     me = lax.axis_index("dp")
     step = pl.program_id(0)
+
+    def hop(at, h):
+        return remote(
+            send_ref.at[at, h], recv_ref.at[at, h], send_sem.at[at, h], recv_sem.at[at, h],
+            dp=lax.rem(me + n - 1, n),
+        )
+
+    @pl.when(step == 0)
+    def _():
+        barrier = pltpu.get_barrier_semaphore()
+
+        @pl.when(me < n - 1)
+        def _():
+            pl.semaphore_signal(barrier, inc=1, device_id={"dp": lax.rem(me + 1, n)}, device_id_type=MESH)
+
+        @pl.when(me == n - 1)
+        def _():
+            recv_ref[...] = jnp.zeros_like(recv_ref)
+
+        @pl.when(me > 0)
+        def _():
+            pl.semaphore_wait(barrier, 1)
+
+        head_ref[...] = jnp.zeros_like(head_ref)
+
+    back_normed = dot(rows_ref[0], weight_ref[...])
+    adds = []
+    head_sum = jnp.zeros((1, HD), f32)
+    for h in range(PAIR):
+        mix, back = mix_ref[0, h], back_normed[:, h * HD : (h + 1) * HD]
+        scale = lax.rsqrt(jnp.mean(mix * mix, axis=-1, keepdims=True) + epsilon)
+        unit = mix * scale
+        head_sum = head_sum + jnp.sum(back * unit, axis=0, keepdims=True)
+        scaled = back * gain_ref[...]
+        out = halves(scale * (scaled - unit * jnp.mean(scaled * unit, axis=-1, keepdims=True)))
+        high_ref[0, h], low_ref[0, h] = out
+        adds.append(narrow_product(halves(carry_ref[0, h]), out, 0))
+    head_ref[...] += jnp.where(
+        lax.broadcasted_iota(jnp.int32, head_ref.shape, 0) == 0, head_sum, 0.0
+    )
+    kws = [halves(kw_ref[0, h].T) for h in range(PAIR)]
+    for h in range(PAIR):
+        @pl.when(me < n - 1)
+        def _():
+            hop(step, h).wait_recv()
+
+        end = recv_ref[step, h]
+        before = adds[h] + end.astype(f32) - short_product(kws[h], end)
+        send_ref[step, h] = before.astype(bf16)
+
+        @pl.when(me > 0)
+        def _():
+            hop(step, h).start()
+
+        end_ref[0, h] = end
+
+    @pl.when((step == steps - 1) & (me > 0))
+    def _():
+        def done(at, carry):
+            for h in range(PAIR):
+                hop(at, h).wait_send()
+            return carry
+
+        lax.fori_loop(0, steps, done, 0)
+
+
+def state_back(rows_back, out_weight, gain, mix, carry, kw):
+    n = lax.axis_size("dp")
+    seqs, rows, width = rows_back.shape
+    steps = mix.shape[0]
+    pairs = steps // seqs
+    wide = PAIR * HD
+
+    def tall(size):
+        return pl.BlockSpec((1, PAIR, size, HD), lambda i: (i, 0, 0, 0))
+
+    def shape(size):
+        return jax.ShapeDtypeStruct((steps, PAIR, size, HD), bf16)
+
+    return pl.pallas_call(
+        functools.partial(state_back_kernel, n, rows, steps, pairs),
+        grid=(steps,),
+        in_specs=[
+            pl.BlockSpec((1, rows, width), lambda i: (lax.div(i, pairs), 0, 0)),
+            pl.BlockSpec((width, wide), lambda i: (0, lax.rem(i, pairs))),
+            pl.BlockSpec((1, HD), lambda i: (0, 0)),
+            tall(rows), tall(rows), tall(HD),
+        ],
+        out_specs=[tall(rows), tall(rows), tall(HD), pl.BlockSpec((8, HD), lambda i: (0, 0))],
+        out_shape=[shape(rows), shape(rows), shape(HD), jax.ShapeDtypeStruct((8, HD), f32)],
+        scratch_shapes=[
+            pltpu.VMEM((steps, PAIR, HD, HD), bf16),
+            pltpu.VMEM((steps, PAIR, HD, HD), bf16),
+            pltpu.SemaphoreType.DMA((steps, PAIR)),
+            pltpu.SemaphoreType.DMA((steps, PAIR)),
+        ],
+        compiler_params=pltpu.CompilerParams(
+            collective_id=6, has_side_effects=True, vmem_limit_bytes=VMEM_LIMIT,
+            dimension_semantics=("arbitrary",),
+        ),
+        name="state_back",
+    )(rows_back, out_weight, gain, mix, carry, kw)
+
+
+def mixer_back_kernel(
+    n, tensor, rows, steps, pairs,
+    pq_ref, pk_ref, pv_ref, strength_ref, filt_ref, high_ref, low_ref, inv_ref, end_ref, state_ref,
+    second_ref, gate_ref, ffn_ref, down_ref, hidden_ref,
+    proj_ref, logit_ref, conv_ref, total_ref, layer_ref,
+    xq_ref, xk_ref, xv_ref, bc_ref, last_ref, rim_ref, next_ref, inward_ref, spare_ref, kept_ref,
+    part_ref, near_ref, far_ref, pass_ref,
+    rim_send, rim_recv, ring_send, ring_recv, a_send, a_recv, x_send, x_recv,
+):
+    me, t = lax.axis_index("dp"), lax.axis_index("tensor")
+    step = pl.program_id(0)
     wide = PAIR * HD
     local = proj_ref.shape[2] // 3
+    seqs = steps // pairs
+    own_len = rows // tensor
+    core, cross = swap_pair(t), swap_half(t, tensor)
+    both = swap_half(core, tensor)
+    count = total_ref.shape[0]
+    ring = RingScatter(
+        n, count, grad_part(count, second_ref, gate_ref, spare_ref), inward_ref, total_ref,
+        ring_send, ring_recv,
+    )
 
     def to_rim(seq):
         return remote(
@@ -534,15 +671,24 @@
             dp=lax.rem(me + n - 1, n),
         )
 
-    def hop(at, h):
+    def span(at):
+        return pl.ds(pl.multiple_of(at * own_len, own_len), own_len)
+
+    def to_core(s, i):
         return remote(
-            send_ref.at[at, h], recv_ref.at[at, h], send_sem.at[at, h], recv_sem.at[at, h],
-            dp=lax.rem(me + n - 1, n),
-        )
+            part_ref.at[s, span((core, both)[i]), :], near_ref.at[s, i],
+            a_send.at[s, i], a_recv.at[s, i], tensor=core,
+        )
+
+    def to_cross(s):
+        return remote(pass_ref.at[s], far_ref.at[s], x_send.at[s], x_recv.at[s], tensor=cross)
 
     @pl.when(step == 0)
     def _():
         barrier = pltpu.get_barrier_semaphore()
+        ring.greet(barrier)
+        for device in (core, cross):
+            pl.semaphore_signal(barrier, inc=1, device_id={"tensor": device}, device_id_type=MESH)
 
         @pl.when(me < n - 1)
         def _():
@@ -550,146 +696,145 @@
 
         @pl.when(me == n - 1)
         def _():
-            recv_ref[...] = jnp.zeros_like(recv_ref)
             next_ref[...] = jnp.zeros_like(next_ref)
 
         @pl.when(me > 0)
         def _():
-            pl.semaphore_wait(barrier, 1)
-
-        head_ref[...] = jnp.zeros_like(head_ref)
+            pl.semaphore_wait(barrier, 5)
+
+        @pl.when(me == 0)
+        def _():
+            pl.semaphore_wait(barrier, 4)
+
+        ring.start()
         bc_ref[...] = jnp.zeros_like(bc_ref)
         conv_ref[...] = jnp.zeros_like(conv_ref)
 
-    @pl.when(step < steps)
-    def _():
-        adds = []
-        head_sum = jnp.zeros((1, HD), f32)
-        for h in range(PAIR):
-            mix, back = mix_ref[0, h], back_ref[0, :, h * HD : (h + 1) * HD]
-            scale = lax.rsqrt(jnp.mean(mix * mix, axis=-1, keepdims=True) + epsilon)
-            unit = mix * scale
-            head_sum = head_sum + jnp.sum(back * unit, axis=0, keepdims=True)
-            scaled = back * gain_ref[...]
-            out = halves(scale * (scaled - unit * jnp.mean(scaled * unit, axis=-1, keepdims=True)))
-            high_ref[step, h], low_ref[step, h] = out
-            adds.append(narrow_product(halves(carry_ref[0, h]), out, 0))
-        head_ref[...] += jnp.where(
-            lax.broadcasted_iota(jnp.int32, head_ref.shape, 0) == 0, head_sum, 0.0
-        )
-
-        for h in range(PAIR):
-            @pl.when(me < n - 1)
+    @pl.when(step < seqs)
+    def _():
+        here = pl.ds(pl.multiple_of(step * rows, rows), rows)
+        part_ref[step] = dot(ffn_ref[here, :], down_ref[...], 1, 1).astype(bf16)
+        for i in (1, 0):
+            to_core(step, i).start()
+
+    @pl.when(step >= steps - seqs)
+    def _():
+        s = step - (steps - seqs)
+        to_core(s, 1).wait_recv()
+        pass_ref[s] = (
+            part_ref[s, span(cross), :].astype(f32) + near_ref[s, 1].astype(f32)
+        ).astype(bf16)
+        to_cross(s).start()
+
+    each = -(-(n - 2) // (steps - 1))
+
+    @pl.when(step > 0)
+    def _():
+        for i in range(each):
+            at = (step - 1) * each + i + 2
+
+            @pl.when(at < n)
             def _():
-                hop(step, h).wait_recv()
-
-            end, kw = recv_ref[step, h], halves(kw_ref[0, h])
-            before = adds[h] + end.astype(f32) - dot(kw[0], end, 0, 0) - dot(kw[1], end, 0, 0)
-            send_ref[step, h] = before.astype(bf16)
-
-            @pl.when(me > 0)
-            def _():
-                hop(step, h).start()
-
-    @pl.when(step >= steps)
-    def _():
-        now = step - steps
-        seq, pair = lax.div(now, pairs), lax.rem(now, pairs)
-        @pl.when(pair == 0)
-        def _():
-            logit_ref[...] = jnp.zeros_like(logit_ref)
-
-        at_row, at_col = masks(rows)
-        strengths = strength_ref[0]
-        lane = lax.broadcasted_iota(jnp.int32, strengths.shape, 1)
-        run_q, gate_q = conv_act(xq_ref, pq_ref[0], filt_ref, 0, rows)
-        run_k, gate_k = conv_act(xk_ref, pk_ref[0], filt_ref, 1, rows)
-        run_v, gate_v = conv_act(xv_ref, pv_ref[0], filt_ref, 2, rows)
-        act_q, act_k, act_v = run_q * gate_q, run_k * gate_k, run_v * gate_v
-        back_acts = ([], [], [])
-        for h in range(PAIR):
-            cut = slice(h * HD, (h + 1) * HD)
-            scale_q, scale_k = unit_scale(act_q[:, cut]), unit_scale(act_k[:, cut])
-            unit_q, unit_k = act_q[:, cut] * scale_q, act_k[:, cut] * scale_k
-            q, k, v = unit_q.astype(bf16), unit_k.astype(bf16), act_v[:, cut].astype(bf16)
-            chosen = lane == pair * PAIR + h
-            beta = jnp.sum(jnp.where(chosen, strengths, 0.0), axis=-1, keepdims=True)
-            gram = dot(k, k, 1, 1)
-            scores = halves(jnp.where(at_row >= at_col, dot(q, k, 1, 1), 0.0))
-            state, end = state_ref[0, h], recv_ref[now, h]
-            out = (high_ref[now, h], low_ref[now, h])
-            inv = halves(inv_ref[h])
-            through = dot(k, beside(state, end))
-            rest = v.astype(f32) - through[:, :HD]
-            update = halves(narrow_product(inv, halves(beta * rest)))
-            back_update = halves(narrow_product(scores, out, 0) + through[:, HD:])
-            back_scores = short_product_t(out, update[0]) + dot(out[0], update[1], 1, 1)
-            back_scores = halves(jnp.where(at_row >= at_col, back_scores, 0.0))
-            solved = narrow_product(inv, back_update, 0)
-            terms = halves(solved)
-            back_low = short_product_t(terms, update[0]) + dot(terms[0], update[1], 1, 1)
-            back_low = jnp.where(at_row > at_col, -back_low, 0.0)
-            back_beta = jnp.sum(back_low * gram, axis=-1, keepdims=True) + jnp.sum(
-                solved * rest, axis=-1, keepdims=True
+                if each == 1:
+                    ring.advance_first(at, kept_ref)
+                else:
+                    ring.advance(at)
+
+    seq, pair = lax.div(step, pairs), lax.rem(step, pairs)
+
+    @pl.when(pair == 0)
+    def _():
+        logit_ref[...] = jnp.zeros_like(logit_ref)
+
+    at_row, at_col = masks(rows)
+    strengths = strength_ref[0]
+    lane = lax.broadcasted_iota(jnp.int32, strengths.shape, 1)
+    run_q, gate_q = conv_act(xq_ref, pq_ref[0], filt_ref, 0, rows)
+    run_k, gate_k = conv_act(xk_ref, pk_ref[0], filt_ref, 1, rows)
+    run_v, gate_v = conv_act(xv_ref, pv_ref[0], filt_ref, 2, rows)
+    act_q, act_k, act_v = run_q * gate_q, run_k * gate_k, run_v * gate_v
+    back_acts = ([], [], [])
+    for h in range(PAIR):
+        cut = slice(h * HD, (h + 1) * HD)
+        scale_q, scale_k = unit_scale(act_q[:, cut]), unit_scale(act_k[:, cut])
+        unit_q, unit_k = act_q[:, cut] * scale_q, act_k[:, cut] * scale_k
+        q, k, v = unit_q.astype(bf16), unit_k.astype(bf16), act_v[:, cut].astype(bf16)
+        chosen = lane == pair * PAIR + h
+        beta = jnp.sum(jnp.where(chosen, strengths, 0.0), axis=-1, keepdims=True)
+        gram = dot(k, k, 1, 1)
+        scores = halves(jnp.where(at_row >= at_col, dot(q, k, 1, 1), 0.0))
+        state, end = state_ref[0, h], end_ref[0, h]
+        out = (high_ref[0, h], low_ref[0, h])
+        inv = halves(inv_ref[h])
+        through = dot(k, beside(state, end))
+        rest = v.astype(f32) - through[:, :HD]
+        update = halves(narrow_product(inv, halves(beta * rest)))
+        back_update = halves(narrow_product(scores, out, 0) + through[:, HD:])
+        back_scores = short_product_t(out, update[0]) + dot(out[0], update[1], 1, 1)
+        back_scores = halves(jnp.where(at_row >= at_col, back_scores, 0.0))
+        solved = narrow_product(inv, back_update, 0)
+        terms = halves(solved)
+        back_low = short_product_t(terms, update[0]) + dot(terms[0], update[1], 1, 1)
+        back_low = jnp.where(at_row > at_col, -back_low, 0.0)
+        back_beta = jnp.sum(back_low * gram, axis=-1, keepdims=True) + jnp.sum(
+            solved * rest, axis=-1, keepdims=True
+        )
+        back_gram = beta * back_low
+        back_gram = halves(back_gram + back_gram.T)
+        back_value = beta * solved
+        back_q = short_product_t(out, state) + dot(back_scores[0], k) + dot(back_scores[1], k)
+        back_k = (
+            dot(back_scores[0], q, 0, 0)
+            + dot(back_scores[1], q, 0, 0)
+            + short_product_t(update, end)
+            + dot(back_gram[0], k)
+            + dot(back_gram[1], k)
+            - short_product_t(halves(back_value), state)
+        )
+        logit_ref[0] += jnp.where(chosen, back_beta * beta * (1.0 - beta), 0.0)
+        back_acts[0].append(
+            (back_q - unit_q * jnp.sum(unit_q * back_q, axis=-1, keepdims=True)) * scale_q
+        )
+        back_acts[1].append(
+            (back_k - unit_k * jnp.sum(unit_k * back_k, axis=-1, keepdims=True)) * scale_k
+        )
+        back_acts[2].append(back_value)
+
+    if each == 1:
+        @pl.when((step > 0) & (step + 1 < n))
+        def _():
+            ring.advance_second(step + 1, kept_ref)
+
+    for column, (running, gate, x_ref) in enumerate(
+        ((run_q, gate_q, xq_ref), (run_k, gate_k, xk_ref), (run_v, gate_v, xv_ref))
+    ):
+        back_conv = beside(*back_acts[column]) * gate * (1.0 + running * (1.0 - gate))
+        bc_ref[pl.ds(RIM, rows), :] = back_conv
+        back_x, back_rim = None, None
+        for tap in range(KCONV):
+            weight = filt_ref[pl.ds(column * KCONV + tap, 1), :]
+            term = weight * bc_ref[pl.ds(RIM + KCONV - 1 - tap, rows), :]
+            edge = weight * bc_ref[pl.ds(KCONV - 1 - tap, RIM), :]
+            back_x = term if back_x is None else back_x + term
+            back_rim = edge if back_rim is None else back_rim + edge
+            grad = jnp.sum(
+                back_conv * x_ref[pl.ds(RIM - KCONV + 1 + tap, rows), :], axis=0, keepdims=True
             )
-            back_gram = beta * back_low
-            back_gram = halves(back_gram + back_gram.T)
-            back_value = beta * solved
-            back_q = short_product_t(out, state) + dot(back_scores[0], k) + dot(back_scores[1], k)
-            back_k = (
-                dot(back_scores[0], q, 0, 0)
-                + dot(back_scores[1], q, 0, 0)
-                + short_product_t(update, end)
-                + dot(back_gram[0], k)
-                + dot(back_gram[1], k)
-                - short_product_t(halves(back_value), state)
-            )
-            logit_ref[0] += jnp.where(chosen, back_beta * beta * (1.0 - beta), 0.0)
-            back_acts[0].append(
-                (back_q - unit_q * jnp.sum(unit_q * back_q, axis=-1, keepdims=True)) * scale_q
-            )
-            back_acts[1].append(
-                (back_k - unit_k * jnp.sum(unit_k * back_k, axis=-1, keepdims=True)) * scale_k
-            )
-            back_acts[2].append(back_value)
-
-        for column, (running, gate, x_ref) in enumerate(
-            ((run_q, gate_q, xq_ref), (run_k, gate_k, xk_ref), (run_v, gate_v, xv_ref))
-        ):
-            back_conv = beside(*back_acts[column]) * gate * (1.0 + running * (1.0 - gate))
-            bc_ref[pl.ds(RIM, rows), :] = back_conv
-            back_x, back_rim = None, None
-            for tap in range(KCONV):
-                weight = filt_ref[pl.ds(column * KCONV + tap, 1), :]
-                term = weight * bc_ref[pl.ds(RIM + KCONV - 1 - tap, rows), :]
-                edge = weight * bc_ref[pl.ds(KCONV - 1 - tap, RIM), :]
-                back_x = term if back_x is None else back_x + term
-                back_rim = edge if back_rim is None else back_rim + edge
-                grad = jnp.sum(
-                    back_conv * x_ref[pl.ds(RIM - KCONV + 1 + tap, rows), :], axis=0, keepdims=True
-                )
-                conv_ref[pair, pl.ds(column * KCONV + tap, 1), :] += grad
-            lanes = pl.ds(pl.multiple_of(column * local + pair * wide, wide), wide)
-            proj_ref[seq, :, lanes] = back_x.astype(bf16)
-            last_ref[seq, :, lanes] = back_x[rows - RIM :, :]
-            rim_ref[seq, :, lanes] = back_rim.astype(bf16)
-
-        @pl.when((pair == pairs - 1) & (me > 0))
-        def _():
-            to_rim(seq).start()
-
-    @pl.when(step == 2 * steps - 1)
-    def _():
-        seqs = steps // pairs
-
+            conv_ref[pair, pl.ds(column * KCONV + tap, 1), :] += grad
+        lanes = pl.ds(pl.multiple_of(column * local + pair * wide, wide), wide)
+        proj_ref[seq, :, lanes] = back_x.astype(bf16)
+        last_ref[seq, :, lanes] = back_x[rows - RIM :, :]
+        rim_ref[seq, :, lanes] = back_rim.astype(bf16)
+
+
+    @pl.when((pair == pairs - 1) & (me > 0))
+    def _():
+        to_rim(seq).start()
+
+    @pl.when(step == steps - 1)
+    def _():
         @pl.when(me > 0)
         def _():
-            def done(at, carry):
-                for h in range(PAIR):
-                    hop(at, h).wait_send()
-                return carry
-
-            lax.fori_loop(0, steps, done, 0)
             for seq in range(seqs):
                 to_rim(seq).wait_send()
 
@@ -702,75 +847,93 @@
             edge = last_ref[seq] + next_ref[seq].astype(f32)
             proj_ref[seq, pl.ds(rows - RIM, RIM), :] = edge.astype(bf16)
 
-
-def mixer_back(projected, strength, filters, gain, back_normed, mix, carry, inverse, kw, state):
-    n = lax.axis_size("dp")
+        def close(s, carry):
+            to_core(s, 0).wait_recv()
+            to_cross(s).wait_recv()
+            total = (
+                part_ref[s, span(t), :].astype(f32) + near_ref[s, 0].astype(f32) + far_ref[s].astype(f32)
+            )
+            layer_ref[s] = (hidden_ref[s] + total).astype(bf16)
+            for i in range(2):
+                to_core(s, i).wait_send()
+            to_cross(s).wait_send()
+            return carry
+
+        lax.fori_loop(0, seqs, close, 0)
+        ring.finish()
+
+
+def mixer_back(projected, strength, filters, out_terms, inverse, end, state, gate_factors, ffn_factors, hidden):
+    n, tensor = lax.axis_size("dp"), lax.axis_size("tensor")
     seqs, extended, width = projected.shape
     rows = extended - RIM
     local = width // 3
     pairs = local // (PAIR * HD)
     wide = PAIR * HD
     steps = seqs * pairs
-    def early(i):
-        return jnp.minimum(i, steps - 1)
-
-    def late(i):
-        return jnp.maximum(i - steps, 0)
+    vmem = pl.BlockSpec(memory_space=pltpu.VMEM)
 
     def part(column):
         return pl.BlockSpec(
-            (1, extended, wide),
-            lambda i: (lax.div(late(i), pairs), 0, column * pairs + lax.rem(late(i), pairs)),
-        )
-
-    def tall(size, when):
-        return pl.BlockSpec((1, PAIR, size, HD), lambda i: (when(i), 0, 0, 0))
+            (1, extended, wide), lambda i: (lax.div(i, pairs), 0, column * pairs + lax.rem(i, pairs))
+        )
+
+    def tall(size):
+        return pl.BlockSpec((1, PAIR, size, HD), lambda i: (i, 0, 0, 0))
 
     def seq(size, span):
-        return pl.BlockSpec((1, size, span), lambda i: (lax.div(late(i), pairs), 0, 0))
+        return pl.BlockSpec((1, size, span), lambda i: (lax.div(i, pairs), 0, 0))
 
     heads = strength.shape[2]
+    own_len, model = hidden.shape[1:]
+    count, columns = gate_factors[0].shape[1] // n, gate_factors[1].shape[1]
     return pl.pallas_call(
-        functools.partial(mixer_back_kernel, n, rows, steps, pairs),
-        grid=(2 * steps,),
+        functools.partial(mixer_back_kernel, n, tensor, rows, steps, pairs),
+        grid=(steps,),
         in_specs=[
             part(0), part(1), part(2),
             seq(rows, heads),
-            pl.BlockSpec((3 * KCONV, wide), lambda i: (0, lax.rem(late(i), pairs))),
-            pl.BlockSpec((1, HD), lambda i: (0, 0)),
-            pl.BlockSpec(
-                (1, rows, wide), lambda i: (lax.div(early(i), pairs), 0, lax.rem(early(i), pairs))
-            ),
-            tall(rows, early), tall(rows, early),
-            pl.BlockSpec((PAIR, rows, rows), lambda i: (late(i), 0, 0)),
-            tall(HD, early), tall(HD, late),
-        ],
+            pl.BlockSpec((3 * KCONV, wide), lambda i: (0, lax.rem(i, pairs))),
+            tall(rows), tall(rows),
+            pl.BlockSpec((PAIR, rows, rows), lambda i: (i, 0, 0)),
+            tall(HD), tall(HD),
+        ]
+        + [vmem] * 5,
         out_specs=[
             pl.BlockSpec((seqs, rows, width), lambda i: (0, 0, 0)),
             seq(rows, heads),
             pl.BlockSpec((pairs, 3 * KCONV, wide), lambda i: (0, 0, 0)),
-            pl.BlockSpec((8, HD), lambda i: (0, 0)),
+            vmem, vmem,
         ],
         out_shape=[
             jax.ShapeDtypeStruct((seqs, rows, width), bf16),
             jax.ShapeDtypeStruct((seqs, rows, heads), f32),
             jax.ShapeDtypeStruct((pairs, 3 * KCONV, wide), f32),
-            jax.ShapeDtypeStruct((8, HD), f32),
+            jax.ShapeDtypeStruct((count, columns), f32),
+            jax.ShapeDtypeStruct((seqs, own_len, model), bf16),
         ],
         scratch_shapes=[
             pltpu.VMEM((extended, wide), f32),
             pltpu.VMEM((extended, wide), f32),
             pltpu.VMEM((extended, wide), f32),
             pltpu.VMEM((rows + 2 * RIM, wide), f32),
-            pltpu.VMEM((steps, PAIR, rows, HD), bf16),
-            pltpu.VMEM((steps, PAIR, rows, HD), bf16),
-            pltpu.VMEM((steps, PAIR, HD, HD), bf16),
-            pltpu.VMEM((steps, PAIR, HD, HD), bf16),
             pltpu.VMEM((seqs, RIM, width), f32),
             pltpu.VMEM((seqs, RIM, width), bf16),
             pltpu.VMEM((seqs, RIM, width), bf16),
-            pltpu.SemaphoreType.DMA((steps, PAIR)),
-            pltpu.SemaphoreType.DMA((steps, PAIR)),
+            pltpu.VMEM((n, count, columns), bf16),
+            spare(count, columns),
+            pltpu.VMEM((2, count // (2 * SUBS), columns), f32),
+            pltpu.VMEM((seqs, rows, model), bf16),
+            pltpu.VMEM((seqs, 2, own_len, model), bf16),
+            pltpu.VMEM((seqs, own_len, model), bf16),
+            pltpu.VMEM((seqs, own_len, model), bf16),
+            pltpu.SemaphoreType.DMA((seqs,)),
+            pltpu.SemaphoreType.DMA((seqs,)),
+        ]
+        + ring_semaphores(n)
+        + [
+            pltpu.SemaphoreType.DMA((seqs, 2)),
+            pltpu.SemaphoreType.DMA((seqs, 2)),
             pltpu.SemaphoreType.DMA((seqs,)),
             pltpu.SemaphoreType.DMA((seqs,)),
         ],
@@ -780,8 +943,8 @@
         ),
         name="mixer_back",
     )(
-        projected, projected, projected, strength, filters, gain,
-        back_normed, mix, carry, inverse, kw, state,
+        projected, projected, projected, strength, filters, *out_terms, inverse, end, state,
+        *gate_factors, *ffn_factors, hidden,
     )
 
 
@@ -960,22 +1123,43 @@
 
 
 def fold_kernel(
-    n, n_seqs, tensor, backward, count,
-    part_ref, own_ref, gain_ref, hidden_ref, *refs,
+    n, n_seqs, tensor, backward, count, terms,
+    own_ref, gain_ref, hidden_ref, *refs,
 ):
     t = lax.axis_index("tensor")
     core, cross = swap_pair(t), swap_half(t, tensor)
     both = swap_half(core, tensor)
     own_len = own_ref.shape[1]
     refs = list(refs)
+    term_hbm, refs = refs[:terms], refs[terms:]
     pieces, refs = refs[:count], refs[count:]
-    outs = 1 if backward else count
+    outs = 1 if backward else count - 1
     (rows_ref, keep_ref, sum_ref), made, refs = refs[:3], refs[3 : 3 + outs], refs[3 + outs :]
+    if not backward:
+        (gate_full, *pieces), (gate_out, up_out), refs = pieces, refs[:2], refs[2:]
+        count -= 1
+    held, part_ref, load_sem, refs = refs[:terms], refs[terms], refs[terms + 1], refs[terms + 2 :]
     (
         near_ref, far_ref, send_ref, own_sum_ref, a_send, a_recv, x_send, x_recv, g_send, g_recv,
         ring_send, ring_recv,
     ) = refs[:12]
     ring_refs = refs[12:]
+    if backward:
+        factors, ring_refs = ring_refs[2:], ring_refs[:2]
+        loads = [
+            pltpu.make_async_copy(source, target, load_sem.at[terms + i])
+            for i, (source, target) in enumerate(zip(pieces, factors))
+        ]
+        pieces = factors
+    else:
+        loads = []
+    ahead = len(loads)
+    loads += [
+        pltpu.make_async_copy(source, target, load_sem.at[i])
+        for i, (source, target) in enumerate(zip(term_hbm, held))
+    ]
+    for load in loads:
+        load.start()
     if backward:
         rings = [
             RingScatter(
@@ -993,8 +1177,7 @@
 
     def advance(hop):
         if hop < n:
-            for ring in rings:
-                ring.advance(hop)
+            rings[0].advance(hop)
 
     barrier = pltpu.get_barrier_semaphore()
     rings[0].greet(barrier)
@@ -1021,11 +1204,16 @@
             piece, peer = rows_ref.at[s, span(t), :], (cross, core)[i]
         return remote(piece, piece, g_send.at[s, i], g_recv.at[s, i], tensor=peer)
 
-    for s in range(n_seqs):
-        for i in (1, 0):
-            to_core(s, i).start()
-    for ring in rings:
-        ring.start()
+    for load in loads[:ahead]:
+        load.wait()
+    rings[0].start()
+    for load in loads[ahead:]:
+        load.wait()
+    if not backward:
+        gate_ref, up_ref, stage_ref, hold_sem, out_sem = ring_refs[2:]
+        load_gate = pltpu.make_async_copy(gate_full, gate_ref, hold_sem.at[0])
+        load_up = pltpu.make_async_copy(made[0], up_ref, hold_sem.at[1])
+        load_gate.start()
 
     def first(s, carry):
         to_core(s, 1).wait_recv()
@@ -1037,10 +1225,33 @@
         own_sum_ref[s] = part_ref[s, span(t), :].astype(f32) + near_ref[s, 0].astype(f32)
         return carry
 
-    lax.fori_loop(0, n_seqs, first, 0)
+    length = own_len * tensor
+
+    def zeroth(s, carry):
+        here = pl.ds(pl.multiple_of(s * length, length), length)
+        part = dot(held[0][here, :], held[1][...], 1, 1)
+        for i in range(2, terms, 2):
+            part = part + dot(held[i][here, :], held[i + 1][...], 1, 1)
+        part_ref[s] = part.astype(bf16)
+        for i in (1, 0):
+            to_core(s, i).start()
+
+        @pl.when(s > 0)
+        def _():
+            first(s - 1, 0)
+
+        for i, at in enumerate(moments[0]):
+            @pl.when(s == at)
+            def _():
+                advance(2 + i)
+
+        return carry
+
+    moments = ((1, 3), (0, 2, 3), (1,)) if backward else ((), (0, 1, 2, 3), (1,))
+    done = [2, 2 + len(moments[0]), 2 + len(moments[0]) + len(moments[1])]
+    lax.fori_loop(0, n_seqs, zeroth, 0)
+    first(n_seqs - 1, 0)
     sum_ref[...] = jnp.zeros_like(sum_ref)
-
-    moments = (0, 1, 2, 3, 1) if backward else (0, 2, 0)
 
     def second(s, carry):
         to_cross(s).wait_recv()
@@ -1064,10 +1275,10 @@
         gather(s, 0).start()
         gather(s, 1).start()
 
-        for i, at in enumerate(moments[:-1]):
+        for i, at in enumerate(moments[1]):
             @pl.when(s == at)
             def _():
-                advance(2 + i)
+                advance(done[1] + i)
 
         return carry
 
@@ -1077,29 +1288,74 @@
         gather(s, 0).wait_recv()
         gather(s, 2).start()
 
-        @pl.when(s == moments[-1])
-        def _():
-            advance(1 + len(moments))
+        @pl.when(s == moments[2][0])
+        def _():
+            advance(done[2])
 
         return carry
 
     lax.fori_loop(0, n_seqs, third, 0)
 
     def rest(hop, carry):
-        for ring in rings:
-            ring.advance(hop)
+        rings[0].advance(hop)
         return carry
 
-    lax.fori_loop(2 + len(moments), n, rest, 0)
-    for ring in rings:
+    lax.fori_loop(done[2] + 1, n, rest, 0)
+    if backward:
+        rings[0].finish()
+    else:
+        def others(s, carry):
+            gather(s, 1).wait_recv()
+            gather(s, 2).wait_recv()
+            return carry
+
+        lax.fori_loop(0, n_seqs, others, 0)
+        rings[1].start()
+
+        def store(which, s):
+            return pltpu.make_async_copy(
+                stage_ref.at[which, s], (gate_out, up_out)[which].at[s], out_sem.at[which, s]
+            )
+
+        def product(which, weight_ref, begin):
+            def one(s, carry):
+                value = dot(rows_ref[s], weight_ref[...].reshape(-1, weight_ref.shape[2]))
+                stage_ref[which, s] = value
+                store(which, s).start()
+
+                @pl.when(begin + s < n)
+                def _():
+                    rings[1].advance(begin + s)
+
+                return carry
+
+            lax.fori_loop(0, n_seqs, one, 0)
+
+        load_gate.wait()
+        product(0, gate_ref, 2)
+        rings[0].settle(1, n - 1)
+        load_up.start()
+        load_up.wait()
+        product(1, up_ref, 2 + n_seqs)
+
+        def remaining(hop, carry):
+            rings[1].advance(hop)
+            return carry
+
+        lax.fori_loop(2 + 2 * n_seqs, n, remaining, 0)
+        rings[1].settle(1, n - 1)
+
+        def stored(s, carry):
+            for which in range(2):
+                store(which, s).wait()
+            return carry
+
+        lax.fori_loop(0, n_seqs, stored, 0)
+
+    def last(s, carry):
         if backward:
-            ring.finish()
-        else:
-            ring.settle(1, n - 1)
-
-    def last(s, carry):
-        gather(s, 1).wait_recv()
-        gather(s, 2).wait_recv()
+            gather(s, 1).wait_recv()
+            gather(s, 2).wait_recv()
         for i in range(2):
             to_core(s, i).wait_send()
         to_cross(s).wait_send()
@@ -1110,7 +1366,7 @@
     lax.fori_loop(0, n_seqs, last, 0)
 
 
-def fold(part, own, gain, pieces, hidden=None):
+def fold(terms, own, gain, pieces, hidden=None):
     n, tensor = lax.axis_size("dp"), lax.axis_size("tensor")
     seqs, own_len, width = own.shape
     backward, count = hidden is not None, len(pieces)
@@ -1119,13 +1375,24 @@
         rows, columns = pieces[0].shape[1] // n, pieces[1].shape[1]
         made = [jax.ShapeDtypeStruct((rows, columns), f32)]
         ring_scratch = [pltpu.VMEM((n, rows, columns), bf16), spare(rows, columns)]
+        ring_scratch += [pltpu.VMEM(piece.shape, bf16) for piece in pieces]
+        piece_specs = [anywhere] * count
     else:
         hidden = jnp.zeros((8, 128), f32)
-        made = [jax.ShapeDtypeStruct((n,) + piece.shape, bf16) for piece in pieces]
-        ring_scratch = [pltpu.SemaphoreType.DMA for _ in pieces]
+        made = [jax.ShapeDtypeStruct((n,) + piece.shape, bf16) for piece in pieces[1:]]
+        columns = pieces[0].shape[2]
+        made += [jax.ShapeDtypeStruct((seqs, tensor * own_len, columns), f32)] * 2
+        ring_scratch = [pltpu.SemaphoreType.DMA for _ in pieces[1:]] + [
+            pltpu.VMEM(pieces[0].shape, bf16),
+            pltpu.VMEM(pieces[0].shape, bf16),
+            pltpu.VMEM((2, seqs, tensor * own_len, columns), f32),
+            pltpu.SemaphoreType.DMA((2,)),
+            pltpu.SemaphoreType.DMA((2, seqs)),
+        ]
+        piece_specs = [anywhere] + [vmem] * (count - 1)
     return pl.pallas_call(
-        functools.partial(fold_kernel, n, seqs, tensor, backward, count),
-        in_specs=[vmem] * (4 + count),
+        functools.partial(fold_kernel, n, seqs, tensor, backward, count, len(terms)),
+        in_specs=[vmem] * 3 + [anywhere] * len(terms) + piece_specs,
         out_specs=[vmem] * 3 + [vmem if backward else anywhere] * len(made),
         out_shape=[
             jax.ShapeDtypeStruct((seqs, tensor * own_len, width), bf16),
@@ -1133,7 +1400,10 @@
             jax.ShapeDtypeStruct((1, width), f32),
         ]
         + made,
-        scratch_shapes=[
+        scratch_shapes=[pltpu.VMEM(term.shape, bf16) for term in terms]
+        + [
+            pltpu.VMEM((seqs, own_len * tensor, width), bf16),
+            pltpu.SemaphoreType.DMA((len(terms) + count,)),
             pltpu.VMEM((seqs, 2, own_len, width), bf16),
             pltpu.VMEM((seqs, own_len, width), bf16),
             pltpu.VMEM((seqs, own_len, width), bf16),
@@ -1152,7 +1422,7 @@
             collective_id=4 if backward else 3, has_side_effects=True, vmem_limit_bytes=VMEM_LIMIT
         ),
         name="fold_back" if backward else "fold",
-    )(part, own, gain, hidden, *pieces)
+    )(own, gain, hidden, *terms, *pieces)
 
 
 def closing_kernel(
@@ -1160,26 +1430,32 @@
     own_ref, tokens_ref, gain_ref, small_ref, *refs,
 ):
     hbm, refs = refs[:9], refs[9:]
-    d_ref, gate_sum, out_sum, qkv_sum, small_sum, gain_sum, shared_ref = refs[:7]
+    d_ref, up_sum, out_sum, qkv_sum, small_sum, gain_sum, shared_ref = refs[:7]
     refs = refs[7:]
     held, refs = refs[:9], refs[9:]
     (
-        gate_in, out_in, qkv_in, small_in, gain_in, spare_gate, spare_out, spare_qkv,
+        up_in, out_in, qkv_in, small_in, gain_in, spare_up, spare_out, spare_qkv,
         part_ref, near_ref, far_ref, send_ref, total_ref, pass_ref, got_ref,
         load_sem, a_send, a_recv, x_send, x_recv, ring_send, ring_recv, s_send, s_recv,
     ) = refs
-    second_ref, gate_ref, back_ref, mix_ref, proj_ref, weight_ref, logit_ref, beta_ref, first_ref = held
+    second_ref, up_ref, back_ref, mix_ref, proj_ref, weight_ref, logit_ref, beta_ref, first_ref = held
     me, t = lax.axis_index("dp"), lax.axis_index("tensor")
     core, cross = swap_pair(t), swap_half(t, tensor)
     both = swap_half(core, tensor)
     own_len = tokens_ref.shape[1]
     length = own_len * tensor
-    rows, width = gate_sum.shape[0], gain_ref.shape[1]
+    rows, width = up_sum.shape[0], gain_ref.shape[1]
     block = gain_sum.shape[1]
 
     loads = [
         pltpu.make_async_copy(source, target, load_sem.at[i])
-        for i, (source, target) in enumerate(zip(hbm, held))
+        for i, (source, target) in enumerate(zip(hbm[:8], held))
+    ] + [
+        pltpu.make_async_copy(
+            hbm[8].at[s, pl.ds(RIM, length), :], first_ref.at[pl.ds(s * length, length), :],
+            load_sem.at[8 + s],
+        )
+        for s in range(n_seqs)
     ]
     for load in loads:
         load.start()
@@ -1191,14 +1467,14 @@
     def ring(i, count, part, inward, total, lanes=2 * SUBS):
         return RingScatter(n, count, part, inward, total, ring_send.at[i], ring_recv.at[i], lanes)
 
-    gate = ring(0, rows, grad_part(rows, second_ref, gate_ref, spare_gate), gate_in, gate_sum)
+    up = ring(0, rows, grad_part(rows, second_ref, up_ref, spare_up), up_in, up_sum)
     out = ring(1, rows, grad_part(rows, back_ref, mix_ref, spare_out), out_in, out_sum)
     qkv = ring(2, rows, grad_part(rows, first_ref, proj_ref, spare_qkv), qkv_in, qkv_sum)
     small = ring(3, small_ref.shape[1], held_part(small_ref), small_in, small_sum, 2)
     gains = ring(4, 32, gain_part, gain_in, gain_sum, 2)
 
     barrier = pltpu.get_barrier_semaphore()
-    gate.greet(barrier)
+    up.greet(barrier)
     for device in (core, cross):
         pl.semaphore_signal(barrier, inc=1, device_id={"tensor": device}, device_id_type=MESH)
     pl.semaphore_wait(barrier, 4)
@@ -1215,7 +1491,7 @@
     def to_cross(s):
         return remote(send_ref.at[s], far_ref.at[s], x_send.at[s], x_recv.at[s], tensor=cross)
 
-    early = (gate, out, small)
+    early = (up, out, small)
     for load in loads[:4]:
         load.wait()
     for chain in early:
@@ -1324,7 +1600,8 @@
             jax.ShapeDtypeStruct((32, block), f32),
             jax.ShapeDtypeStruct(shared, f32),
         ],
-        scratch_shapes=[pltpu.VMEM(factor.shape, bf16) for factor in factors]
+        scratch_shapes=[pltpu.VMEM(factor.shape, bf16) for factor in factors[:8]]
+        + [pltpu.VMEM((seqs * own_len * tensor, width), bf16)]
         + [pltpu.VMEM((n, rows, count), bf16) for count in columns]
         + [pltpu.VMEM(small.shape, bf16), pltpu.VMEM((n, 32, block), bf16)]
         + [spare(rows, count) for count in columns]
@@ -1336,7 +1613,7 @@
             pltpu.VMEM((32, width), f32),
             pltpu.VMEM((2,) + shared, f32),
             pltpu.VMEM((2,) + shared, f32),
-            pltpu.SemaphoreType.DMA((9,)),
+            pltpu.SemaphoreType.DMA((8 + seqs,)),
             pltpu.SemaphoreType.DMA((seqs, 2)),
             pltpu.SemaphoreType.DMA((seqs, 2)),
             pltpu.SemaphoreType.DMA((seqs,)),
@@ -1369,27 +1646,6 @@
 
 def matmul(spec, left, right):
     return jnp.einsum(spec, left, right, preferred_element_type=f32)
-
-
-def swap(block, axis, half):
-    count = lax.axis_size(axis)
-    route = [(i, (i + count // 2) % count if half else i ^ 1) for i in range(count)]
-    return lax.ppermute(block, axis, route)
-
-
-def tensor_scatter(part):
-    tensor, t = lax.axis_size("tensor"), lax.axis_index("tensor")
-    seqs, rows, width = part.shape
-    chunks = part.reshape(seqs, tensor, rows // tensor, width)
-
-    def chunk(at):
-        return lax.dynamic_index_in_dim(chunks, at, 1, keepdims=False)
-
-    core, cross = swap_pair(t), swap_half(t, tensor)
-    both = swap_half(core, tensor)
-    near_own, near_cross = swap(chunk(core), "tensor", False), swap(chunk(both), "tensor", False)
-    far = swap((chunk(cross).astype(f32) + near_cross.astype(f32)).astype(bf16), "tensor", True)
-    return chunk(t).astype(f32) + near_own.astype(f32) + far.astype(f32)
 
 
 def shards(
@@ -1448,15 +1704,13 @@
     normed_mix, mix, carry, inverse, kw, state, full_gate = mixer(
         projected, strength, filters, head_row, gate_weight
     )
-    full_gate = full_gate.reshape(width, hidden)
-
-    branch_part = matmul("stk,dk->std", normed_mix, full_out).astype(bf16)
-    normed_second, hidden_state, _, full_up, full_down = fold(
-        branch_part, tokens, gains[1:2], [up_weight, down_weight.T]
+
+    normed_second, hidden_state, _, full_up, full_down, gate_pre, up_pre = fold(
+        [flat(normed_mix), full_out], tokens, gains[1:2], [full_gate, up_weight, down_weight.T]
     )
-    full_up, full_down = full_up.reshape(width, hidden), full_down.reshape(width, hidden)
-    gate_pre = matmul("std,df->stf", normed_second, full_gate)
-    up_pre = matmul("std,df->stf", normed_second, full_up)
+    full_gate, full_up, full_down = (
+        weight.reshape(width, hidden) for weight in (full_gate, full_up, full_down)
+    )
     gate_sigmoid = jax.nn.sigmoid(gate_pre)
     ffn_hidden = (gate_pre * gate_sigmoid * up_pre).astype(bf16)
 
@@ -1465,18 +1719,14 @@
         back_hidden * up_pre * gate_sigmoid * (1.0 + gate_pre * (1.0 - gate_sigmoid))
     ).astype(bf16)
     back_up = (back_hidden * gate_pre * gate_sigmoid).astype(bf16)
-    back_second = matmul("stf,df->std", back_gate, full_gate) + matmul("stf,df->std", back_up, full_up)
     rows_back, back_state, gain_second, grad_down = fold(
-        back_second.astype(bf16), cotangent, gains[1:2],
+        [flat(back_gate), full_gate, flat(back_up), full_up], cotangent, gains[1:2],
         [flat(rows_cotangent), flat(ffn_hidden)], hidden_state,
     )
-    rows_back, back_up, ffn_hidden = lax.optimization_barrier((rows_back, back_up, ffn_hidden))
-    grad_up = matmul("std,stf->df", normed_second, back_up)
-    ffn_part = matmul("stf,df->std", ffn_hidden, full_down).astype(bf16)
-    layer_out = (hidden_state + tensor_scatter(ffn_part)).astype(bf16)
-    back_normed = matmul("std,dk->stk", rows_back, full_out)
-    back_proj, back_logit, conv_part, head_part = mixer_back(
-        projected, strength, filters, head_row, back_normed, mix, carry, inverse, kw, state
+    high, low, end, head_part = state_back(rows_back, full_out, head_row, mix, carry, kw)
+    back_proj, back_logit, conv_part, grad_gate, layer_out = mixer_back(
+        projected, strength, filters, (high, low), inverse, end, state,
+        (flat(normed_second), flat(back_gate)), (flat(ffn_hidden), full_down), hidden_state,
     )
     back_logit = back_logit.astype(bf16)
     grad_beta = matmul("std,sth->dh", normed_first, back_logit)
@@ -1493,11 +1743,11 @@
     )
     small_grads = jnp.pad(small_grads, ((0, 0), (0, block - small_grads.shape[1])))
     lanes = ((0, 0), (0, 128 - heads))
-    d_tokens, grad_gate, grad_out, grad_qkv, small_grads, _, shared = closing(
+    d_tokens, grad_up, grad_out, grad_qkv, small_grads, _, shared = closing(
         back_state, tokens, gains[0:1], small_grads.astype(bf16).reshape(n, -1, 128),
         [
-            flat(normed_second), flat(back_gate), flat(rows_back), flat(normed_mix), flat(back_proj),
-            full_qkv, jnp.pad(flat(back_logit), lanes), jnp.pad(full_beta, lanes), flat(normed_first),
+            flat(normed_second), flat(back_up), flat(rows_back), flat(normed_mix), flat(back_proj),
+            full_qkv, jnp.pad(flat(back_logit), lanes), jnp.pad(full_beta, lanes), normed_ext,
         ],
     )
     gain_row = shared[1, : max(1, width // n // 128)].reshape(-1)
@@ -1507,10 +1757,6 @@
     shared = shared[0]
     small_grads, shared = small_grads.reshape(-1), shared.reshape(-1)
 
-    def scatter(grad):
-        return lax.psum_scatter(grad.astype(bf16), "dp", scatter_dimension=0, tiled=True).astype(f32)
-
-    grad_up = scatter(grad_up)
     return (
         layer_out,
         d_tokens,

time: 797 us -> 737 us (0.925)
  matrix products: 95.9 us -> 33.3 us
  Pallas kernels: 615 us -> 651 us
  between operations: 14.9 us -> 1.35 us
  other arithmetic: 18.4 us -> 8.79 us
  local copies, waits for them, and re-layouts: 42.2 us -> 32.9 us
    dot_general x12 -> x4, matrix products: 95.9 us -> 33.3 us  [matmul(): return jnp.einsum(spec, left, right, preferred_element_type=f32)]
    pallas_call x1 -> x2, Pallas kernels: 90.9 us -> 120 us  [the longest x1 75.4 us: mixer_back(): pl.pallas_call(functools.partial(mixer_back_kernel, n, tensor, rows, step...]
    convert_element_type x3 -> x0, other arithmetic: 8.48 us -> none  [the longest x1 3.58 us: shards(): layer_out = (hidden_state + tensor_scatter(ffn_part)).astype(bf16)]
    unnamed x61 -> x39, local copies, waits for them, and re-layouts: 20 us -> 18.1 us
  transfers between devices with their start and end apart: 4 -> 0, of which waited for: 0 -> 0; matrix products, arithmetic and copies ran while one was open for 6% -> 0% of each run, Pallas kernels for 31% -> 0%
where the time goes in v4:
time: 737 us; the launch traced here: 727 us
  Pallas kernels  651 us (88%)
  matrix products  33.3 us (5%)
  local copies, waits for them, and re-layouts  32.9 us (4%)
  other arithmetic  8.79 us (1%)
    pallas_call x2, Pallas kernels, fold(): pl.pallas_call(functools.partial(fold_kernel, n, seqs, tensor, backward,...  215 us
    pallas_call x1, Pallas kernels, closing(): pl.pallas_call(functools.partial(closing_kernel, n, seqs, tensor), in_spe...  156 us
    pallas_call x1, Pallas kernels, opening(): pl.pallas_call(functools.partial(opening_kernel, n, tensor), in_specs=[vm...  88.7 us
    pallas_call x1, Pallas kernels, mixer_back(): pl.pallas_call(functools.partial(mixer_back_kernel, n, tensor, rows, step...  75.4 us
    pallas_call x1, Pallas kernels, mixer(): pl.pallas_call(functools.partial(mixer_kernel, n, rows, steps, pairs, lim...  71.5 us
    pallas_call x1, Pallas kernels, state_back(): pl.pallas_call(functools.partial(state_back_kernel, n, rows, steps, pairs...  44.4 us
    dot_general x4, matrix products, matmul(): return jnp.einsum(spec, left, right, preferred_element_type=f32)  33.3 us
    unnamed x39, local copies, waits for them, and re-layouts  18.1 us

profile of v4, /device:TPU:0, one launch (start us, length us, event | category | flops | bytes accessed | tf_op | source)
XLA Modules:
  0.0 727.5 jit_solution(11837318118574979763)
XLA Ops:
  4.4 1.8 copy.61
  6.2 2.2 copy.67
  8.5 88.7 %opening.1 = (bf16[8,256,1536]{2,1,0:T(8,128)(2,1)}, bf16[8,32,128]{2,1,0:T(8,128)(2,1)}, bf16[4,264,2048]{2,1,0:T(8,128)(2,1)}, bf16[4,256,2048]{2,1,0:T(8,128)(2,1)}, bf16[8,256,512]{2,1,0:T(8,128)(2,1)}) custom-call(bf16[256,512]{1,0:T(8,128)(2,1)} %q_ref.1, bf16[256,512]{1,0:T(8,128)(2,1)} %k_ref.1, bf16[256,512]{1,0:T(8,128)(2,1)} %v_ref.1, ...), custom_call_target="tpu_custom_call" | custom-call | tf_op jit(solution)/shard_map/opening/pallas_call | solution.py:1097
  98.6 3.3 fusion
  103.2 3.0 fusion.2.refs_8_
  107.3 1.1 reshape.165
  108.5 4.4 fusion.22.strength_ref
  113.8 10.3 %convolution_convert_fusion.pq_ref.pk_ref.pv_ref = bf16[4,264,1536]{2,1,0:T(8,128)(2,1)} fusion(bf16[4,264,2048]{2,1,0:T(8,128)(2,1)S(1)} %bitcast.81, bf16[2048,1536,1]{1,0,2:T(8,128)(2,1)} %bitcast.93), kind=kOutput, calls=%fused_computation.9 | convolution fusion | flops 6645399552 | bytes 13860864 | tf_op jit(solution)/shard_map/std,dm->stm/dot_general | solution.py:1648
  124.1 71.5 %mixer.1 = (bf16[4,256,512]{2,1,0:T(8,128)(2,1)}, f32[8,2,256,128]{3,2,1,0:T(8,128)}, f32[8,2,256,128]{3,2,1,0:T(8,128)}, f32[16,256,256]{2,1,0:T(8,128)}, f32[8...) custom-call(bf16[4,264,1536]{2,1,0:T(8,128)(2,1)} %convolution_convert_fusion.pq_ref.pk_ref.pv, ...), custom_call_target="tpu_custom_call" | custom-call | tf_op jit(solution)/shard_map/mixer/pallas_call | solution.py:485
  196.2 140.3 %fold.1 = (bf16[4,256,2048]{2,1,0:T(8,128)(2,1)}, f32[4,64,2048]{2,1,0:T(8,128)}, f32[1,2048]{1,0:T(1,128)}, bf16[8,256,1408]{2,1,0:T(8,128)(2,1)}, bf16[8,256,1...) custom-call(bf16[4,64,2048]{2,1,0:T(8,128)(2,1)} %tokens_ref.3, f32[1,2048]{1,0:T(1,128)} %bitcast.114, ...), custom_call_target="tpu_custom_call" | custom-call | tf_op jit(solution)/shard_map/fold/pallas_call | solution.py:1393
  336.5 15.7 %multiply_convert_fusion = (bf16[4,256,1408]{2,1,0:T(8,128)(2,1)}, bf16[4,256,1408]{2,1,0:T(8,128)(2,1)}, bf16[4,256,1408]{2,1,0:T(8,128)(2,1)}) fusion(f32[4,256,1408]{2,1,0:T(8,128)} %get-tuple-element.59, f32[4,256,1408]{2,1,0:T(8,128)} %get-tuple-element.60, bf16[4,256,2048]{2,1,0:T(8,128)(2,1)} %get-tuple-element.57, bf16[2048,1408,1]{1,0,2:T(8,128)(2,1)} %bitcast.95), kind=kOutput, calls=%fused_computation.5 | convolution fusion | flops 5928648704 | bytes 30146560 | tf_op jit(solution)/shard_map/std,df->stf/dot_general | solution.py:1648
  352.2 75.0 %fold_back.1 = (bf16[4,256,2048]{2,1,0:T(8,128)(2,1)}, f32[4,64,2048]{2,1,0:T(8,128)}, f32[1,2048]{1,0:T(1,128)}, f32[256,1408]{1,0:T(8,128)}) custom-call(bf16[4,64,2048]{2,1,0:T(8,128)(2,1)} %own_ref.5, f32[1,2048]{1,0:T(1,128)} %bitcast.115, f32[4,64,2048]{2,1,0:T(8,128)} %get-tuple-element.56.hidden_ref, bf16[1024,1408]{1,0:T(8,128)(2,1)} %bitcast.89, ...), custom_call_target="tpu_custom_call" | custom-call | tf_op jit(solution)/shard_map/fold_back/pallas_call | solution.py:1393
  427.3 44.4 %state_back.1 = (bf16[8,2,256,128]{3,2,1,0:T(8,128)(2,1)}, bf16[8,2,256,128]{3,2,1,0:T(8,128)(2,1)}, bf16[8,2,128,128]{3,2,1,0:T(8,128)(2,1)}, f32[8,128]{1,0:T(8,128)}) custom-call(bf16[4,256,2048]{2,1,0:T(8,128)(2,1)} %get-tuple-element.62.rows_ref, bf16[2048,512]{1,0:T(8,128)(2,1)} %bitcast.92, f32[1,128]{1,0:T(1,128)} %reshape.186.gain_ref, ...), custom_call_target="tpu_custom_call" | custom-call | tf_op jit(solution)/shard_map/state_back/pallas_call | solution.py:620
  471.7 75.4 %mixer_back.1 = (bf16[4,256,1536]{2,1,0:T(8,128)(2,1)}, f32[4,256,4]{2,1,0:T(8,128)}, f32[2,12,256]{2,1,0:T(8,128)}, f32[256,1408]{1,0:T(8,128)}, bf16[4,64,2048]{2,1,0:T(8,128)(2,1)}) custom-call(bf16[4,264,1536]{2,1,0:T(8,128)(2,1)} %convolution_convert_fusion.pq_ref.pk_ref.pv_ref, bf16[4,264,1536]{2,1,0:T(8,128)(2,1)} %convolution_convert_fusion.pq_ref.pk_ref.pv_ref, ...), custom_call_target="tpu_custom_call" | custom-call | tf_op jit(solution)/shard_map/mixer_back/pallas_call | solution.py:890
  548.4 1.1 convert_element_type.69
  549.5 2.9 fusion.10
  555.1 155.7 %closing.1 = (bf16[4,64,2048]{2,1,0:T(8,128)(2,1)}, f32[256,1408]{1,0:T(8,128)}, f32[256,512]{1,0:T(8,128)}, f32[256,1536]{1,0:T(8,128)}, f32[32,128]{1,0:T(8,12...) custom-call(f32[4,64,2048]{2,1,0:T(8,128)} %get-tuple-element.73.own_ref, bf16[4,64,2048]{2,1,0:T(8,128)(2,1)} %tokens_ref.3, ...), custom_call_target="tpu_custom_call" | custom-call | tf_op jit(solution)/shard_map/closing/pallas_call | solution.py:1592
  714.8 1.2 slice.79
  716.7 2.0 copy.73
  718.8 2.9 copy.74
  721.7 1.2 fusion.26
  722.9 1.0 copy.98
  724.8 1.1 copy.100
  725.9 1.1 copy.101
  (70 shorter events, 18.6 us)
Async XLA Ops:
  98.6 4.6 copy-start
  107.3 6.5 slice-start
  108.5 5.3 slice-start.1
  471.7 75.5 %copy-start.7 = (f32[8,128]{1,0:T(8,128)S(1)}, f32[8,128]{1,0:T(8,128)}, u32[]{:S(2)}) copy-start(f32[8,128]{1,0:T(8,128)} %get-tuple-element.76) | copy-start | bytes 12292
  471.7 75.6 %copy-start.6 = (f32[1,2048]{1,0:T(1,128)S(1)}, f32[1,2048]{1,0:T(1,128)}, u32[]{:S(2)}) copy-start(f32[1,2048]{1,0:T(1,128)} %get-tuple-element.75) | copy-start | bytes 24580
  710.7 10.9 %copy-start.1 = (f32[256,1536]{1,0:T(8,128)S(1)}, f32[256,1536]{1,0:T(8,128)}, u32[]{:S(2)}) copy-start(f32[256,1536]{1,0:T(8,128)} %get-tuple-element.80) | copy-start | bytes 4718596
  710.8 12.1 %copy-start.4 = (bf16[4,64,2048]{2,1,0:T(8,128)(2,1)S(1)}, bf16[4,64,2048]{2,1,0:T(8,128)(2,1)}, u32[]{:S(2)}) copy-start(bf16[4,64,2048]{2,1,0:T(8,128)(2,1)} %get-tuple-element.163) | copy-start | bytes 3145732
  721.7 2.2 copy-start.5
  721.7 3.1 copy-start.2
  722.9 3.1 copy-start.3
